TPU v7x, 512 devices: a whole 4x8x8 slice. The times are simulated.
512 devices in a mesh: seq: 32 (over x, y), req: 16 (over z, core).
Axes of the slice: x: 4, y: 8, z: 8, core: 2. Of those that a mesh axis runs over, the one named last changes fastest.
Arguments:
- x_in: bfloat16 [96, 4, 1536], P('req'), may hold values from -6 to 6
- attn_gain: float32 [1536], replicated, may hold values from 0.25 to 1.75
- moe_gain: float32 [1536], replicated, may hold values from 0.25 to 1.75
- w_qkv: bfloat16 [1536, 2560], P(None, 'seq'), may hold values from -0.15625 to 0.15625
- w_o: bfloat16 [1536, 1536], P(None, 'seq'), may hold values from -0.3125 to 0.3125
- cache_k: bfloat16 [96, 4096, 512], P('req', 'seq'), may hold values from -1024 to 1024
- cache_v: bfloat16 [96, 4096, 512], P('req', 'seq'), may hold values from -6 to 6
- page_map: int32 [96, 256], P('req', 'seq'), may hold values from 0 to 255, as said below
- lengths: int32 [96], P('req'), may hold values from 2 to 4096, as said below
- routes: int32 [96, 4, 8], P('req'), may hold values from 0 to 31, all different within a row; in each aligned block of 24 rows (0 to 23, 24 to 47, ..., all dimensions but the last counted through in order) at most 12 rows name the same one
- route_weights: float32 [96, 4, 8], P('req'), may hold values from 0.1 to 1
- w_gate_up: bfloat16 [32, 1536, 1024], P('seq', 'req'), may hold values from -0.15625 to 0.15625
- w_down: bfloat16 [32, 512, 1536], P('seq', None, 'req'), may hold values from -0.375 to 0.375
Outputs:
- layer_out: bfloat16 [96, 4, 1536], P('req', None, 'seq')
Inputs may be any that keep to these rules, and one draw needn't show every extreme that they name: `lengths`: every index of req holds one request with exactly 4096 cached positions. `page_map`: each row is a permutation of the request's 256 logical pages. `routes`: A token names 8 different experts. Among the 24 tokens of one index of req no expert is named more than 12 times.
All inputs are finite; a program needn't handle non-finite values.
Results may differ from a plain program's by a relative error of at most 0.01.
Values may be sent and summed in bfloat16 or wider, within the bound.
A program may use at most 64 MiB of HBM per device.

v0:
```python
import math

import jax
import jax.numpy as jnp
from jax import lax
from jax.sharding import PartitionSpec as P

D = 1536
HEADS = 24
KVH = 8
HD = 64
FFE = 512
TOP = 8
NSTEP = 4
PAGE = 16
ATT = 1536
KVD = 512
GROUP = 3
CAP = 12


EPS = 1e-05
NEG = -1e30


def combined_all(value, axis, join):
    pieces = jax.tree.map(lambda part: lax.all_gather(part, axis), value)
    head = jax.tree.map(lambda part: part[0], pieces)
    tail = jax.tree.map(lambda part: part[1:], pieces)
    so_far, _ = lax.scan(lambda so_far, piece: (join(so_far, piece), None), head, tail)
    return so_far


def normalize(values, gain):
    power = jnp.mean(values * values, axis=-1, keepdims=True)
    return values * lax.rsqrt(power + EPS) * gain


def rotate(values, position):
    half = values.shape[-1] // 2
    rates = jnp.exp(
        jnp.arange(half, dtype=jnp.float32) * (-2.0 * math.log(10000.0) / values.shape[-1])
    )
    angle = position[..., None, None] * rates
    cosine = jnp.cos(angle)
    sine = jnp.sin(angle)
    first_half = values[..., :half]
    second_half = values[..., half:]
    return jnp.concatenate(
        [first_half * cosine - second_half * sine, second_half * cosine + first_half * sine],
        axis=-1,
    )


def softmax_join(left, right):
    left_top, left_total, left_sums = left
    right_top, right_total, right_sums = right
    highest = jnp.maximum(left_top, right_top)
    left_factor = jnp.exp(left_top - highest)
    right_factor = jnp.exp(right_top - highest)
    row_count, head_count = highest.shape
    left_part = left_sums.reshape(row_count, head_count, -1) * left_factor[:, :, None]
    right_part = right_sums.reshape(row_count, head_count, -1) * right_factor[:, :, None]
    joined = (left_part + right_part).reshape(row_count, -1)
    return (highest, left_total * left_factor + right_total * right_factor, joined)


def project_with(left, piece):
    return jnp.dot(left, piece, preferred_element_type=jnp.float32)


def local(
    x_in,
    attn_gain,
    moe_gain,
    w_qkv,
    w_o,
    cache_k,
    cache_v,
    page_map,
    lengths,
    routes,
    route_weights,
    w_gate_up,
    w_down,
):
    local_requests = x_in.shape[0]
    row_count = local_requests * NSTEP
    inputs = x_in.astype(jnp.float32).reshape(row_count, D)
    normed = normalize(inputs, attn_gain).astype(jnp.bfloat16)
    projected = project_with(normed, lax.all_gather(w_qkv, "seq", axis=1, tiled=True))
    queries = projected[:, :ATT].reshape(local_requests, NSTEP, HEADS, HD)
    keys_new = projected[:, ATT : ATT + KVD].reshape(local_requests, NSTEP, KVH, HD)
    values_new = (
        projected[:, ATT + KVD :].reshape(local_requests, NSTEP, KVH, HD).astype(jnp.bfloat16)
    )
    position = (lengths[:, None] + jnp.arange(NSTEP, dtype=jnp.int32)[None, :]).astype(jnp.float32)
    queries = (
        rotate(queries, position)
        .astype(jnp.bfloat16)
        .reshape(local_requests, NSTEP, KVH, GROUP, HD)
    )
    keys_new = rotate(keys_new, position).astype(jnp.bfloat16)
    scale = HD ** (-0.5)
    slot_count = cache_k.shape[1]
    cached_keys = cache_k.reshape(local_requests, slot_count, KVH, HD)
    cached_values = cache_v.reshape(local_requests, slot_count, KVH, HD)
    slot_position = (
        page_map[:, :, None] * PAGE + jnp.arange(PAGE, dtype=jnp.int32)[None, None, :]
    ).reshape(local_requests, slot_count)
    live = (slot_position < lengths[:, None])[:, None, None, None, :]
    scores = (
        jnp.einsum("rskgd,rtkd->rskgt", queries, cached_keys, preferred_element_type=jnp.float32)
        * scale
    )
    scores = jnp.where(live, scores, NEG)
    local_top = jnp.max(scores, axis=-1)
    exp_scores = jnp.where(live, jnp.exp(scores - local_top[..., None]), 0.0)
    local_total = jnp.sum(exp_scores, axis=-1).reshape(row_count, HEADS)
    local_sums = jnp.einsum(
        "rskgt,rtkd->rskgd",
        exp_scores.astype(jnp.bfloat16),
        cached_values,
        preferred_element_type=jnp.float32,
    ).reshape(row_count, ATT)
    local_top = local_top.reshape(row_count, HEADS)
    cache_top, cache_total, cache_sums = combined_all(
        (local_top, local_total, local_sums), "seq", softmax_join
    )
    causal = (
        jnp.arange(NSTEP, dtype=jnp.int32)[:, None] >= jnp.arange(NSTEP, dtype=jnp.int32)[None, :]
    )[None, :, None, None, :]
    fresh = (
        jnp.einsum("rskgd,rukd->rskgu", queries, keys_new, preferred_element_type=jnp.float32)
        * scale
    )
    fresh = jnp.where(causal, fresh, NEG).reshape(row_count, HEADS, NSTEP)
    highest = jnp.maximum(cache_top, jnp.max(fresh, axis=-1))
    fresh_exp = jnp.exp(fresh - highest[:, :, None])
    carried = jnp.exp(cache_top - highest)
    denominator = cache_total * carried + jnp.sum(fresh_exp, axis=-1)
    fresh_probs = fresh_exp.reshape(local_requests, NSTEP, KVH, GROUP, NSTEP).astype(jnp.bfloat16)
    fresh_sums = jnp.einsum(
        "rskgu,rukd->rskgd", fresh_probs, values_new, preferred_element_type=jnp.float32
    ).reshape(row_count, HEADS, HD)
    numerator = cache_sums.reshape(row_count, HEADS, HD) * carried[:, :, None] + fresh_sums
    attended = (numerator / denominator[:, :, None]).reshape(row_count, ATT).astype(jnp.bfloat16)
    attn_mixed = project_with(attended, lax.all_gather(w_o, "seq", axis=1, tiled=True))
    resid = inputs + attn_mixed
    mixed_in = normalize(resid, moe_gain).astype(jnp.bfloat16)
    local_experts = w_gate_up.shape[0]
    groups = lax.axis_size("req")
    owned = lax.axis_index("seq") * local_experts + jnp.arange(local_experts, dtype=jnp.int32)
    chosen = routes.reshape(row_count, TOP)
    gates = route_weights.reshape(row_count, TOP)
    matches = chosen[None, :, :] == owned[:, None, None]
    routed = jnp.any(matches, axis=-1)
    route_scale = jnp.sum(jnp.where(matches, gates[None, :, :], 0.0), axis=-1)
    ordinal = jnp.cumsum(routed.astype(jnp.int32), axis=1) - 1
    placed = routed[:, :, None] & (
        ordinal[:, :, None] == jnp.arange(CAP, dtype=jnp.int32)[None, None, :]
    )
    outgoing = jnp.einsum(
        "erc,rd->ecd", placed.astype(jnp.bfloat16), mixed_in, preferred_element_type=jnp.float32
    ).astype(jnp.bfloat16)
    arrived = lax.all_to_all(outgoing[:, None], "req", split_axis=3, concat_axis=1, tiled=True)
    slice_width = arrived.shape[3]
    arrived = arrived.reshape(local_experts, groups * CAP, slice_width)
    partial_values = jnp.einsum(
        "end,edf->enf", arrived, w_gate_up, preferred_element_type=jnp.float32
    )
    gate_up = lax.psum(partial_values, "req")
    hidden = (jax.nn.silu(gate_up[..., :FFE]) * gate_up[..., FFE:]).astype(jnp.bfloat16)
    produced = jnp.einsum("enf,efd->end", hidden, w_down, preferred_element_type=jnp.float32)
    returned = lax.all_to_all(
        produced.reshape(local_experts, groups, CAP, slice_width),
        "req",
        split_axis=1,
        concat_axis=3,
        tiled=True,
    )[:, 0]
    weighted = placed.astype(jnp.float32) * route_scale[:, :, None]
    expert_total = jnp.einsum("erc,ecd->rd", weighted, returned, precision=lax.Precision.HIGHEST)
    own_share = lax.psum_scatter(expert_total, "seq", scatter_dimension=1, tiled=True)
    share_width = own_share.shape[1]
    resid_share = lax.dynamic_slice_in_dim(
        resid, lax.axis_index("seq") * share_width, share_width, 1
    )
    return (
        (resid_share + own_share).astype(jnp.bfloat16).reshape(local_requests, NSTEP, share_width)
    )


def solution(mesh):
    in_specs = (
        P("req", None, None),
        P(),
        P(),
        P(None, "seq"),
        P(None, "seq"),
        P("req", "seq", None),
        P("req", "seq", None),
        P("req", "seq"),
        P("req"),
        P("req", None, None),
        P("req", None, None),
        P("seq", "req", None),
        P("seq", None, "req"),
    )
    out_specs = P("req", None, "seq")
    return jax.shard_map(local, mesh=mesh, in_specs=in_specs, out_specs=out_specs, check_vma=False)
```

profile of v0, /device:TPU:448, one launch (start us, length us, event | category | flops | bytes accessed | tf_op | source)
XLA Modules:
  0.0 680.2 jit_solution(8462379774662940309)
XLA Ops:
  8.2 1.0 multiply_reduce_fusion.1
  10.2 1.5 copy.83
  11.8 1.5 copy.86
  14.9 96.2 %all-gather.4.cloned.1.call-done = bf16[1536,2560]{0,1:T(8,128)(2,1)} async-done(((bf16[1536,80]{0,1:T(8,128)(2,1)}), bf16[1536,2560]{0,1:T(8,128)(2,1)}) %all-gather.4.cloned.1.call-update) | async-done | bytes 7864336 | tf_op jit(solution)/shard_map/all_gather | solution.py:91
  111.1 5.4 fusion.21
  121.6 47.5 %all_gather.17 = f32[32,24,24]{2,1,0:T(8,128)S(1)} all-gather(f32[1,24,24]{2,1,0:T(8,128)S(1)} %all_gather_reshape.10), channel_id=1, replica_groups=mesh['seq'=32,'req'=16] {'seq'}, dimensions={0}, use_global_device_ids=true | all-gather | bytes 76032 | tf_op jit(solution)/shard_map/all_gather | solution.py:27
  169.6 47.9 %all_gather.16 = f32[32,24,24]{2,1,0:T(8,128)S(1)} all-gather(f32[1,24,24]{2,1,0:T(8,128)S(1)} %all_gather_reshape.9), channel_id=1, replica_groups=mesh['seq'=32,'req'=16] {'seq'}, dimensions={0}, use_global_device_ids=true | all-gather | bytes 76032 | tf_op jit(solution)/shard_map/all_gather | solution.py:27
  217.8 1.1 fusion.38
  219.6 4.8 slice.69
  225.4 48.3 %while.14 = (s32[]{:T(128)}, f32[24,24]{1,0:T(8,128)S(1)}, f32[24,24]{1,0:T(8,128)S(1)}, f32[24,1536]{1,0:T(8,128)S(1)}, f32[31,24,24]{2,1,0:T(8,128)S(1)}, /*in...) while((s32[]{:T(128)}, f32[24,24]{1,0:T(8,128)S(1)}, f32[24,24]{1,0:T(8,128)S(1)}, ...), condition=%wide.region_4.5_spmd, body=%wide.region_3.4_spmd.sunk | while | flops 114050 | bytes 1645149 | solution.py:30
  261.7 1.0 fusion.50
  268.0 1.0 fusion.50
  269.6 1.0 fusion.50
  276.3 19.0 %all-gather.8.cloned.1.call-done = bf16[1536,1536]{0,1:T(8,128)(2,1)} async-done(((bf16[1536,48]{0,1:T(8,128)(2,1)}), bf16[1536,1536]{0,1:T(8,128)(2,1)}) %all-gather.8.cloned.1.call-update) | async-done | bytes 4718608 | tf_op jit(solution)/shard_map/all_gather | solution.py:148
  295.4 3.8 multiply_reduce_fusion
  300.6 8.8 %reduce.7 = bf16[1536,12]{1,0:T(8,128)(2,1)S(1)} reduce(bf16[1536,1,1,12]{3,2,1,0:T(2,128)(2,1)S(1)} %bitcast.100, bf16[]{:T(256)} %broadcast.244), dimensions={1,2}, to_apply=%bitcast.81.reduce_sub_computation | reduce | bytes 73730
  309.9 11.6 %all_to_all.30 = bf16[16,2,576]{2,1,0:T(2,128)(2,1)S(1)} all-to-all(bf16[16,2,576]{2,1,0:T(2,128)(2,1)S(1)} %reshape.406), channel_id=1, replica_groups=mesh['seq'=32,'req'=16] {'req'}, dimensions={0} | all-to-all | bytes 73728 | tf_op jit(solution)/shard_map/all_to_all | solution.py:166
  323.0 1.2 convolution_bitcast_fusion.1
  324.3 109.2 %all-reduce.2.cloned.1.call-done = f32[1,192,1024]{2,1,0:T(8,128)} async-done(((f32[1,192,1024]{2,1,0:T(8,128)}), f32[1,192,1024]{2,1,0:T(8,128)}) %all-reduce.2.cloned.1.call-update) | async-done | bytes 786448 | tf_op jit(solution)/shard_map/psum | solution.py:172
  433.5 1.2 fusion.8
  435.8 8.9 %all-to-all-start.1 = ((f32[1,16,12,96]{3,0,2,1:T(1,128)}), f32[1,16,12,96]{3,0,2,1:T(1,128)S(1)}, u32[]{:S(2)}, u32[]{:S(2)}) async-start(f32[1,16,12,96]{3,0,2,1:T(1,128)} %copy.100), calls=%async_computation.1 | async-start | bytes 196608 | tf_op jit(solution)/shard_map/all_to_all | solution.py:175
  444.9 5.3 all-to-all-done.1
  450.3 2.3 convolution_bitcast_fusion
  452.6 219.6 %reduce-scatter.4.cloned.1.call-done = f32[48,24]{1,0:T(8,128)} async-done(((f32[1536,24]{1,0:T(8,128)}), f32[48,24]{1,0:T(8,128)}) %reduce-scatter.4.cloned.1.call-update) | async-done | bytes 4624
  (284 shorter events, 64.6 us)
Async XLA Ops:
  6.5 316.5 %copy-start = (bf16[1,96,1024]{2,1,0:T(8,128)(2,1)S(1)}, bf16[1,96,1024]{2,1,0:T(8,128)(2,1)}, u32[]{:S(2)}) copy-start(bf16[1,96,1024]{2,1,0:T(8,128)(2,1)} %param.26) | copy-start | bytes 589828
  6.5 104.6 %all-gather.4.cloned.1.call-start = ((), (), s32[]{:S(2)}) async-start(), calls=%async_computation.3 | async-start | bytes 8110080 | tf_op jit(solution)/shard_map/all_gather | solution.py:91
  7.3 212.4 %all-gather.6.cloned.1.call-start = ((), (), s32[]{:S(2)}) async-start(), calls=%async_computation.4 | async-start | bytes 4866048 | tf_op jit(solution)/shard_map/all_gather | solution.py:27
  116.5 3.5 copy-start.2
  116.5 3.5 copy-start.3
  119.2 176.2 %all-gather.8.cloned.1.call-start = ((), (), s32[]{:S(2)}) async-start(), calls=%async_computation.5 | async-start | bytes 4866048 | tf_op jit(solution)/shard_map/all_gather | solution.py:148
  119.9 313.6 %all-reduce.2.cloned.1.call-start = ((), (), s32[]{:S(2)}) async-start(), calls=%async_computation.6 | async-start | bytes 1572864 | tf_op jit(solution)/shard_map/psum | solution.py:172
  274.6 24.6 %copy-start.4 = (f32[1536]{0:T(1024)S(1)}, f32[1536]{0:T(1024)}, u32[]{:S(2)}) copy-start(f32[1536]{0:T(1024)} %param.17) | copy-start | bytes 18436
  299.1 135.7 %copy-start.1 = (bf16[1,512,96]{1,2,0:T(8,128)(2,1)S(1)}, bf16[1,512,96]{1,2,0:T(8,128)(2,1)}, u32[]{:S(2)}) copy-start(bf16[1,512,96]{1,2,0:T(8,128)(2,1)} %param.27) | copy-start | bytes 294916
  435.8 14.4 %all-to-all-start.1 = ((f32[1,16,12,96]{3,0,2,1:T(1,128)}), f32[1,16,12,96]{3,0,2,1:T(1,128)S(1)}, u32[]{:S(2)}, u32[]{:S(2)}) async-start(f32[1,16,12,96]{3,0,2,1:T(1,128)} %copy.100), calls=%async_computation.1 | async-start | bytes 196608 | tf_op jit(solution)/shard_map/all_to_all | solution.py:175
  444.7 227.5 %reduce-scatter.4.cloned.1.call-start = ((), (), s32[]{:S(2)}) async-start(), calls=%async_computation.7 | async-start | bytes 811008
Sparse Core Ops, SparseCore 0:
  10.5 100.5 all-gather.3
  119.3 86.8 all-gather.5
  209.4 85.9 all-gather.7
  324.3 109.1 all-reduce.1
  452.7 219.4 reduce-scatter.3
where the time goes:
time: 686 us; the launch traced here: 680 us
  waiting for transfers between devices  451 us (66%)
  blocking collectives  107 us (16%)
  other arithmetic  46.7 us (7%)
  local copies, waits for them, and re-layouts  36.1 us (5%)
  matrix products  15.7 us (2%)
  between operations  13.6 us (2%)
  starting transfers between devices  9.07 us (1%)
    unnamed x6, waiting for transfers between devices  221 us
    psum x1, waiting for transfers between devices, local(): gate_up = lax.psum(partial_values, 'req')  109 us
    all_gather x1, waiting for transfers between devices, local(): lax.all_gather(w_qkv, 'seq', axis=1, tiled=True)  96.2 us
    all_gather x2, blocking collectives, combined_all(): pieces = jax.tree.map(lambda part: lax.all_gather(part, axis), value)  95.4 us
    add x31, other arithmetic, softmax_join(): joined = (left_part + right_part).reshape(row_count, -1)  30.3 us
    all_gather x1, waiting for transfers between devices, local(): lax.all_gather(w_o, 'seq', axis=1, tiled=True)  19 us
  transfers between devices with their start and end apart: 6, of which 5 were waited for; matrix products, arithmetic and copies ran while one was open for 10% of the time, Pallas kernels for 0%

commit v1 on v0

v1 whole, which is shorter than its diff:
```python
import math

import jax
import jax.numpy as jnp
from jax import lax
from jax.sharding import PartitionSpec as P

D = 1536
HEADS = 24
KVH = 8
HD = 64
FFE = 512
TOP = 8
NSTEP = 4
PAGE = 16
ATT = 1536
KVD = 512
GROUP = 3
CAP = 12


EPS = 1e-05
NEG = -1e30


def normalize(values, gain):
    power = jnp.mean(values * values, axis=-1, keepdims=True)
    return values * lax.rsqrt(power + EPS) * gain


def rotate(values, position):
    half = values.shape[-1] // 2
    rates = jnp.exp(
        jnp.arange(half, dtype=jnp.float32) * (-2.0 * math.log(10000.0) / values.shape[-1])
    )
    angle = position[..., None, None] * rates
    cosine = jnp.cos(angle)
    sine = jnp.sin(angle)
    first_half = values[..., :half]
    second_half = values[..., half:]
    return jnp.concatenate(
        [first_half * cosine - second_half * sine, second_half * cosine + first_half * sine],
        axis=-1,
    )


def gather_columns(part, axis_name):
    count = lax.axis_size(axis_name)
    copies = jnp.broadcast_to(part[None], (count,) + part.shape)
    pieces = lax.all_to_all(copies, axis_name, split_axis=0, concat_axis=0, tiled=True)
    rows, width = part.shape
    return jnp.moveaxis(pieces, 0, 1).reshape(rows, count * width)


def sum_scatter_columns(value, axis_name):
    count = lax.axis_size(axis_name)
    rows, width = value.shape
    chunks = jnp.moveaxis(value.reshape(rows, count, width // count), 1, 0)
    pieces = lax.all_to_all(chunks, axis_name, split_axis=0, concat_axis=0, tiled=True)
    return jnp.sum(pieces, axis=0)


def local(
    x_in,
    attn_gain,
    moe_gain,
    w_qkv,
    w_o,
    cache_k,
    cache_v,
    page_map,
    lengths,
    routes,
    route_weights,
    w_gate_up,
    w_down,
):
    expert_in = lax.all_gather(w_gate_up[0], "req", axis=0, tiled=True)
    expert_out = lax.all_gather(w_down[0], "req", axis=1, tiled=True)

    seq_count = lax.axis_size("seq")
    me = lax.axis_index("seq")
    local_requests = x_in.shape[0]
    row_count = local_requests * NSTEP
    inputs = x_in.astype(jnp.float32).reshape(row_count, D)
    normed = normalize(inputs, attn_gain).astype(jnp.bfloat16)
    projected = gather_columns(
        jnp.dot(normed, w_qkv, preferred_element_type=jnp.float32), "seq"
    )
    queries = projected[:, :ATT].reshape(local_requests, NSTEP, HEADS, HD)
    keys_new = projected[:, ATT : ATT + KVD].reshape(local_requests, NSTEP, KVH, HD)
    values_new = (
        projected[:, ATT + KVD :].reshape(local_requests, NSTEP, KVH, HD).astype(jnp.bfloat16)
    )
    position = (lengths[:, None] + jnp.arange(NSTEP, dtype=jnp.int32)[None, :]).astype(jnp.float32)
    queries = (
        rotate(queries, position)
        .astype(jnp.bfloat16)
        .reshape(local_requests, NSTEP, KVH, GROUP, HD)
    )
    keys_new = rotate(keys_new, position).astype(jnp.bfloat16)
    scale = HD ** (-0.5)
    slot_count = cache_k.shape[1]
    cached_keys = cache_k.reshape(local_requests, slot_count, KVH, HD)
    cached_values = cache_v.reshape(local_requests, slot_count, KVH, HD)
    slot_position = (
        page_map[:, :, None] * PAGE + jnp.arange(PAGE, dtype=jnp.int32)[None, None, :]
    ).reshape(local_requests, slot_count)
    live = (slot_position < lengths[:, None])[:, None, None, None, :]
    scores = (
        jnp.einsum("rskgd,rtkd->rskgt", queries, cached_keys, preferred_element_type=jnp.float32)
        * scale
    )
    scores = jnp.where(live, scores, NEG)
    local_top = jnp.max(scores, axis=-1)
    exp_scores = jnp.where(live, jnp.exp(scores - local_top[..., None]), 0.0)
    local_total = jnp.sum(exp_scores, axis=-1).reshape(row_count, HEADS)
    local_sums = jnp.einsum(
        "rskgt,rtkd->rskgd",
        exp_scores.astype(jnp.bfloat16),
        cached_values,
        preferred_element_type=jnp.float32,
    ).reshape(row_count, ATT)
    local_top = local_top.reshape(row_count, HEADS)

    width = ATT // seq_count
    sum_chunks = jnp.moveaxis(local_sums.reshape(row_count, seq_count, width), 1, 0)
    extras = jnp.broadcast_to(
        jnp.concatenate([local_total, local_top], axis=1)[None],
        (seq_count, row_count, 2 * HEADS),
    )
    outgoing = jnp.concatenate([sum_chunks, extras], axis=2)
    arrived = lax.all_to_all(outgoing, "seq", split_axis=0, concat_axis=0, tiled=True)
    part_sums = arrived[:, :, :width]
    part_totals = arrived[:, :, width : width + HEADS]
    part_tops = arrived[:, :, width + HEADS :]

    causal = (
        jnp.arange(NSTEP, dtype=jnp.int32)[:, None] >= jnp.arange(NSTEP, dtype=jnp.int32)[None, :]
    )[None, :, None, None, :]
    fresh = (
        jnp.einsum("rskgd,rukd->rskgu", queries, keys_new, preferred_element_type=jnp.float32)
        * scale
    )
    fresh = jnp.where(causal, fresh, NEG).reshape(row_count, HEADS, NSTEP)
    cache_top = jnp.max(part_tops, axis=0)
    highest = jnp.maximum(cache_top, jnp.max(fresh, axis=-1))
    factors = jnp.exp(part_tops - highest[None])
    fresh_exp = jnp.exp(fresh - highest[:, :, None])
    denominator = jnp.sum(part_totals * factors, axis=0) + jnp.sum(fresh_exp, axis=-1)
    fresh_probs = fresh_exp.reshape(local_requests, NSTEP, KVH, GROUP, NSTEP).astype(jnp.bfloat16)
    fresh_sums = jnp.einsum(
        "rskgu,rukd->rskgd", fresh_probs, values_new, preferred_element_type=jnp.float32
    ).reshape(row_count, ATT)
    start = me * width
    head_of = (start + jnp.arange(width, dtype=jnp.int32)) // HD
    chunk_factors = jnp.take(factors, head_of, axis=2)
    numerator = jnp.sum(part_sums * chunk_factors, axis=0) + lax.dynamic_slice_in_dim(
        fresh_sums, start, width, 1
    )
    chunk_denominator = jnp.take(denominator, head_of, axis=1)
    attended_part = (numerator / chunk_denominator).astype(jnp.bfloat16)
    attended = gather_columns(attended_part, "seq")
    attn_mixed = gather_columns(
        jnp.dot(attended, w_o, preferred_element_type=jnp.float32), "seq"
    )
    resid = inputs + attn_mixed
    mixed_in = normalize(resid, moe_gain).astype(jnp.bfloat16)

    expert = me
    chosen = routes.reshape(row_count, TOP)
    gates = route_weights.reshape(row_count, TOP)
    route_scale = jnp.sum(jnp.where(chosen == expert, gates, 0.0), axis=-1)
    gate_up = jnp.dot(mixed_in, expert_in, preferred_element_type=jnp.float32)
    hidden = (jax.nn.silu(gate_up[:, :FFE]) * gate_up[:, FFE:]).astype(jnp.bfloat16)
    produced = jnp.dot(hidden, expert_out, preferred_element_type=jnp.float32)
    own_share = sum_scatter_columns(route_scale[:, None] * produced, "seq")
    share_width = own_share.shape[1]
    resid_share = lax.dynamic_slice_in_dim(resid, me * share_width, share_width, 1)
    return (
        (resid_share + own_share).astype(jnp.bfloat16).reshape(local_requests, NSTEP, share_width)
    )


def solution(mesh):
    in_specs = (
        P("req", None, None),
        P(),
        P(),
        P(None, "seq"),
        P(None, "seq"),
        P("req", "seq", None),
        P("req", "seq", None),
        P("req", "seq"),
        P("req"),
        P("req", None, None),
        P("req", None, None),
        P("seq", "req", None),
        P("seq", None, "req"),
    )
    out_specs = P("req", None, "seq")
    return jax.shard_map(local, mesh=mesh, in_specs=in_specs, out_specs=out_specs, check_vma=False)
```

time: 686 us -> 134 us (0.20)
  the two profiles are of different devices: /device:TPU:448 before, /device:TPU:8 now
where the time goes in v1:
time: 134 us; the launch traced here: 133 us
  waiting for transfers between devices  35.4 us (26%)
  blocking collectives  33.9 us (25%)
  starting transfers between devices  19.6 us (15%)
  between operations  13.9 us (10%)
  local copies, waits for them, and re-layouts  13.6 us (10%)
  other arithmetic  8.64 us (6%)
  matrix products  8.09 us (6%)
    all_to_all x1, blocking collectives, sum_scatter_columns(): lax.all_to_all(chunks, axis_name, split_axis=0, concat_axis=0, tiled=True)  20.2 us
    all_to_all x2, waiting for transfers between devices, gather_columns(): lax.all_to_all(copies, axis_name, split_axis=0, concat_axis=0, tiled=True)  20 us
    all_to_all x2, starting transfers between devices, gather_columns(): lax.all_to_all(copies, axis_name, split_axis=0, concat_axis=0, tiled=True)  14.8 us
    all_to_all x1, blocking collectives, gather_columns(): lax.all_to_all(copies, axis_name, split_axis=0, concat_axis=0, tiled=True)  13.7 us
    all_to_all x1, waiting for transfers between devices, local(): lax.all_to_all(outgoing, 'seq', split_axis=0, concat_axis=0, tiled=True)  12.8 us
    unnamed x33, local copies, waits for them, and re-layouts  5.05 us
    all_to_all x1, starting transfers between devices, local(): lax.all_to_all(outgoing, 'seq', split_axis=0, concat_axis=0, tiled=True)  4.78 us
  transfers between devices with their start and end apart: 5, of which 4 were waited for; matrix products, arithmetic and copies ran while one was open for 19% of the time, Pallas kernels for 0%

profile of v1, /device:TPU:8, one launch (start us, length us, event | category | flops | bytes accessed | tf_op | source)
XLA Modules:
  0.0 133.1 jit_solution(5938386089773424564)
XLA Ops:
  6.5 0.7 all-gather.5.cloned.1.call-update
  7.3 0.9 reshape.267
  8.2 1.0 multiply_reduce_fusion.2
  9.3 0.9 fusion.18
  10.2 0.8 broadcast_in_dim.66
  11.0 10.2 %all-to-all-start = ((f32[32,24,80]{2,1,0:T(8,128)}), f32[32,24,80]{2,1,0:T(8,128)S(1)}, u32[]{:S(2)}, u32[]{:S(2)}) async-start(f32[32,24,80]{2,1,0:T(8,128)} %broadcast_in_dim.66), calls=%async_computation | async-start | bytes 786432 | tf_op jit(solution)/shard_map/all_to_all | solution.py:50
  21.2 0.7 all-gather.7.cloned.1.call-update
  22.0 0.7 add_convert_fusion.3
  23.7 1.5 %copy.66 = bf16[6,128,512]{1,2,0:T(8,128)(2,1)S(1)} copy(bf16[6,128,512]{2,1,0:T(8,128)(2,1)} %param.18) | data formatting | bytes 1572864 | tf_op args[5]
  25.8 10.2 %all-to-all-done = f32[32,24,80]{2,1,0:T(8,128)S(1)} async-done(((f32[32,24,80]{2,1,0:T(8,128)}), f32[32,24,80]{2,1,0:T(8,128)S(1)}, u32[]{:S(2)}, u32[]{:S(2)}) %all-to-all-start) | async-done | bytes 245792 | tf_op jit(solution)/shard_map/all_to_all | solution.py:50
  40.2 0.9 pad_maximum_fusion
  41.1 4.8 %all-to-all-start.1 = ((f32[32,24,96]{2,1,0:T(8,128)}), f32[32,24,96]{2,1,0:T(8,128)S(1)}, u32[]{:S(2)}, u32[]{:S(2)}) async-start(f32[32,24,96]{2,1,0:T(8,128)} %pad_maximum_fusion), calls=%async_computation.1 | async-start | bytes 786432 | tf_op jit(solution)/shard_map/all_to_all | solution.py:133
  46.2 1.1 fusion.36
  47.6 12.8 %all-to-all-done.1 = f32[32,24,96]{2,1,0:T(8,128)S(1)} async-done(((f32[32,24,96]{2,1,0:T(8,128)}), f32[32,24,96]{2,1,0:T(8,128)S(1)}, u32[]{:S(2)}, u32[]{:S(2)}) %all-to-all-start.1) | async-done | bytes 294944 | tf_op jit(solution)/shard_map/all_to_all | solution.py:133
  65.2 13.7 %all_to_all.25 = bf16[32,2,576]{2,1,0:T(2,128)(2,1)S(1)} all-to-all(bf16[32,2,576]{2,1,0:T(2,128)(2,1)S(1)} %reshape.306), channel_id=1, replica_groups=mesh['seq'=32,'req'=16] {'seq'}, dimensions={0} | all-to-all | bytes 147456 | tf_op jit(solution)/shard_map/all_to_all | solution.py:50
  79.6 1.1 reshape.308
  80.7 4.6 %all-to-all-start.3 = ((f32[32,1,1152]{2,1,0:T(1,128)}), f32[32,1,1152]{2,1,0:T(1,128)S(1)}, u32[]{:S(2)}, u32[]{:S(2)}) async-start(f32[32,1,1152]{2,1,0:T(1,128)} %reshape.308), calls=%async_computation.3 | async-start | bytes 294912 | tf_op jit(solution)/shard_map/all_to_all | solution.py:50
  85.5 9.8 %all-to-all-done.3 = f32[32,1,1152]{2,1,0:T(1,128)S(1)} async-done(((f32[32,1,1152]{2,1,0:T(1,128)}), f32[32,1,1152]{2,1,0:T(1,128)S(1)}, u32[]{:S(2)}, u32[]{:S(2)}) %all-to-all-start.3) | async-done | bytes 147488 | tf_op jit(solution)/shard_map/all_to_all | solution.py:50
  95.8 1.0 reduce.5
  97.8 2.5 %fusion = f32[24,1024]{1,0:T(8,128)S(1)} fusion(bf16[1,1536,1024]{2,1,0:T(8,128)(2,1)} %all-gather.5.cloned.1.call-done, f32[24,1536]{1,0:T(8,128)S(1)} %add.165, f32[1536]{0:T(1024)S(1)} %copy-done.8, f32[24]{0:T(128)S(1)} %rsqrt.25), kind=kOutput, calls=%fused_computation.2 | convolution fusion | flops 75608064 | bytes 3397728 | tf_op jit(solution)/shard_map/dot_general | solution.py:174
  100.3 1.2 all-gather.7.cloned.1.call-done
  101.4 1.9 %convolution_multiply_fusion = f32[24,1536]{1,0:T(8,128)S(1)} fusion(bf16[1,512,1536]{1,2,0:T(8,128)(2,1)} %all-gather.7.cloned.1.call-done, f32[24]{0:T(128)S(1)} %mul.213, f32[24,1024]{1,0:T(8,128)S(1)} %fusion), kind=kOutput, calls=%fused_computation.4 | convolution fusion | flops 37859328 | bytes 1818720 | tf_op jit(solution)/shard_map/dot_general | solution.py:176
  104.2 20.2 %all_to_all.26 = f32[32,1,1152]{2,1,0:T(1,128)S(1)} all-to-all(f32[32,1,1152]{2,1,0:T(1,128)S(1)} %reshape.310), channel_id=1, replica_groups=mesh['seq'=32,'req'=16] {'seq'}, dimensions={0} | all-to-all | bytes 294912 | tf_op jit(solution)/shard_map/all_to_all | solution.py:59
  124.4 1.0 reduce.6
  (113 shorter events, 15.0 us)
Async XLA Ops:
  6.5 2.7 %copy-start = (bf16[1536,80]{0,1:T(8,128)(2,1)S(1)}, bf16[1536,80]{0,1:T(8,128)(2,1)}, u32[]{:S(2)}) copy-start(bf16[1536,80]{0,1:T(8,128)(2,1)} %param.16) | copy-start | bytes 737284
  6.5 19.0 %copy-start.9 = (s32[6]{0:T(128)S(1)}, s32[6]{0:T(128)}, u32[]{:S(2)}) copy-start(s32[6]{0:T(128)} %param.21) | copy-start | bytes 76
  6.5 18.6 %copy-start.3 = (bf16[6,128,512]{2,1,0:T(8,128)(2,1)S(1)}, bf16[6,128,512]{2,1,0:T(8,128)(2,1)}, u32[]{:S(2)}) copy-start(bf16[6,128,512]{2,1,0:T(8,128)(2,1)} %param.19) | copy-start | bytes 2359300
  6.5 91.2 %all-gather.5.cloned.1.call-start = ((), (), s32[]{:S(2)}) async-start(), calls=%async_computation.5 | async-start | bytes 3342336 | tf_op jit(solution)/shard_map/all_gather | solution.py:78
  11.0 25.1 %all-to-all-start = ((f32[32,24,80]{2,1,0:T(8,128)}), f32[32,24,80]{2,1,0:T(8,128)S(1)}, u32[]{:S(2)}, u32[]{:S(2)}) async-start(f32[32,24,80]{2,1,0:T(8,128)} %broadcast_in_dim.66), calls=%async_computation | async-start | bytes 786432 | tf_op jit(solution)/shard_map/all_to_all | solution.py:50
  21.2 80.2 %all-gather.7.cloned.1.call-start = ((), (), s32[]{:S(2)}) async-start(), calls=%async_computation.6 | async-start | bytes 1671168 | tf_op jit(solution)/shard_map/all_gather | solution.py:79
  36.4 3.1 %copy-start.1 = (f32[24,2560]{1,0:T(8,128)}, f32[24,2560]{1,0:T(8,128)S(1)}, u32[]{:S(2)}) copy-start(f32[24,2560]{1,0:T(8,128)S(1)} %reshape.268) | copy-start | bytes 737284
  39.5 6.4 %slice-start = ((f32[24,2560]{1,0:T(8,128)}), f32[24,512]{1,0:T(8,128)S(1)}, s32[]{:S(2)}) async-start(f32[24,2560]{1,0:T(8,128)} %copy-done.1), calls=%async_computation.7 | async-start | bytes 98304 | tf_op jit(solution)/shard_map/slice | solution.py:91
  39.5 7.8 %copy-start.2 = (f32[24,2560]{1,0:T(8,128)S(1)}, f32[24,2560]{1,0:T(8,128)}, u32[]{:S(2)}) copy-start(f32[24,2560]{1,0:T(8,128)} %copy-done.1) | copy-start | bytes 737284
  41.1 19.3 %all-to-all-start.1 = ((f32[32,24,96]{2,1,0:T(8,128)}), f32[32,24,96]{2,1,0:T(8,128)S(1)}, u32[]{:S(2)}, u32[]{:S(2)}) async-start(f32[32,24,96]{2,1,0:T(8,128)} %pad_maximum_fusion), calls=%async_computation.1 | async-start | bytes 786432 | tf_op jit(solution)/shard_map/all_to_all | solution.py:133
  62.2 17.3 %copy-start.5 = (bf16[1536,48]{0,1:T(8,128)(2,1)S(1)}, bf16[1536,48]{0,1:T(8,128)(2,1)}, u32[]{:S(2)}) copy-start(bf16[1536,48]{0,1:T(8,128)(2,1)} %param.17) | copy-start | bytes 442372
  62.8 22.5 %copy-start.6 = (f32[6,4,8]{2,1,0:T(4,128)S(1)}, f32[6,4,8]{2,1,0:T(4,128)}, u32[]{:S(2)}) copy-start(f32[6,4,8]{2,1,0:T(4,128)} %param.23) | copy-start | bytes 2308
  62.8 22.5 %copy-start.7 = (s32[6,4,8]{2,1,0:T(4,128)S(1)}, s32[6,4,8]{2,1,0:T(4,128)}, u32[]{:S(2)}) copy-start(s32[6,4,8]{2,1,0:T(4,128)} %param.22) | copy-start | bytes 2308
  64.8 32.8 %copy-start.4 = (bf16[6,4,1536]{2,1,0:T(4,128)(2,1)S(1)}, bf16[6,4,1536]{2,1,0:T(4,128)(2,1)}, u32[]{:S(2)}) copy-start(bf16[6,4,1536]{2,1,0:T(4,128)(2,1)} %param.13) | copy-start | bytes 221188
  64.9 32.9 %copy-start.8 = (f32[1536]{0:T(1024)S(1)}, f32[1536]{0:T(1024)}, u32[]{:S(2)}) copy-start(f32[1536]{0:T(1024)} %param.15) | copy-start | bytes 18436
  80.7 14.6 %all-to-all-start.3 = ((f32[32,1,1152]{2,1,0:T(1,128)}), f32[32,1,1152]{2,1,0:T(1,128)S(1)}, u32[]{:S(2)}, u32[]{:S(2)}) async-start(f32[32,1,1152]{2,1,0:T(1,128)} %reshape.308), calls=%async_computation.3 | async-start | bytes 294912 | tf_op jit(solution)/shard_map/all_to_all | solution.py:50
Sparse Core Ops, SparseCore 0:
  9.5 49.0 all-gather.4
  60.7 40.6 all-gather.6

commit v2 on v1

--- a/solution.py
+++ b/solution.py
@@ -1,8 +1,11 @@
+import functools
 import math
 
 import jax
 import jax.numpy as jnp
 from jax import lax
+from jax.experimental import pallas as pl
+from jax.experimental.pallas import tpu as pltpu
 from jax.sharding import PartitionSpec as P
 
 D = 1536
@@ -44,19 +47,74 @@
     )
 
 
-def gather_columns(part, axis_name):
+MESH = pl.DeviceIdType.MESH
+
+
+def exchange_kernel(count, axis_name, gather, x_ref, o_ref, send_sem, recv_sem):
+    me = lax.axis_index(axis_name)
+    barrier = pltpu.get_barrier_semaphore()
+
+    def greet(k, carry):
+        peer = lax.rem(me + k, count)
+        pl.semaphore_signal(barrier, inc=1, device_id={axis_name: peer}, device_id_type=MESH)
+        return carry
+
+    lax.fori_loop(1, count, greet, 0)
+    pl.semaphore_wait(barrier, count - 1)
+
+    def describe(k):
+        peer = lax.rem(me + k, count)
+        return pltpu.make_async_remote_copy(
+            src_ref=x_ref if gather else x_ref.at[peer],
+            dst_ref=o_ref.at[me],
+            send_sem=send_sem.at[k],
+            recv_sem=recv_sem.at[k],
+            device_id={axis_name: peer},
+            device_id_type=MESH,
+        )
+
+    def send(k, carry):
+        describe(k).start()
+        return carry
+
+    lax.fori_loop(1, count, send, 0)
+    o_ref[me] = x_ref[...] if gather else x_ref[me]
+
+    def finish(k, carry):
+        describe(k).wait()
+        return carry
+
+    lax.fori_loop(1, count, finish, 0)
+
+
+def exchange(value, axis_name, collective_id, gather):
     count = lax.axis_size(axis_name)
-    copies = jnp.broadcast_to(part[None], (count,) + part.shape)
-    pieces = lax.all_to_all(copies, axis_name, split_axis=0, concat_axis=0, tiled=True)
+    shape = value.shape if not gather else (count,) + value.shape
+    return pl.pallas_call(
+        functools.partial(exchange_kernel, count, axis_name, gather),
+        out_shape=jax.ShapeDtypeStruct(shape, value.dtype),
+        in_specs=[pl.BlockSpec(memory_space=pltpu.VMEM)],
+        out_specs=pl.BlockSpec(memory_space=pltpu.VMEM),
+        scratch_shapes=[
+            pltpu.SemaphoreType.DMA((count,)),
+            pltpu.SemaphoreType.DMA((count,)),
+        ],
+        compiler_params=pltpu.CompilerParams(collective_id=collective_id, has_side_effects=True),
+    )(value)
+
+
+def gather_columns(part, axis_name, collective_id):
+    count = lax.axis_size(axis_name)
+    pieces = exchange(part.astype(jnp.float32), axis_name, collective_id, True)
     rows, width = part.shape
-    return jnp.moveaxis(pieces, 0, 1).reshape(rows, count * width)
-
-
-def sum_scatter_columns(value, axis_name):
+    return jnp.moveaxis(pieces, 0, 1).reshape(rows, count * width).astype(part.dtype)
+
+
+def sum_scatter_columns(value, axis_name, collective_id):
     count = lax.axis_size(axis_name)
     rows, width = value.shape
     chunks = jnp.moveaxis(value.reshape(rows, count, width // count), 1, 0)
-    pieces = lax.all_to_all(chunks, axis_name, split_axis=0, concat_axis=0, tiled=True)
+    pieces = exchange(chunks, axis_name, collective_id, False)
     return jnp.sum(pieces, axis=0)
 
 
@@ -85,7 +143,7 @@
     inputs = x_in.astype(jnp.float32).reshape(row_count, D)
     normed = normalize(inputs, attn_gain).astype(jnp.bfloat16)
     projected = gather_columns(
-        jnp.dot(normed, w_qkv, preferred_element_type=jnp.float32), "seq"
+        jnp.dot(normed, w_qkv, preferred_element_type=jnp.float32), "seq", 0
     )
     queries = projected[:, :ATT].reshape(local_requests, NSTEP, HEADS, HD)
     keys_new = projected[:, ATT : ATT + KVD].reshape(local_requests, NSTEP, KVH, HD)
@@ -130,7 +188,7 @@
         (seq_count, row_count, 2 * HEADS),
     )
     outgoing = jnp.concatenate([sum_chunks, extras], axis=2)
-    arrived = lax.all_to_all(outgoing, "seq", split_axis=0, concat_axis=0, tiled=True)
+    arrived = exchange(outgoing, "seq", 1, False)
     part_sums = arrived[:, :, :width]
     part_totals = arrived[:, :, width : width + HEADS]
     part_tops = arrived[:, :, width + HEADS :]
@@ -160,9 +218,9 @@
     )
     chunk_denominator = jnp.take(denominator, head_of, axis=1)
     attended_part = (numerator / chunk_denominator).astype(jnp.bfloat16)
-    attended = gather_columns(attended_part, "seq")
+    attended = gather_columns(attended_part, "seq", 2)
     attn_mixed = gather_columns(
-        jnp.dot(attended, w_o, preferred_element_type=jnp.float32), "seq"
+        jnp.dot(attended, w_o, preferred_element_type=jnp.float32), "seq", 3
     )
     resid = inputs + attn_mixed
     mixed_in = normalize(resid, moe_gain).astype(jnp.bfloat16)
@@ -174,7 +232,7 @@
     gate_up = jnp.dot(mixed_in, expert_in, preferred_element_type=jnp.float32)
     hidden = (jax.nn.silu(gate_up[:, :FFE]) * gate_up[:, FFE:]).astype(jnp.bfloat16)
     produced = jnp.dot(hidden, expert_out, preferred_element_type=jnp.float32)
-    own_share = sum_scatter_columns(route_scale[:, None] * produced, "seq")
+    own_share = sum_scatter_columns(route_scale[:, None] * produced, "seq", 4)
     share_width = own_share.shape[1]
     resid_share = lax.dynamic_slice_in_dim(resid, me * share_width, share_width, 1)
     return (

time: 134 us -> 139 us (1.037)
  the two profiles are of different devices: /device:TPU:8 before, /device:TPU:448 now
where the time goes in v2:
time: 139 us; the launch traced here: 138 us
  Pallas kernels  92.1 us (66%)
  between operations  13.9 us (10%)
  local copies, waits for them, and re-layouts  13 us (9%)
  matrix products  9.33 us (7%)
  other arithmetic  8.61 us (6%)
    pallas_call x5, Pallas kernels, exchange(): pl.pallas_call(functools.partial(exchange_kernel, count, axis_name, gathe...  92.1 us
  transfers between devices with their start and end apart: 2, of which 0 were waited for; matrix products, arithmetic and copies ran while one was open for 19% of the time, Pallas kernels for 54%

profile of v2, /device:TPU:448, one launch (start us, length us, event | category | flops | bytes accessed | tf_op | source)
XLA Modules:
  0.0 138.4 jit_solution(14181995283019766344)
XLA Ops:
  6.6 0.7 all-gather.5.cloned.1.call-update
  7.3 0.7 all-gather.7.cloned.1.call-update
  8.0 0.9 reshape.263
  8.9 1.0 multiply_reduce_fusion.2
  10.0 1.5 %fusion.18.x_ref = f32[24,80]{1,0:T(8,128)} fusion(bf16[1536,80]{0,1:T(8,128)(2,1)S(1)} %copy-done, f32[24,1536]{1,0:T(8,128)S(1)} %reshape.263, f32[1536]{0:T(1024)} %param.14, f32[24]{0:T(128)S(1)} %rsqrt.23), kind=kOutput, calls=%fused_computation.42 | convolution fusion | flops 6008832 | bytes 407136 | tf_op jit(solution)/shard_map/dot_general | solution.py:146
  11.6 20.5 %shard_map.127 = f32[32,24,80]{2,1,0:T(8,128)} custom-call(f32[24,80]{1,0:T(8,128)} %fusion.18.x_ref), custom_call_target="tpu_custom_call" | custom-call | tf_op jit(solution)/shard_map/pallas_call | solution.py:93
  32.1 1.1 copy.44
  36.9 1.5 %copy.48 = bf16[6,128,512]{1,2,0:T(8,128)(2,1)S(1)} copy(bf16[6,128,512]{2,1,0:T(8,128)(2,1)} %param.19) | data formatting | bytes 1572864 | tf_op args[6]
  39.7 0.9 pad_maximum_fusion.x_ref
  40.6 18.5 %shard_map.128 = f32[32,24,96]{2,1,0:T(8,128)} custom-call(f32[32,24,96]{2,1,0:T(8,128)} %pad_maximum_fusion.x_ref), custom_call_target="tpu_custom_call" | custom-call | tf_op jit(solution)/shard_map/pallas_call | solution.py:93
  59.4 1.2 slice_reduce_fusion
  61.1 1.1 fusion.37
  66.4 0.7 fusion.30.x_ref
  67.1 18.2 %shard_map.129 = f32[32,24,48]{2,1,0:T(8,128)} custom-call(f32[24,48]{1,0:T(8,128)} %fusion.30.x_ref), custom_call_target="tpu_custom_call" | custom-call | tf_op jit(solution)/shard_map/pallas_call | solution.py:93
  85.3 1.0 convert_bitcast_fusion
  86.6 0.8 fusion.38.x_ref
  87.4 17.6 %shard_map.130 = f32[32,24,48]{2,1,0:T(8,128)} custom-call(f32[24,48]{1,0:T(8,128)} %fusion.38.x_ref), custom_call_target="tpu_custom_call" | custom-call | tf_op jit(solution)/shard_map/pallas_call | solution.py:93
  105.0 1.1 copy.67
  107.0 2.5 %fusion = f32[24,1024]{1,0:T(8,128)S(1)} fusion(bf16[1,1536,1024]{2,1,0:T(8,128)(2,1)} %all-gather.5.cloned.1.call-done, f32[24,1536]{1,0:T(8,128)S(1)} %add.165, f32[1536]{0:T(1024)S(1)} %copy-done.9, f32[24]{0:T(128)S(1)} %rsqrt.25), kind=kOutput, calls=%fused_computation.2 | convolution fusion | flops 75608064 | bytes 3397728 | tf_op jit(solution)/shard_map/dot_general | solution.py:232
  109.4 1.9 %convolution_multiply_fusion = f32[24,1536]{1,0:T(8,128)S(1)} fusion(bf16[1,512,1536]{1,2,0:T(8,128)(2,1)} %all-gather.7.cloned.1.call-done, f32[24]{0:T(128)S(1)} %mul.213, f32[24,1024]{1,0:T(8,128)S(1)} %fusion), kind=kOutput, calls=%fused_computation.4 | convolution fusion | flops 37859328 | bytes 1818720 | tf_op jit(solution)/shard_map/dot_general | solution.py:234
  111.5 1.0 copy.89
  112.5 17.3 %shard_map.131 = f32[32,24,48]{2,1,0:T(8,128)} custom-call(f32[32,24,48]{2,1,0:T(8,128)} %bitcast.75), custom_call_target="tpu_custom_call" | custom-call | tf_op jit(solution)/shard_map/pallas_call | solution.py:93
  129.8 1.0 reduce_sum.82
  130.9 0.7 add_convert_fusion.2
  (101 shorter events, 11.1 us)
Async XLA Ops:
  6.5 3.5 %copy-start = (bf16[1536,80]{0,1:T(8,128)(2,1)S(1)}, bf16[1536,80]{0,1:T(8,128)(2,1)}, u32[]{:S(2)}) copy-start(bf16[1536,80]{0,1:T(8,128)(2,1)} %param.16) | copy-start | bytes 737284
  6.5 27.0 %copy-start.11 = (s32[6]{0:T(128)S(1)}, s32[6]{0:T(128)}, u32[]{:S(2)}) copy-start(s32[6]{0:T(128)} %param.21) | copy-start | bytes 76
  6.5 27.6 %copy-start.10 = (s32[6,8]{1,0:T(8,128)S(1)}, s32[6,8]{1,0:T(8,128)}, u32[]{:S(2)}) copy-start(s32[6,8]{1,0:T(8,128)} %param.20) | copy-start | bytes 580
  6.5 27.8 %copy-start.4 = (bf16[6,128,512]{2,1,0:T(8,128)(2,1)S(1)}, bf16[6,128,512]{2,1,0:T(8,128)(2,1)}, u32[]{:S(2)}) copy-start(bf16[6,128,512]{2,1,0:T(8,128)(2,1)} %param.18) | copy-start | bytes 2359300
  6.5 100.4 %all-gather.5.cloned.1.call-start = ((), (), s32[]{:S(2)}) async-start(), calls=%async_computation | async-start | bytes 3342336 | tf_op jit(solution)/shard_map/all_gather | solution.py:136
  7.3 102.1 %all-gather.7.cloned.1.call-start = ((), (), s32[]{:S(2)}) async-start(), calls=%async_computation.1 | async-start | bytes 1671168 | tf_op jit(solution)/shard_map/all_gather | solution.py:137
  33.4 3.2 %copy-start.2 = (f32[24,2560]{1,0:T(8,128)}, f32[24,2560]{1,0:T(8,128)S(1)}, u32[]{:S(2)}) copy-start(f32[24,2560]{1,0:T(8,128)S(1)} %reshape.264) | copy-start | bytes 737284
  38.4 20.8 %slice-start = ((f32[24,2560]{1,0:T(8,128)}), f32[24,512]{1,0:T(8,128)S(1)}, s32[]{:S(2)}) async-start(f32[24,2560]{1,0:T(8,128)} %copy-done.2), calls=%async_computation.2 | async-start | bytes 98304 | tf_op jit(solution)/shard_map/slice | solution.py:149
  39.0 21.6 %copy-start.3 = (f32[24,2560]{1,0:T(8,128)S(1)}, f32[24,2560]{1,0:T(8,128)}, u32[]{:S(2)}) copy-start(f32[24,2560]{1,0:T(8,128)} %copy-done.2) | copy-start | bytes 737284
  59.2 4.5 %copy-start.1 = (f32[32,24,96]{2,1,0:T(8,128)S(1)}, f32[32,24,96]{2,1,0:T(8,128)}, u32[]{:S(2)}) copy-start(f32[32,24,96]{2,1,0:T(8,128)} %shard_map.128) | copy-start | bytes 884740
  64.0 22.6 %copy-start.6 = (bf16[1536,48]{0,1:T(8,128)(2,1)S(1)}, bf16[1536,48]{0,1:T(8,128)(2,1)}, u32[]{:S(2)}) copy-start(bf16[1536,48]{0,1:T(8,128)(2,1)} %param.17) | copy-start | bytes 442372
  65.1 41.4 %copy-start.5 = (bf16[6,4,1536]{2,1,0:T(4,128)(2,1)S(1)}, bf16[6,4,1536]{2,1,0:T(4,128)(2,1)}, u32[]{:S(2)}) copy-start(bf16[6,4,1536]{2,1,0:T(4,128)(2,1)} %param.13) | copy-start | bytes 221188
  65.4 41.4 %copy-start.7 = (f32[6,4,8]{2,1,0:T(4,128)S(1)}, f32[6,4,8]{2,1,0:T(4,128)}, u32[]{:S(2)}) copy-start(f32[6,4,8]{2,1,0:T(4,128)} %param.23) | copy-start | bytes 2308
  65.4 41.4 %copy-start.8 = (s32[6,4,8]{2,1,0:T(4,128)S(1)}, s32[6,4,8]{2,1,0:T(4,128)}, u32[]{:S(2)}) copy-start(s32[6,4,8]{2,1,0:T(4,128)} %param.22) | copy-start | bytes 2308
  65.4 41.5 %copy-start.9 = (f32[1536]{0:T(1024)S(1)}, f32[1536]{0:T(1024)}, u32[]{:S(2)}) copy-start(f32[1536]{0:T(1024)} %param.15) | copy-start | bytes 18436
Sparse Core Ops, SparseCore 0:
  9.5 41.8 all-gather.4
  53.5 40.2 all-gather.6

commit v3 on v1

--- a/solution.py
+++ b/solution.py
@@ -75,8 +75,21 @@
     w_gate_up,
     w_down,
 ):
-    expert_in = lax.all_gather(w_gate_up[0], "req", axis=0, tiled=True)
-    expert_out = lax.all_gather(w_down[0], "req", axis=1, tiled=True)
+    pieces = 4
+    expert_in = jnp.concatenate(
+        [
+            lax.all_gather(part, "req", axis=0, tiled=True)
+            for part in jnp.split(w_gate_up[0], pieces, axis=1)
+        ],
+        axis=1,
+    )
+    expert_out = jnp.concatenate(
+        [
+            lax.all_gather(part, "req", axis=1, tiled=True)
+            for part in jnp.split(w_down[0], pieces // 2, axis=0)
+        ],
+        axis=0,
+    )
 
     seq_count = lax.axis_size("seq")
     me = lax.axis_index("seq")

time: 134 us -> 218 us (1.63)
  blocking collectives: 33.9 us -> 139 us
  waiting for transfers between devices: 35.4 us -> 13.8 us
  starting transfers between devices: 19.6 us -> 34.6 us
  between operations: 13.9 us -> 0.58 us
    all_gather x0 -> x6, blocking collectives: none -> 118 us  [the longest x4 80.8 us: local(): lax.all_gather(part, 'req', axis=0, tiled=True)]
    all_to_all x2 -> x3, waiting for transfers between devices: 20 us -> 0.01 us  [gather_columns(): lax.all_to_all(copies, axis_name, split_axis=0, concat_axis=0, tiled=True)]
    all_to_all x1 -> x0, blocking collectives: 13.7 us -> none  [gather_columns(): lax.all_to_all(copies, axis_name, split_axis=0, concat_axis=0, tiled=True)]
    all_to_all x2 -> x3, starting transfers between devices: 14.8 us -> 24.7 us  [gather_columns(): lax.all_to_all(copies, axis_name, split_axis=0, concat_axis=0, tiled=True)]
    all_to_all x1, starting transfers between devices: 4.78 us -> 9.92 us  [local(): lax.all_to_all(outgoing, 'seq', split_axis=0, concat_axis=0, tiled=True)]
    unnamed x33 -> x49, local copies, waits for them, and re-layouts: 5.05 us -> 6.93 us
  transfers between devices with their start and end apart: 5 -> 4, of which waited for: 4 -> 1; matrix products, arithmetic and copies ran while one was open for 19% -> 2% of each run, Pallas kernels for 0% -> 0%
where the time goes in v3:
time: 218 us; the launch traced here: 217 us
  blocking collectives  139 us (64%)
  starting transfers between devices  34.6 us (16%)
  local copies, waits for them, and re-layouts  15.5 us (7%)
  waiting for transfers between devices  13.8 us (6%)
  other arithmetic  7.28 us (3%)
  matrix products  6.84 us (3%)
    all_gather x4, blocking collectives, local(): lax.all_gather(part, 'req', axis=0, tiled=True)  80.8 us
    all_gather x2, blocking collectives, local(): lax.all_gather(part, 'req', axis=1, tiled=True)  37.5 us
    all_to_all x3, starting transfers between devices, gather_columns(): lax.all_to_all(copies, axis_name, split_axis=0, concat_axis=0, tiled=True)  24.7 us
    all_to_all x1, blocking collectives, sum_scatter_columns(): lax.all_to_all(chunks, axis_name, split_axis=0, concat_axis=0, tiled=True)  20.2 us
    all_to_all x1, waiting for transfers between devices, local(): lax.all_to_all(outgoing, 'seq', split_axis=0, concat_axis=0, tiled=True)  13.8 us
    all_to_all x1, starting transfers between devices, local(): lax.all_to_all(outgoing, 'seq', split_axis=0, concat_axis=0, tiled=True)  9.92 us
    unnamed x49, local copies, waits for them, and re-layouts  6.93 us
  transfers between devices with their start and end apart: 4, of which 1 were waited for; matrix products, arithmetic and copies ran while one was open for 2% of the time, Pallas kernels for 0%

profile of v3, /device:TPU:8, one launch (start us, length us, event | category | flops | bytes accessed | tf_op | source)
XLA Modules:
  0.0 217.1 jit_solution(889715388834273330)
XLA Ops:
  0.0 0.9 reshape.269
  0.9 1.0 multiply_reduce_fusion.2
  2.1 1.0 fusion.26
  3.1 0.8 broadcast_in_dim.66
  3.9 10.2 %all-to-all-start = ((f32[32,24,80]{2,1,0:T(8,128)}), f32[32,24,80]{2,1,0:T(8,128)S(1)}, u32[]{:S(2)}, u32[]{:S(2)}) async-start(f32[32,24,80]{2,1,0:T(8,128)} %broadcast_in_dim.66), calls=%async_computation | async-start | bytes 786432 | tf_op jit(solution)/shard_map/all_to_all | solution.py:50
  15.5 1.2 copy.67
  16.8 25.3 %all_gather.18 = bf16[1536,256]{1,0:T(8,128)(2,1)S(1)} all-gather(bf16[96,256]{1,0:T(8,128)(2,1)S(1)} %get-tuple-element.14), channel_id=1, replica_groups=mesh['seq'=32,'req'=16] {'req'}, dimensions={0}, use_global_device_ids=true | all-gather | bytes 835584 | tf_op jit(solution)/shard_map/all_gather | solution.py:81
  42.1 18.1 %all_gather.19 = bf16[1536,256]{1,0:T(8,128)(2,1)} all-gather(bf16[96,256]{1,0:T(8,128)(2,1)S(1)} %get-tuple-element.17), channel_id=1, replica_groups=mesh['seq'=32,'req'=16] {'req'}, dimensions={0}, use_global_device_ids=true | all-gather | bytes 835584 | tf_op jit(solution)/shard_map/all_gather | solution.py:81
  60.2 19.3 %all_gather.20 = bf16[1536,256]{1,0:T(8,128)(2,1)} all-gather(bf16[96,256]{1,0:T(8,128)(2,1)S(1)} %get-tuple-element.16), channel_id=1, replica_groups=mesh['seq'=32,'req'=16] {'req'}, dimensions={0}, use_global_device_ids=true | all-gather | bytes 835584 | tf_op jit(solution)/shard_map/all_gather | solution.py:81
  79.8 18.0 %all_gather.21 = bf16[1536,256]{1,0:T(8,128)(2,1)} all-gather(bf16[96,256]{1,0:T(8,128)(2,1)S(1)} %get-tuple-element.15), channel_id=1, replica_groups=mesh['seq'=32,'req'=16] {'req'}, dimensions={0}, use_global_device_ids=true | all-gather | bytes 835584 | tf_op jit(solution)/shard_map/all_gather | solution.py:81
  102.4 0.9 pad_maximum_fusion
  103.3 9.9 %all-to-all-start.1 = ((f32[32,24,96]{2,1,0:T(8,128)}), f32[32,24,96]{2,1,0:T(8,128)S(1)}, u32[]{:S(2)}, u32[]{:S(2)}) async-start(f32[32,24,96]{2,1,0:T(8,128)} %pad_maximum_fusion), calls=%async_computation.1 | async-start | bytes 786432 | tf_op jit(solution)/shard_map/all_to_all | solution.py:146
  113.6 1.1 fusion.48
  114.9 13.8 %all-to-all-done.1 = f32[32,24,96]{2,1,0:T(8,128)S(1)} async-done(((f32[32,24,96]{2,1,0:T(8,128)}), f32[32,24,96]{2,1,0:T(8,128)S(1)}, u32[]{:S(2)}, u32[]{:S(2)}) %all-to-all-start.1) | async-done | bytes 294944 | tf_op jit(solution)/shard_map/all_to_all | solution.py:146
  133.2 0.9 reshape.308
  134.1 4.8 %all-to-all-start.2 = ((bf16[32,2,576]{2,1,0:T(2,128)(2,1)}), bf16[32,2,576]{2,1,0:T(2,128)(2,1)S(1)}, u32[]{:S(2)}, u32[]{:S(2)}) async-start(bf16[32,2,576]{2,1,0:T(2,128)(2,1)} %reshape.308), calls=%async_computation.2 | async-start | bytes 163840 | tf_op jit(solution)/shard_map/all_to_all | solution.py:50
  138.9 19.5 %all-gather = bf16[1,256,1536]{1,2,0:T(8,128)(2,1)} all-gather(bf16[1,256,96]{1,2,0:T(8,128)(2,1)S(1)} %get-tuple-element.20), channel_id=2, replica_groups=mesh['seq'=32,'req'=16] {'req'}, dimensions={2}, use_global_device_ids=true | all-gather | bytes 835584 | tf_op jit(solution)/shard_map/all_gather | solution.py:88
  159.3 1.0 reshape.310
  160.3 9.8 %all-to-all-start.3 = ((f32[32,1,1152]{2,1,0:T(1,128)}), f32[32,1,1152]{2,1,0:T(1,128)S(1)}, u32[]{:S(2)}, u32[]{:S(2)}) async-start(f32[32,1,1152]{2,1,0:T(1,128)} %reshape.310), calls=%async_computation.3 | async-start | bytes 294912 | tf_op jit(solution)/shard_map/all_to_all | solution.py:50
  170.1 18.0 %all-gather.1 = bf16[1,256,1536]{1,2,0:T(8,128)(2,1)} all-gather(bf16[1,256,96]{1,2,0:T(8,128)(2,1)S(1)} %get-tuple-element.21), channel_id=3, replica_groups=mesh['seq'=32,'req'=16] {'req'}, dimensions={2}, use_global_device_ids=true | all-gather | bytes 835584 | tf_op jit(solution)/shard_map/all_gather | solution.py:88
  188.6 1.0 reduce.5
  191.1 2.6 %fusion = f32[24,1024]{1,0:T(8,128)S(1)} fusion(bf16[1536,256]{1,0:T(8,128)(2,1)} %all_gather.21, bf16[1536,256]{1,0:T(8,128)(2,1)} %all_gather.20, bf16[1536,256]{1,0:T(8,128)(2,1)S(1)} %copy-done.5, bf16[1536,256]{1,0:T(8,128)(2,1)S(1)} %all_gather.18, f32[24,1536]{1,0:T(8,128)S(1)} %add.165, f32[1536]{0:T(1024)S(1)} %copy-done.17, f32[24]{0:T(128)S(1)} %rsqrt.25), kind=kOutput, calls=%fused_computation.2 | convolution fusion | flops 88190976 | bytes 3397728 | tf_op jit(solution)/shard_map/dot_general | solution.py:187
  195.0 20.2 %all_to_all.25 = f32[32,1,1152]{2,1,0:T(1,128)S(1)} all-to-all(f32[32,1,1152]{2,1,0:T(1,128)S(1)} %reshape.312), channel_id=1, replica_groups=mesh['seq'=32,'req'=16] {'seq'}, dimensions={0} | all-to-all | bytes 294912 | tf_op jit(solution)/shard_map/all_to_all | solution.py:59
  215.2 1.0 reduce.6
  (132 shorter events, 16.2 us)
Async XLA Ops:
  0.0 2.0 copy-start
  2.0 12.0 %copy-start.16 = (s32[6]{0:T(128)S(1)}, s32[6]{0:T(128)}, u32[]{:S(2)}) copy-start(s32[6]{0:T(128)} %param.21) | copy-start | bytes 76
  2.0 12.1 %copy-start.15 = (s32[6,8]{1,0:T(8,128)S(1)}, s32[6,8]{1,0:T(8,128)}, u32[]{:S(2)}) copy-start(s32[6,8]{1,0:T(8,128)} %param.20) | copy-start | bytes 580
  2.1 12.3 %copy-start.3 = (bf16[6,128,512]{2,1,0:T(8,128)(2,1)S(1)}, bf16[6,128,512]{2,1,0:T(8,128)(2,1)}, u32[]{:S(2)}) copy-start(bf16[6,128,512]{2,1,0:T(8,128)(2,1)} %param.18) | copy-start | bytes 2359300
  3.9 94.0 %all-to-all-start = ((f32[32,24,80]{2,1,0:T(8,128)}), f32[32,24,80]{2,1,0:T(8,128)S(1)}, u32[]{:S(2)}, u32[]{:S(2)}) async-start(f32[32,24,80]{2,1,0:T(8,128)} %broadcast_in_dim.66), calls=%async_computation | async-start | bytes 786432 | tf_op jit(solution)/shard_map/all_to_all | solution.py:50
  14.4 1.1 copy-start.4
  15.5 1.2 copy-start.10
  42.1 37.5 %copy-start.12 = (bf16[1,512,96]{1,2,0:T(8,128)(2,1)S(1)}, bf16[1,512,96]{1,2,0:T(8,128)(2,1)}, u32[]{:S(2)}) copy-start(bf16[1,512,96]{1,2,0:T(8,128)(2,1)} %param.25) | copy-start | bytes 294916
  98.2 0.7 copy-start.1
  99.5 1.5 copy-start.6
  102.4 10.9 %slice-start = ((f32[24,2560]{1,0:T(8,128)}), f32[24,512]{1,0:T(8,128)S(1)}, s32[]{:S(2)}) async-start(f32[24,2560]{1,0:T(8,128)} %copy-done.1), calls=%async_computation.5 | async-start | bytes 98304 | tf_op jit(solution)/shard_map/slice | solution.py:104
  103.3 10.1 %copy-start.2 = (f32[24,2560]{1,0:T(8,128)S(1)}, f32[24,2560]{1,0:T(8,128)}, u32[]{:S(2)}) copy-start(f32[24,2560]{1,0:T(8,128)} %copy-done.1) | copy-start | bytes 737284
  103.3 25.4 %all-to-all-start.1 = ((f32[32,24,96]{2,1,0:T(8,128)}), f32[32,24,96]{2,1,0:T(8,128)S(1)}, u32[]{:S(2)}, u32[]{:S(2)}) async-start(f32[32,24,96]{2,1,0:T(8,128)} %pad_maximum_fusion), calls=%async_computation.1 | async-start | bytes 786432 | tf_op jit(solution)/shard_map/all_to_all | solution.py:146
  132.9 25.4 %copy-start.13 = (f32[6,4,8]{2,1,0:T(4,128)S(1)}, f32[6,4,8]{2,1,0:T(4,128)}, u32[]{:S(2)}) copy-start(f32[6,4,8]{2,1,0:T(4,128)} %param.23) | copy-start | bytes 2308
  133.0 25.4 %copy-start.14 = (s32[6,4,8]{2,1,0:T(4,128)S(1)}, s32[6,4,8]{2,1,0:T(4,128)}, u32[]{:S(2)}) copy-start(s32[6,4,8]{2,1,0:T(4,128)} %param.22) | copy-start | bytes 2308
  134.1 24.4 %all-to-all-start.2 = ((bf16[32,2,576]{2,1,0:T(2,128)(2,1)}), bf16[32,2,576]{2,1,0:T(2,128)(2,1)S(1)}, u32[]{:S(2)}, u32[]{:S(2)}) async-start(bf16[32,2,576]{2,1,0:T(2,128)(2,1)} %reshape.308), calls=%async_computation.2 | async-start | bytes 163840 | tf_op jit(solution)/shard_map/all_to_all | solution.py:50
  138.9 20.2 %copy-start.11 = (bf16[1536,48]{0,1:T(8,128)(2,1)S(1)}, bf16[1536,48]{0,1:T(8,128)(2,1)}, u32[]{:S(2)}) copy-start(bf16[1536,48]{0,1:T(8,128)(2,1)} %param.17) | copy-start | bytes 442372
  160.3 27.8 %all-to-all-start.3 = ((f32[32,1,1152]{2,1,0:T(1,128)}), f32[32,1,1152]{2,1,0:T(1,128)S(1)}, u32[]{:S(2)}, u32[]{:S(2)}) async-start(f32[32,1,1152]{2,1,0:T(1,128)} %reshape.310), calls=%async_computation.3 | async-start | bytes 294912 | tf_op jit(solution)/shard_map/all_to_all | solution.py:50
  189.9 0.9 copy-start.9
  189.9 1.2 copy-start.5
  189.9 1.2 copy-start.17
  191.1 2.6 %copy-start.7 = (bf16[1,256,1536]{1,2,0:T(8,128)(2,1)S(1)}, bf16[1,256,1536]{1,2,0:T(8,128)(2,1)}, u32[]{:S(2)}) copy-start(bf16[1,256,1536]{1,2,0:T(8,128)(2,1)} %all-gather) | copy-start | bytes 2359300
  191.1 2.6 %copy-start.8 = (bf16[1,256,1536]{1,2,0:T(8,128)(2,1)S(1)}, bf16[1,256,1536]{1,2,0:T(8,128)(2,1)}, u32[]{:S(2)}) copy-start(bf16[1,256,1536]{1,2,0:T(8,128)(2,1)} %all-gather.1) | copy-start | bytes 2359300

commit v4 on v1

--- a/solution.py
+++ b/solution.py
@@ -1,8 +1,11 @@
+import functools
 import math
 
 import jax
 import jax.numpy as jnp
 from jax import lax
+from jax.experimental import pallas as pl
+from jax.experimental.pallas import tpu as pltpu
 from jax.sharding import PartitionSpec as P
 
 D = 1536
@@ -58,6 +61,76 @@
     chunks = jnp.moveaxis(value.reshape(rows, count, width // count), 1, 0)
     pieces = lax.all_to_all(chunks, axis_name, split_axis=0, concat_axis=0, tiled=True)
     return jnp.sum(pieces, axis=0)
+
+
+MESH = pl.DeviceIdType.MESH
+
+
+def mixed_kernel(count, axis_name, part_ref, wt_ref, o_ref, full, mine, send_sem, recv_sem, own_sem):
+    me = lax.axis_index(axis_name)
+    width = part_ref.shape[0]
+    rows = pl.ds(pl.multiple_of(me * width, 8), width)
+    barrier = pltpu.get_barrier_semaphore()
+
+    def greet(k, carry):
+        peer = lax.rem(me + k, count)
+        pl.semaphore_signal(barrier, inc=1, device_id={axis_name: peer}, device_id_type=MESH)
+        return carry
+
+    lax.fori_loop(1, count, greet, 0)
+    pl.semaphore_wait(barrier, count - 1)
+
+    def spread(stage, source, target):
+        def describe(k):
+            peer = lax.rem(me + k, count)
+            return pltpu.make_async_remote_copy(
+                src_ref=source,
+                dst_ref=target.at[rows],
+                send_sem=send_sem.at[stage, k],
+                recv_sem=recv_sem.at[stage, k],
+                device_id={axis_name: peer},
+                device_id_type=MESH,
+            )
+
+        def send(k, carry):
+            describe(k).start()
+            return carry
+
+        def finish(k, carry):
+            describe(k).wait()
+            return carry
+
+        lax.fori_loop(1, count, send, 0)
+        own = pltpu.make_async_copy(source, target.at[rows], own_sem.at[stage])
+        own.start()
+        lax.fori_loop(1, count, finish, 0)
+        own.wait()
+
+    spread(0, part_ref, full)
+    mine[...] = jnp.dot(
+        wt_ref[...], full[...].astype(jnp.bfloat16), preferred_element_type=jnp.float32
+    )
+    spread(1, mine, o_ref)
+
+
+def project_out(attended_part, w_o, axis_name, collective_id):
+    count = lax.axis_size(axis_name)
+    rows, width = attended_part.shape
+    out_t = pl.pallas_call(
+        functools.partial(mixed_kernel, count, axis_name),
+        out_shape=jax.ShapeDtypeStruct((count * width, rows), jnp.float32),
+        in_specs=[pl.BlockSpec(memory_space=pltpu.VMEM)] * 2,
+        out_specs=pl.BlockSpec(memory_space=pltpu.VMEM),
+        scratch_shapes=[
+            pltpu.VMEM((count * width, rows), jnp.float32),
+            pltpu.VMEM((width, rows), jnp.float32),
+            pltpu.SemaphoreType.DMA((2, count)),
+            pltpu.SemaphoreType.DMA((2, count)),
+            pltpu.SemaphoreType.DMA((2,)),
+        ],
+        compiler_params=pltpu.CompilerParams(collective_id=collective_id, has_side_effects=True),
+    )(attended_part.astype(jnp.float32).T, w_o.T)
+    return out_t.T
 
 
 def local(
@@ -160,10 +233,7 @@
     )
     chunk_denominator = jnp.take(denominator, head_of, axis=1)
     attended_part = (numerator / chunk_denominator).astype(jnp.bfloat16)
-    attended = gather_columns(attended_part, "seq")
-    attn_mixed = gather_columns(
-        jnp.dot(attended, w_o, preferred_element_type=jnp.float32), "seq"
-    )
+    attn_mixed = project_out(attended_part, w_o, "seq", 0)
     resid = inputs + attn_mixed
     mixed_in = normalize(resid, moe_gain).astype(jnp.bfloat16)
 

time: 134 us -> 144 us (1.075)
  the two profiles are of different devices: /device:TPU:8 before, /device:TPU:448 now
where the time goes in v4:
time: 144 us
  Pallas kernels  43.6 us (30%)
  waiting for transfers between devices  21.6 us (15%)
  blocking collectives  18 us (12%)
  starting transfers between devices  15.1 us (10%)
  between operations  13.8 us (10%)
  local copies, waits for them, and re-layouts  12.6 us (9%)
  other arithmetic  9.52 us (7%)
  matrix products  9.31 us (6%)
    pallas_call x1, Pallas kernels, project_out(): pl.pallas_call(functools.partial(mixed_kernel, count, axis_name), out_sha...  43.6 us
    all_to_all x1, blocking collectives, sum_scatter_columns(): lax.all_to_all(chunks, axis_name, split_axis=0, concat_axis=0, tiled=True)  18 us
    all_to_all x1, waiting for transfers between devices, local(): lax.all_to_all(outgoing, 'seq', split_axis=0, concat_axis=0, tiled=True)  12.2 us
    all_to_all x1, starting transfers between devices, gather_columns(): lax.all_to_all(copies, axis_name, split_axis=0, concat_axis=0, tiled=True)  9.95 us
    all_to_all x1, waiting for transfers between devices, gather_columns(): lax.all_to_all(copies, axis_name, split_axis=0, concat_axis=0, tiled=True)  7.93 us
    all_to_all x1, starting transfers between devices, local(): lax.all_to_all(outgoing, 'seq', split_axis=0, concat_axis=0, tiled=True)  5.14 us
    unnamed x21, local copies, waits for them, and re-layouts  4.07 us
  transfers between devices with their start and end apart: 4, of which 2 were waited for; matrix products, arithmetic and copies ran while one was open for 18% of the time, Pallas kernels for 30%

profile of v4, /device:TPU:448, one launch (start us, length us, event | category | flops | bytes accessed | tf_op | source)
XLA Modules:
  0.0 143.6 jit_solution(17888071098835532830)
XLA Ops:
  6.5 0.7 all-gather.5.cloned.1.call-update
  7.3 0.9 reshape.247
  8.2 1.0 multiply_reduce_fusion.2
  9.3 0.9 fusion.20
  10.2 0.8 broadcast_in_dim.91
  11.0 10.0 %all-to-all-start = ((f32[32,24,80]{2,1,0:T(8,128)}), f32[32,24,80]{2,1,0:T(8,128)S(1)}, u32[]{:S(2)}, u32[]{:S(2)}) async-start(f32[32,24,80]{2,1,0:T(8,128)} %broadcast_in_dim.91), calls=%async_computation | async-start | bytes 786432 | tf_op jit(solution)/shard_map/all_to_all | solution.py:53
  21.0 0.7 all-gather.7.cloned.1.call-update
  21.8 0.7 add_convert_fusion.3
  22.5 0.7 broadcast_multiply_fusion
  23.2 0.8 select_reduce_fusion
  25.0 2.3 %copy.72 = bf16[6,128,512]{1,2,0:T(8,128)(2,1)} copy(bf16[6,128,512]{2,1,0:T(8,128)(2,1)} %param.19) | data formatting | bytes 1572864 | tf_op args[6]
  27.6 7.9 %all-to-all-done = f32[32,24,80]{2,1,0:T(8,128)S(1)} async-done(((f32[32,24,80]{2,1,0:T(8,128)}), f32[32,24,80]{2,1,0:T(8,128)S(1)}, u32[]{:S(2)}, u32[]{:S(2)}) %all-to-all-start) | async-done | bytes 245792 | tf_op jit(solution)/shard_map/all_to_all | solution.py:53
  38.3 1.7 %convolution_bitcast_fusion = f32[6,4,8,3,64]{4,1,3,2,0:T(4,128)S(1)} fusion(bf16[6,128,8,64,1]{1,3,4,2,0:T(8,128)(2,1)} %bitcast.79, f32[6,4,8,3,128]{4,1,3,2,0:T(4,128)S(1)} %get-tuple-element.21, f32[6,4,8,3]{1,3,2,0:T(4,128)S(1)} %get-tuple-element.20, pred[6,128]{1,0:T(8,128)(4,1)S(1)} %add_compare_fusion), kind=kOutput, calls=%fused_computation.9 | convolution fusion | flops 9658368 | bytes 1231872 | tf_op jit(solution)/shard_map/rskgt,rtkd->rskgd/dot_general | solution.py:191
  40.8 0.9 pad_maximum_fusion
  41.7 5.1 %all-to-all-start.1 = ((f32[32,24,96]{2,1,0:T(8,128)}), f32[32,24,96]{2,1,0:T(8,128)S(1)}, u32[]{:S(2)}, u32[]{:S(2)}) async-start(f32[32,24,96]{2,1,0:T(8,128)} %pad_maximum_fusion), calls=%async_computation.1 | async-start | bytes 786432 | tf_op jit(solution)/shard_map/all_to_all | solution.py:206
  47.2 1.1 fusion.36
  48.5 12.2 %all-to-all-done.1 = f32[32,24,96]{2,1,0:T(8,128)S(1)} async-done(((f32[32,24,96]{2,1,0:T(8,128)}), f32[32,24,96]{2,1,0:T(8,128)S(1)}, u32[]{:S(2)}, u32[]{:S(2)}) %all-to-all-start.1) | async-done | bytes 294944 | tf_op jit(solution)/shard_map/all_to_all | solution.py:206
  65.1 0.7 convert_bitcast_fusion.part_ref
  65.7 43.6 %shard_map.127 = f32[1536,24]{1,0:T(8,128)} custom-call(f32[48,24]{1,0:T(8,128)} %convert_bitcast_fusion.part_ref, bf16[48,1536]{1,0:T(8,128)(2,1)} %bitcast.85), custom_call_target="tpu_custom_call" | custom-call | tf_op jit(solution)/shard_map/pallas_call | solution.py:119
  109.4 1.4 multiply_reduce_fusion
  110.8 2.7 %fusion = f32[24,1024]{1,0:T(8,128)S(1)} fusion(bf16[1,1536,1024]{2,1,0:T(8,128)(2,1)} %all-gather.5.cloned.1.call-done, f32[24,1536]{0,1:T(8,128)S(1)} %get-tuple-element.6, f32[1536]{0:T(1024)S(1)} %copy-done.4, f32[24]{0:T(128)S(1)} %add_rsqrt_fusion.1), kind=kOutput, calls=%fused_computation.2 | convolution fusion | flops 75608064 | bytes 3397728 | tf_op jit(solution)/shard_map/dot_general | solution.py:244
  113.4 1.9 %convolution_multiply_fusion = f32[24,1536]{1,0:T(8,128)S(1)} fusion(bf16[1,512,1536]{1,2,0:T(8,128)(2,1)} %all-gather.7.cloned.1.call-done, f32[24]{0:T(128)S(1)} %mul.212, f32[24,1024]{1,0:T(8,128)S(1)} %fusion), kind=kOutput, calls=%fused_computation.4 | convolution fusion | flops 37859328 | bytes 1818720 | tf_op jit(solution)/shard_map/dot_general | solution.py:246
  116.2 18.0 %all_to_all.15 = f32[32,1,1152]{2,1,0:T(1,128)S(1)} all-to-all(f32[32,1,1152]{2,1,0:T(1,128)S(1)} %reshape.283), channel_id=1, replica_groups=mesh['seq'=32,'req'=16] {'seq'}, dimensions={0} | all-to-all | bytes 294912 | tf_op jit(solution)/shard_map/all_to_all | solution.py:62
  134.7 1.0 reduce.4
  (90 shorter events, 11.8 us)
Async XLA Ops:
  6.5 2.7 %copy-start = (bf16[1536,80]{0,1:T(8,128)(2,1)S(1)}, bf16[1536,80]{0,1:T(8,128)(2,1)}, u32[]{:S(2)}) copy-start(bf16[1536,80]{0,1:T(8,128)(2,1)} %param.16) | copy-start | bytes 737284
  6.5 18.0 %copy-start.3 = (bf16[6,128,512]{2,1,0:T(8,128)(2,1)S(1)}, bf16[6,128,512]{2,1,0:T(8,128)(2,1)}, u32[]{:S(2)}) copy-start(bf16[6,128,512]{2,1,0:T(8,128)(2,1)} %param.18) | copy-start | bytes 2359300
  6.5 104.2 %all-gather.5.cloned.1.call-start = ((), (), s32[]{:S(2)}) async-start(), calls=%async_computation.3 | async-start | bytes 3342336 | tf_op jit(solution)/shard_map/all_gather | solution.py:151
  7.3 20.1 %copy-start.5 = (s32[6]{0:T(128)S(1)}, s32[6]{0:T(128)}, u32[]{:S(2)}) copy-start(s32[6]{0:T(128)} %param.21) | copy-start | bytes 76
  11.0 24.5 %all-to-all-start = ((f32[32,24,80]{2,1,0:T(8,128)}), f32[32,24,80]{2,1,0:T(8,128)S(1)}, u32[]{:S(2)}, u32[]{:S(2)}) async-start(f32[32,24,80]{2,1,0:T(8,128)} %broadcast_in_dim.91), calls=%async_computation | async-start | bytes 786432 | tf_op jit(solution)/shard_map/all_to_all | solution.py:53
  21.0 92.4 %all-gather.7.cloned.1.call-start = ((), (), s32[]{:S(2)}) async-start(), calls=%async_computation.4 | async-start | bytes 1671168 | tf_op jit(solution)/shard_map/all_gather | solution.py:152
  35.8 4.2 %copy-start.1 = (f32[24,2560]{1,0:T(8,128)}, f32[24,2560]{1,0:T(8,128)S(1)}, u32[]{:S(2)}) copy-start(f32[24,2560]{1,0:T(8,128)S(1)} %reshape.248) | copy-start | bytes 737284
  40.1 6.7 %slice-start = ((f32[24,2560]{1,0:T(8,128)}), f32[24,512]{1,0:T(8,128)S(1)}, s32[]{:S(2)}) async-start(f32[24,2560]{1,0:T(8,128)} %copy-done.1), calls=%async_computation.5 | async-start | bytes 98304 | tf_op jit(solution)/shard_map/slice | solution.py:164
  40.1 6.9 %copy-start.2 = (f32[24,2560]{1,0:T(8,128)S(1)}, f32[24,2560]{1,0:T(8,128)}, u32[]{:S(2)}) copy-start(f32[24,2560]{1,0:T(8,128)} %copy-done.1) | copy-start | bytes 737284
  41.7 19.0 %all-to-all-start.1 = ((f32[32,24,96]{2,1,0:T(8,128)}), f32[32,24,96]{2,1,0:T(8,128)S(1)}, u32[]{:S(2)}, u32[]{:S(2)}) async-start(f32[32,24,96]{2,1,0:T(8,128)} %pad_maximum_fusion), calls=%async_computation.1 | async-start | bytes 786432 | tf_op jit(solution)/shard_map/all_to_all | solution.py:206
  63.2 47.5 %copy-start.4 = (f32[1536]{0:T(1024)S(1)}, f32[1536]{0:T(1024)}, u32[]{:S(2)}) copy-start(f32[1536]{0:T(1024)} %param.15) | copy-start | bytes 18436
Sparse Core Ops, SparseCore 0:
  9.5 41.8 all-gather.4
  53.5 40.3 all-gather.6

commit v5 on v1

--- a/solution.py
+++ b/solution.py
@@ -45,11 +45,7 @@
 
 
 def gather_columns(part, axis_name):
-    count = lax.axis_size(axis_name)
-    copies = jnp.broadcast_to(part[None], (count,) + part.shape)
-    pieces = lax.all_to_all(copies, axis_name, split_axis=0, concat_axis=0, tiled=True)
-    rows, width = part.shape
-    return jnp.moveaxis(pieces, 0, 1).reshape(rows, count * width)
+    return lax.all_gather(part, axis_name, axis=1, tiled=True)
 
 
 def sum_scatter_columns(value, axis_name):

time: 134 us -> 217 us (1.62)
  the two profiles are of different devices: /device:TPU:8 before, /device:TPU:448 now
where the time goes in v5:
time: 217 us; the launch traced here: 215 us
  blocking collectives  159 us (73%)
  between operations  13.9 us (6%)
  local copies, waits for them, and re-layouts  10.1 us (5%)
  waiting for transfers between devices  10.1 us (5%)
  matrix products  9 us (4%)
  starting transfers between devices  6.88 us (3%)
  other arithmetic  6.29 us (3%)
    all_gather x3, blocking collectives, gather_columns(): return lax.all_gather(part, axis_name, axis=1, tiled=True)  143 us
    all_to_all x1, blocking collectives, sum_scatter_columns(): lax.all_to_all(chunks, axis_name, split_axis=0, concat_axis=0, tiled=True)  16.3 us
    all_to_all x1, waiting for transfers between devices, local(): lax.all_to_all(outgoing, 'seq', split_axis=0, concat_axis=0, tiled=True)  8.68 us
    all_to_all x1, starting transfers between devices, local(): lax.all_to_all(outgoing, 'seq', split_axis=0, concat_axis=0, tiled=True)  6.81 us
  transfers between devices with their start and end apart: 3, of which 1 were waited for; matrix products, arithmetic and copies ran while one was open for 9% of the time, Pallas kernels for 0%

profile of v5, /device:TPU:448, one launch (start us, length us, event | category | flops | bytes accessed | tf_op | source)
XLA Modules:
  0.0 215.5 jit_solution(10925747045508079071)
XLA Ops:
  6.6 0.7 all-gather.8.cloned.1.call-update
  7.3 0.9 reshape.243
  8.2 1.0 multiply_reduce_fusion.2
  9.3 0.9 convolution_bitcast_fusion.3
  10.2 50.3 %all-gather.2 = f32[32,80,24]{1,2,0:T(8,128)S(1)} all-gather(f32[1,80,24]{1,2,0:T(8,128)S(1)} %convolution_bitcast_fusion.3), channel_id=1, replica_groups=mesh['seq'=32,'req'=16] {'seq'}, dimensions={0}, use_global_device_ids=true | all-gather | bytes 253440 | tf_op jit(solution)/shard_map/all_gather | solution.py:48
  61.5 0.7 copy.65
  62.9 1.4 fusion.35
  64.7 0.5 fusion.10
  66.2 0.6 convolution_bitcast_fusion
  67.6 0.9 pad_maximum_fusion
  68.5 6.8 %all-to-all-start = ((f32[32,24,96]{2,1,0:T(8,128)}), f32[32,24,96]{2,1,0:T(8,128)S(1)}, u32[]{:S(2)}, u32[]{:S(2)}) async-start(f32[32,24,96]{2,1,0:T(8,128)} %pad_maximum_fusion), calls=%async_computation | async-start | bytes 786432 | tf_op jit(solution)/shard_map/all_to_all | solution.py:129
  75.4 0.7 all-gather.10.cloned.1.call-update
  76.5 1.1 fusion.36
  78.0 8.7 %all-to-all-done = f32[32,24,96]{2,1,0:T(8,128)S(1)} async-done(((f32[32,24,96]{2,1,0:T(8,128)}), f32[32,24,96]{2,1,0:T(8,128)S(1)}, u32[]{:S(2)}, u32[]{:S(2)}) %all-to-all-start) | async-done | bytes 294944 | tf_op jit(solution)/shard_map/all_to_all | solution.py:129
  89.5 0.6 gather_fusion
  90.1 0.6 gather_fusion.1
  91.2 45.2 %all-gather.3 = bf16[32,48,24]{1,2,0:T(8,128)(2,1)S(1)} all-gather(bf16[1,48,24]{1,2,0:T(8,128)(2,1)S(1)} %copy.87), channel_id=1, replica_groups=mesh['seq'=32,'req'=16] {'seq'}, dimensions={0}, use_global_device_ids=true | all-gather | bytes 76032 | tf_op jit(solution)/shard_map/all_gather | solution.py:48
  136.9 47.4 %all-gather.4 = f32[32,48,24]{1,2,0:T(8,128)S(1)} all-gather(f32[1,48,24]{1,2,0:T(8,128)S(1)} %convolution_bitcast_fusion.2), channel_id=1, replica_groups=mesh['seq'=32,'req'=16] {'seq'}, dimensions={0}, use_global_device_ids=true | all-gather | bytes 152064 | tf_op jit(solution)/shard_map/all_gather | solution.py:48
  184.7 2.5 %fusion = f32[24,1024]{1,0:T(8,128)S(1)} fusion(bf16[1,1536,1024]{2,1,0:T(8,128)(2,1)} %all-gather.8.cloned.1.call-done, f32[24,1536]{1,0:T(8,128)S(1)} %get-tuple-element.6, f32[1536]{0:T(1024)S(1)} %copy-done.9, f32[24]{0:T(128)S(1)} %add_rsqrt_fusion.1), kind=kOutput, calls=%fused_computation.2 | convolution fusion | flops 75608064 | bytes 3397728 | tf_op jit(solution)/shard_map/dot_general | solution.py:170
  187.1 1.9 convolution_multiply_fusion
  189.9 16.3 %all_to_all.10 = f32[32,1,1152]{2,1,0:T(1,128)S(1)} all-to-all(f32[32,1,1152]{2,1,0:T(1,128)S(1)} %reshape.284), channel_id=1, replica_groups=mesh['seq'=32,'req'=16] {'seq'}, dimensions={0} | all-to-all | bytes 294912 | tf_op jit(solution)/shard_map/all_to_all | solution.py:55
  206.2 0.5 broadcast.246
  206.7 1.0 reduce.4
  207.9 0.7 add_convert_fusion.2
  (103 shorter events, 9.6 us)
Async XLA Ops:
  6.5 2.7 %copy-start = (bf16[1536,80]{0,1:T(8,128)(2,1)S(1)}, bf16[1536,80]{0,1:T(8,128)(2,1)}, u32[]{:S(2)}) copy-start(bf16[1536,80]{0,1:T(8,128)(2,1)} %param.16) | copy-start | bytes 737284
  6.5 54.5 %copy-start.11 = (s32[6]{0:T(128)S(1)}, s32[6]{0:T(128)}, u32[]{:S(2)}) copy-start(s32[6]{0:T(128)} %param.21) | copy-start | bytes 76
  6.5 55.7 %copy-start.10 = (s32[6,8]{1,0:T(8,128)S(1)}, s32[6,8]{1,0:T(8,128)}, u32[]{:S(2)}) copy-start(s32[6,8]{1,0:T(8,128)} %param.20) | copy-start | bytes 580
  6.5 55.9 %copy-start.1 = (bf16[6,128,512]{2,1,0:T(8,128)(2,1)S(1)}, bf16[6,128,512]{2,1,0:T(8,128)(2,1)}, u32[]{:S(2)}) copy-start(bf16[6,128,512]{2,1,0:T(8,128)(2,1)} %param.18) | copy-start | bytes 2359300
  6.5 178.1 %all-gather.8.cloned.1.call-start = ((), (), s32[]{:S(2)}) async-start(), calls=%async_computation.2 | async-start | bytes 3342336 | tf_op jit(solution)/shard_map/all_gather | solution.py:74
  60.9 5.0 %copy-start.2 = (bf16[6,128,512]{2,1,0:T(8,128)(2,1)S(1)}, bf16[6,128,512]{2,1,0:T(8,128)(2,1)}, u32[]{:S(2)}) copy-start(bf16[6,128,512]{2,1,0:T(8,128)(2,1)} %param.19) | copy-start | bytes 2359300
  61.2 1.7 copy-start.5
  66.8 9.6 %copy-start.6 = (f32[6,4,32]{2,1,0:T(4,128)S(1)}, f32[6,4,32]{2,1,0:T(4,128)}, u32[]{:S(2)}) copy-start(f32[6,4,32]{2,1,0:T(4,128)} %copy-done.5) | copy-start | bytes 9220
  66.8 9.7 %copy-start.3 = (bf16[6,4,24,32]{3,1,2,0:T(4,128)(2,1)S(1)}, bf16[6,4,24,32]{3,1,2,0:T(4,128)(2,1)}, u32[]{:S(2)}) copy-start(bf16[6,4,24,32]{3,1,2,0:T(4,128)(2,1)} %copy.65) | copy-start | bytes 110596
  66.9 10.9 %copy-start.7 = (f32[6,4,8]{2,1,0:T(4,128)S(1)}, f32[6,4,8]{2,1,0:T(4,128)}, u32[]{:S(2)}) copy-start(f32[6,4,8]{2,1,0:T(4,128)} %param.23) | copy-start | bytes 2308
  66.9 10.9 %copy-start.8 = (s32[6,4,8]{2,1,0:T(4,128)S(1)}, s32[6,4,8]{2,1,0:T(4,128)}, u32[]{:S(2)}) copy-start(s32[6,4,8]{2,1,0:T(4,128)} %param.22) | copy-start | bytes 2308
  68.5 18.2 %all-to-all-start = ((f32[32,24,96]{2,1,0:T(8,128)}), f32[32,24,96]{2,1,0:T(8,128)S(1)}, u32[]{:S(2)}, u32[]{:S(2)}) async-start(f32[32,24,96]{2,1,0:T(8,128)} %pad_maximum_fusion), calls=%async_computation | async-start | bytes 786432 | tf_op jit(solution)/shard_map/all_to_all | solution.py:129
  75.3 111.8 %all-gather.10.cloned.1.call-start = ((), (), s32[]{:S(2)}) async-start(), calls=%async_computation.3 | async-start | bytes 1671168 | tf_op jit(solution)/shard_map/all_gather | solution.py:75
  88.3 48.4 %copy-start.4 = (bf16[1536,48]{0,1:T(8,128)(2,1)S(1)}, bf16[1536,48]{0,1:T(8,128)(2,1)}, u32[]{:S(2)}) copy-start(bf16[1536,48]{0,1:T(8,128)(2,1)} %param.17) | copy-start | bytes 442372
  89.2 95.5 %copy-start.9 = (f32[1536]{0:T(1024)S(1)}, f32[1536]{0:T(1024)}, u32[]{:S(2)}) copy-start(f32[1536]{0:T(1024)} %param.15) | copy-start | bytes 18436
Sparse Core Ops, SparseCore 0:
  9.5 41.6 all-gather.7
  78.3 39.3 all-gather.9

commit v6 on v1

--- a/solution.py
+++ b/solution.py
@@ -75,8 +75,11 @@
     w_gate_up,
     w_down,
 ):
-    expert_in = lax.all_gather(w_gate_up[0], "req", axis=0, tiled=True)
-    expert_out = lax.all_gather(w_down[0], "req", axis=1, tiled=True)
+    expert_both = lax.all_gather(
+        jnp.concatenate([w_gate_up[0], w_down[0].T], axis=1), "req", axis=0, tiled=True
+    )
+    expert_in = expert_both[:, : 2 * FFE]
+    expert_out_t = expert_both[:, 2 * FFE :]
 
     seq_count = lax.axis_size("seq")
     me = lax.axis_index("seq")
@@ -173,7 +176,9 @@
     route_scale = jnp.sum(jnp.where(chosen == expert, gates, 0.0), axis=-1)
     gate_up = jnp.dot(mixed_in, expert_in, preferred_element_type=jnp.float32)
     hidden = (jax.nn.silu(gate_up[:, :FFE]) * gate_up[:, FFE:]).astype(jnp.bfloat16)
-    produced = jnp.dot(hidden, expert_out, preferred_element_type=jnp.float32)
+    produced = lax.dot_general(
+        hidden, expert_out_t, (((1,), (1,)), ((), ())), preferred_element_type=jnp.float32
+    )
     own_share = sum_scatter_columns(route_scale[:, None] * produced, "seq")
     share_width = own_share.shape[1]
     resid_share = lax.dynamic_slice_in_dim(resid, me * share_width, share_width, 1)

time: 134 us -> 128 us (0.955)
  the two profiles are of different devices: /device:TPU:8 before, /device:TPU:448 now
where the time goes in v6:
time: 128 us; the launch traced here: 127 us
  waiting for transfers between devices  32.9 us (26%)
  blocking collectives  29.1 us (23%)
  starting transfers between devices  19.1 us (15%)
  between operations  13.9 us (11%)
  local copies, waits for them, and re-layouts  13.6 us (11%)
  other arithmetic  10.4 us (8%)
  matrix products  8.09 us (6%)
    all_to_all x2, waiting for transfers between devices, gather_columns(): lax.all_to_all(copies, axis_name, split_axis=0, concat_axis=0, tiled=True)  20.6 us
    all_to_all x1, blocking collectives, gather_columns(): lax.all_to_all(copies, axis_name, split_axis=0, concat_axis=0, tiled=True)  15.1 us
    all_to_all x1, blocking collectives, sum_scatter_columns(): lax.all_to_all(chunks, axis_name, split_axis=0, concat_axis=0, tiled=True)  14 us
    all_to_all x2, starting transfers between devices, gather_columns(): lax.all_to_all(copies, axis_name, split_axis=0, concat_axis=0, tiled=True)  14 us
    all_to_all x1, waiting for transfers between devices, local(): lax.all_to_all(outgoing, 'seq', split_axis=0, concat_axis=0, tiled=True)  12.3 us
    all_to_all x1, starting transfers between devices, local(): lax.all_to_all(outgoing, 'seq', split_axis=0, concat_axis=0, tiled=True)  5.13 us
    unnamed x29, local copies, waits for them, and re-layouts  5.04 us
  transfers between devices with their start and end apart: 4, of which 3 were waited for; matrix products, arithmetic and copies ran while one was open for 18% of the time, Pallas kernels for 0%

profile of v6, /device:TPU:448, one launch (start us, length us, event | category | flops | bytes accessed | tf_op | source)
XLA Modules:
  0.0 127.1 jit_solution(5797062609684549817)
XLA Ops:
  6.5 1.8 %pad_maximum_fusion.1 = bf16[96,1536]{1,0:T(8,128)(2,1)} fusion(bf16[96,512]{1,0:T(8,128)(2,1)} %bitcast.82, bf16[96,1024]{1,0:T(8,128)(2,1)} %bitcast.81), kind=kLoop, calls=%fused_computation.18 | loop fusion | flops 589824 | bytes 589824 | tf_op jit(solution)/shard_map/concatenate | solution.py:79
  8.4 0.9 reshape.267
  9.3 1.0 multiply_reduce_fusion.2
  10.4 0.9 fusion.18
  11.3 0.8 broadcast_in_dim.66
  12.1 10.0 %all-to-all-start = ((f32[32,24,80]{2,1,0:T(8,128)}), f32[32,24,80]{2,1,0:T(8,128)S(1)}, u32[]{:S(2)}, u32[]{:S(2)}) async-start(f32[32,24,80]{2,1,0:T(8,128)} %broadcast_in_dim.66), calls=%async_computation | async-start | bytes 786432 | tf_op jit(solution)/shard_map/all_to_all | solution.py:50
  22.1 0.7 add_convert_fusion.3
  22.8 0.7 broadcast_multiply_fusion
  23.8 1.5 %copy.66 = bf16[6,128,512]{1,2,0:T(8,128)(2,1)S(1)} copy(bf16[6,128,512]{2,1,0:T(8,128)(2,1)} %param.18) | data formatting | bytes 1572864 | tf_op args[5]
  26.0 10.6 %all-to-all-done = f32[32,24,80]{2,1,0:T(8,128)S(1)} async-done(((f32[32,24,80]{2,1,0:T(8,128)}), f32[32,24,80]{2,1,0:T(8,128)S(1)}, u32[]{:S(2)}, u32[]{:S(2)}) %all-to-all-start) | async-done | bytes 245792 | tf_op jit(solution)/shard_map/all_to_all | solution.py:50
  40.7 0.9 pad_maximum_fusion
  41.6 5.1 %all-to-all-start.1 = ((f32[32,24,96]{2,1,0:T(8,128)}), f32[32,24,96]{2,1,0:T(8,128)S(1)}, u32[]{:S(2)}, u32[]{:S(2)}) async-start(f32[32,24,96]{2,1,0:T(8,128)} %pad_maximum_fusion), calls=%async_computation.1 | async-start | bytes 786432 | tf_op jit(solution)/shard_map/all_to_all | solution.py:136
  47.1 1.1 fusion.36
  48.4 12.3 %all-to-all-done.1 = f32[32,24,96]{2,1,0:T(8,128)S(1)} async-done(((f32[32,24,96]{2,1,0:T(8,128)}), f32[32,24,96]{2,1,0:T(8,128)S(1)}, u32[]{:S(2)}, u32[]{:S(2)}) %all-to-all-start.1) | async-done | bytes 294944 | tf_op jit(solution)/shard_map/all_to_all | solution.py:136
  65.5 15.1 %all_to_all.25 = bf16[32,2,576]{2,1,0:T(2,128)(2,1)S(1)} all-to-all(bf16[32,2,576]{2,1,0:T(2,128)(2,1)S(1)} %reshape.304), channel_id=1, replica_groups=mesh['seq'=32,'req'=16] {'seq'}, dimensions={0} | all-to-all | bytes 147456 | tf_op jit(solution)/shard_map/all_to_all | solution.py:50
  81.3 1.1 reshape.306
  82.4 4.0 %all-to-all-start.3 = ((f32[32,1,1152]{2,1,0:T(1,128)}), f32[32,1,1152]{2,1,0:T(1,128)S(1)}, u32[]{:S(2)}, u32[]{:S(2)}) async-start(f32[32,1,1152]{2,1,0:T(1,128)} %reshape.306), calls=%async_computation.3 | async-start | bytes 294912 | tf_op jit(solution)/shard_map/all_to_all | solution.py:50
  86.6 10.0 %all-to-all-done.3 = f32[32,1,1152]{2,1,0:T(1,128)S(1)} async-done(((f32[32,1,1152]{2,1,0:T(1,128)}), f32[32,1,1152]{2,1,0:T(1,128)S(1)}, u32[]{:S(2)}, u32[]{:S(2)}) %all-to-all-start.3) | async-done | bytes 147488 | tf_op jit(solution)/shard_map/all_to_all | solution.py:50
  97.1 1.0 reduce.5
  99.1 2.5 %fusion = f32[24,1024]{1,0:T(8,128)S(1)} fusion(bf16[1536,1536]{1,0:T(8,128)(2,1)} %all-gather.2.cloned.1.call-done, f32[24,1536]{1,0:T(8,128)S(1)} %add.165, f32[1536]{0:T(1024)S(1)} %copy-done.6, f32[24]{0:T(128)S(1)} %rsqrt.25), kind=kOutput, calls=%fused_computation.2 | convolution fusion | flops 75608064 | bytes 3397728 | tf_op jit(solution)/shard_map/dot_general | solution.py:177
  101.6 1.9 %convolution_multiply_fusion = f32[24,1536]{1,0:T(8,128)S(1)} fusion(bf16[1536,1536]{1,0:T(8,128)(2,1)} %all-gather.2.cloned.1.call-done, f32[24]{0:T(128)S(1)} %mul.213, f32[24,1024]{1,0:T(8,128)S(1)} %fusion), kind=kOutput, calls=%fused_computation.4 | convolution fusion | flops 37859328 | bytes 1818720 | tf_op jit(solution)/shard_map/dot_general | solution.py:179
  104.3 14.0 %all_to_all.26 = f32[32,1,1152]{2,1,0:T(1,128)S(1)} all-to-all(f32[32,1,1152]{2,1,0:T(1,128)S(1)} %reshape.308), channel_id=1, replica_groups=mesh['seq'=32,'req'=16] {'seq'}, dimensions={0} | all-to-all | bytes 294912 | tf_op jit(solution)/shard_map/all_to_all | solution.py:59
  118.4 1.0 reduce.6
  119.6 0.7 add_convert_fusion.2
  (106 shorter events, 13.6 us)
Async XLA Ops:
  6.5 3.8 %copy-start = (bf16[1536,80]{0,1:T(8,128)(2,1)S(1)}, bf16[1536,80]{0,1:T(8,128)(2,1)}, u32[]{:S(2)}) copy-start(bf16[1536,80]{0,1:T(8,128)(2,1)} %param.16) | copy-start | bytes 737284
  6.5 19.2 %copy-start.7 = (s32[6]{0:T(128)S(1)}, s32[6]{0:T(128)}, u32[]{:S(2)}) copy-start(s32[6]{0:T(128)} %param.21) | copy-start | bytes 76
  6.5 18.8 %copy-start.1 = (bf16[6,128,512]{2,1,0:T(8,128)(2,1)S(1)}, bf16[6,128,512]{2,1,0:T(8,128)(2,1)}, u32[]{:S(2)}) copy-start(bf16[6,128,512]{2,1,0:T(8,128)(2,1)} %param.19) | copy-start | bytes 2359300
  6.5 92.6 %all-gather.2.cloned.1.call-start = ((), (), s32[]{:S(2)}) async-start(), calls=%async_computation.5 | async-start | bytes 5013504 | tf_op jit(solution)/shard_map/all_gather | solution.py:78
  12.1 24.5 %all-to-all-start = ((f32[32,24,80]{2,1,0:T(8,128)}), f32[32,24,80]{2,1,0:T(8,128)S(1)}, u32[]{:S(2)}, u32[]{:S(2)}) async-start(f32[32,24,80]{2,1,0:T(8,128)} %broadcast_in_dim.66), calls=%async_computation | async-start | bytes 786432 | tf_op jit(solution)/shard_map/all_to_all | solution.py:50
  41.6 19.0 %all-to-all-start.1 = ((f32[32,24,96]{2,1,0:T(8,128)}), f32[32,24,96]{2,1,0:T(8,128)S(1)}, u32[]{:S(2)}, u32[]{:S(2)}) async-start(f32[32,24,96]{2,1,0:T(8,128)} %pad_maximum_fusion), calls=%async_computation.1 | async-start | bytes 786432 | tf_op jit(solution)/shard_map/all_to_all | solution.py:136
  61.5 19.6 %copy-start.3 = (bf16[1536,48]{0,1:T(8,128)(2,1)S(1)}, bf16[1536,48]{0,1:T(8,128)(2,1)}, u32[]{:S(2)}) copy-start(bf16[1536,48]{0,1:T(8,128)(2,1)} %param.17) | copy-start | bytes 442372
  62.1 24.4 %copy-start.4 = (f32[6,4,8]{2,1,0:T(4,128)S(1)}, f32[6,4,8]{2,1,0:T(4,128)}, u32[]{:S(2)}) copy-start(f32[6,4,8]{2,1,0:T(4,128)} %param.23) | copy-start | bytes 2308
  62.1 24.4 %copy-start.5 = (s32[6,4,8]{2,1,0:T(4,128)S(1)}, s32[6,4,8]{2,1,0:T(4,128)}, u32[]{:S(2)}) copy-start(s32[6,4,8]{2,1,0:T(4,128)} %param.22) | copy-start | bytes 2308
  63.2 35.7 %copy-start.2 = (bf16[6,4,1536]{2,1,0:T(4,128)(2,1)S(1)}, bf16[6,4,1536]{2,1,0:T(4,128)(2,1)}, u32[]{:S(2)}) copy-start(bf16[6,4,1536]{2,1,0:T(4,128)(2,1)} %param.13) | copy-start | bytes 221188
  63.2 35.9 %copy-start.6 = (f32[1536]{0:T(1024)S(1)}, f32[1536]{0:T(1024)}, u32[]{:S(2)}) copy-start(f32[1536]{0:T(1024)} %param.15) | copy-start | bytes 18436
  82.4 14.2 %all-to-all-start.3 = ((f32[32,1,1152]{2,1,0:T(1,128)}), f32[32,1,1152]{2,1,0:T(1,128)S(1)}, u32[]{:S(2)}, u32[]{:S(2)}) async-start(f32[32,1,1152]{2,1,0:T(1,128)} %reshape.306), calls=%async_computation.3 | async-start | bytes 294912 | tf_op jit(solution)/shard_map/all_to_all | solution.py:50
Sparse Core Ops, SparseCore 0:
  9.5 43.8 all-gather.1

commit v7 on v6

--- a/solution.py
+++ b/solution.py
@@ -1,6 +1,7 @@
 import math
 
 import jax
+import numpy as np
 import jax.numpy as jnp
 from jax import lax
 from jax.sharding import PartitionSpec as P
@@ -127,41 +128,49 @@
     local_top = local_top.reshape(row_count, HEADS)
 
     width = ATT // seq_count
+    first_head = np.arange(seq_count) * width // HD
+    last_head = (np.arange(seq_count) * width + width - 1) // HD
+    pair = np.stack([first_head, last_head], axis=1)
     sum_chunks = jnp.moveaxis(local_sums.reshape(row_count, seq_count, width), 1, 0)
-    extras = jnp.broadcast_to(
-        jnp.concatenate([local_total, local_top], axis=1)[None],
-        (seq_count, row_count, 2 * HEADS),
-    )
-    outgoing = jnp.concatenate([sum_chunks, extras], axis=2)
+    pair_totals = jnp.moveaxis(local_total[:, pair], 1, 0)
+    pair_tops = jnp.moveaxis(local_top[:, pair], 1, 0)
+    outgoing = jnp.concatenate([sum_chunks, pair_totals, pair_tops], axis=2)
     arrived = lax.all_to_all(outgoing, "seq", split_axis=0, concat_axis=0, tiled=True)
     part_sums = arrived[:, :, :width]
-    part_totals = arrived[:, :, width : width + HEADS]
-    part_tops = arrived[:, :, width + HEADS :]
-
+    part_totals = arrived[:, :, width : width + 2]
+    part_tops = arrived[:, :, width + 2 :]
+
+    start = me * width
+    my_pair = jnp.stack([start // HD, (start + width - 1) // HD])
     causal = (
         jnp.arange(NSTEP, dtype=jnp.int32)[:, None] >= jnp.arange(NSTEP, dtype=jnp.int32)[None, :]
-    )[None, :, None, None, :]
+    )[None, :, None, :]
+    pair_queries = jnp.take(
+        queries.reshape(local_requests, NSTEP, HEADS, HD), my_pair, axis=2
+    )
+    pair_keys = jnp.take(keys_new, my_pair // GROUP, axis=2)
+    pair_values = jnp.take(values_new, my_pair // GROUP, axis=2)
     fresh = (
-        jnp.einsum("rskgd,rukd->rskgu", queries, keys_new, preferred_element_type=jnp.float32)
+        jnp.einsum("rspd,rupd->rspu", pair_queries, pair_keys, preferred_element_type=jnp.float32)
         * scale
     )
-    fresh = jnp.where(causal, fresh, NEG).reshape(row_count, HEADS, NSTEP)
+    fresh = jnp.where(causal, fresh, NEG).reshape(row_count, 2, NSTEP)
     cache_top = jnp.max(part_tops, axis=0)
     highest = jnp.maximum(cache_top, jnp.max(fresh, axis=-1))
     factors = jnp.exp(part_tops - highest[None])
     fresh_exp = jnp.exp(fresh - highest[:, :, None])
     denominator = jnp.sum(part_totals * factors, axis=0) + jnp.sum(fresh_exp, axis=-1)
-    fresh_probs = fresh_exp.reshape(local_requests, NSTEP, KVH, GROUP, NSTEP).astype(jnp.bfloat16)
+    fresh_probs = fresh_exp.reshape(local_requests, NSTEP, 2, NSTEP).astype(jnp.bfloat16)
     fresh_sums = jnp.einsum(
-        "rskgu,rukd->rskgd", fresh_probs, values_new, preferred_element_type=jnp.float32
-    ).reshape(row_count, ATT)
-    start = me * width
-    head_of = (start + jnp.arange(width, dtype=jnp.int32)) // HD
-    chunk_factors = jnp.take(factors, head_of, axis=2)
-    numerator = jnp.sum(part_sums * chunk_factors, axis=0) + lax.dynamic_slice_in_dim(
-        fresh_sums, start, width, 1
-    )
-    chunk_denominator = jnp.take(denominator, head_of, axis=1)
+        "rspu,rupd->rspd", fresh_probs, pair_values, preferred_element_type=jnp.float32
+    ).reshape(row_count, 2 * HD)
+    feature = start + jnp.arange(width, dtype=jnp.int32)
+    side = feature // HD - my_pair[0]
+    chunk_factors = jnp.take(factors, side, axis=2)
+    numerator = jnp.sum(part_sums * chunk_factors, axis=0) + jnp.take(
+        fresh_sums, side * HD + feature % HD, axis=1
+    )
+    chunk_denominator = jnp.take(denominator, side, axis=1)
     attended_part = (numerator / chunk_denominator).astype(jnp.bfloat16)
     attended = gather_columns(attended_part, "seq")
     attn_mixed = gather_columns(

time: 128 us -> 129 us (level)
  blocking collectives: 29.1 us -> 13.7 us
  local copies, waits for them, and re-layouts: 13.6 us -> 19.1 us
  other arithmetic: 10.4 us -> 14.4 us
  starting transfers between devices: 19.1 us -> 23 us
  waiting for transfers between devices: 32.9 us -> 36.6 us
    all_to_all x1 -> x0, blocking collectives: 14 us -> none  [sum_scatter_columns(): lax.all_to_all(chunks, axis_name, split_axis=0, concat_axis=0, tiled=True)]
    all_to_all x0 -> x1, waiting for transfers between devices: none -> 10.3 us  [sum_scatter_columns(): lax.all_to_all(chunks, axis_name, split_axis=0, concat_axis=0, tiled=True)]
    gather x2 -> x10, local copies, waits for them, and re-layouts: 1.19 us -> 5.83 us  [the longest x2 1.03 us: local(): pair_tops = jnp.moveaxis(local_top[:, pair], 1, 0)]
    all_to_all x0 -> x1, starting transfers between devices: none -> 3.89 us  [sum_scatter_columns(): lax.all_to_all(chunks, axis_name, split_axis=0, concat_axis=0, tiled=True)]
    all_to_all x2, waiting for transfers between devices: 20.6 us -> 16.9 us  [gather_columns(): lax.all_to_all(copies, axis_name, split_axis=0, concat_axis=0, tiled=True)]
    all_to_all x1, waiting for transfers between devices: 12.3 us -> 9.27 us  [local(): lax.all_to_all(outgoing, 'seq', split_axis=0, concat_axis=0, tiled=True)]
    unnamed x29 -> x40, local copies, waits for them, and re-layouts: 5.04 us -> 6.99 us
    gather x1 -> x5, other arithmetic: 0.01 us -> 1.86 us  [the longest x1 0.66 us: local(): pair_totals = jnp.moveaxis(local_total[:, pair], 1, 0)]
  transfers between devices with their start and end apart: 4 -> 5, of which waited for: 3 -> 4; matrix products, arithmetic and copies ran while one was open for 18% -> 24% of each run, Pallas kernels for 0% -> 0%
where the time goes in v7:
time: 129 us; the launch traced here: 128 us
  waiting for transfers between devices  36.6 us (28%)
  starting transfers between devices  23 us (18%)
  local copies, waits for them, and re-layouts  19.1 us (15%)
  other arithmetic  14.4 us (11%)
  between operations  14 us (11%)
  blocking collectives  13.7 us (11%)
  matrix products  7.02 us (5%)
    all_to_all x2, waiting for transfers between devices, gather_columns(): lax.all_to_all(copies, axis_name, split_axis=0, concat_axis=0, tiled=True)  16.9 us
    all_to_all x2, starting transfers between devices, gather_columns(): lax.all_to_all(copies, axis_name, split_axis=0, concat_axis=0, tiled=True)  14 us
    all_to_all x1, blocking collectives, gather_columns(): lax.all_to_all(copies, axis_name, split_axis=0, concat_axis=0, tiled=True)  13.7 us
    all_to_all x1, waiting for transfers between devices, sum_scatter_columns(): lax.all_to_all(chunks, axis_name, split_axis=0, concat_axis=0, tiled=True)  10.3 us
    all_to_all x1, waiting for transfers between devices, local(): lax.all_to_all(outgoing, 'seq', split_axis=0, concat_axis=0, tiled=True)  9.27 us
    unnamed x40, local copies, waits for them, and re-layouts  6.99 us
    all_to_all x1, starting transfers between devices, local(): lax.all_to_all(outgoing, 'seq', split_axis=0, concat_axis=0, tiled=True)  5.13 us
    all_to_all x1, starting transfers between devices, sum_scatter_columns(): lax.all_to_all(chunks, axis_name, split_axis=0, concat_axis=0, tiled=True)  3.89 us
  transfers between devices with their start and end apart: 5, of which 4 were waited for; matrix products, arithmetic and copies ran while one was open for 24% of the time, Pallas kernels for 0%

profile of v7, /device:TPU:448, one launch (start us, length us, event | category | flops | bytes accessed | tf_op | source)
XLA Modules:
  0.0 127.8 jit_solution(404382198978012065)
XLA Ops:
  6.5 1.8 %pad_maximum_fusion.1 = bf16[96,1536]{1,0:T(8,128)(2,1)} fusion(bf16[96,512]{1,0:T(8,128)(2,1)} %bitcast.99, bf16[96,1024]{1,0:T(8,128)(2,1)} %bitcast.98), kind=kLoop, calls=%fused_computation.24 | loop fusion | flops 589824 | bytes 589824 | tf_op jit(solution)/shard_map/concatenate | solution.py:80
  8.4 0.9 reshape.447
  9.3 1.0 multiply_reduce_fusion.1
  10.4 0.9 fusion.17
  11.3 0.8 broadcast_in_dim.130
  12.1 10.0 %all-to-all-start = ((f32[32,24,80]{2,1,0:T(8,128)}), f32[32,24,80]{2,1,0:T(8,128)S(1)}, u32[]{:S(2)}, u32[]{:S(2)}) async-start(f32[32,24,80]{2,1,0:T(8,128)} %broadcast_in_dim.130), calls=%async_computation | async-start | bytes 786432 | tf_op jit(solution)/shard_map/all_to_all | solution.py:51
  25.3 0.7 add_convert_fusion.3
  27.5 1.5 %copy.101 = bf16[6,128,512]{1,2,0:T(8,128)(2,1)S(1)} copy(bf16[6,128,512]{2,1,0:T(8,128)(2,1)} %param.23) | data formatting | bytes 1572864 | tf_op args[5]
  29.6 7.0 %all-to-all-done = f32[32,24,80]{2,1,0:T(8,128)S(1)} async-done(((f32[32,24,80]{2,1,0:T(8,128)}), f32[32,24,80]{2,1,0:T(8,128)S(1)}, u32[]{:S(2)}, u32[]{:S(2)}) %all-to-all-start) | async-done | bytes 245792 | tf_op jit(solution)/shard_map/all_to_all | solution.py:51
  43.9 1.1 reshape.537
  45.0 5.1 %all-to-all-start.1 = ((f32[32,1,1248]{2,1,0:T(1,128)}), f32[32,1,1248]{2,1,0:T(1,128)S(1)}, u32[]{:S(2)}, u32[]{:S(2)}) async-start(f32[32,1,1248]{2,1,0:T(1,128)} %reshape.537), calls=%async_computation.1 | async-start | bytes 327680 | tf_op jit(solution)/shard_map/all_to_all | solution.py:138
  51.5 9.3 %all-to-all-done.1 = f32[32,1,1248]{2,1,0:T(1,128)S(1)} async-done(((f32[32,1,1248]{2,1,0:T(1,128)}), f32[32,1,1248]{2,1,0:T(1,128)S(1)}, u32[]{:S(2)}, u32[]{:S(2)}) %all-to-all-start.1) | async-done | bytes 159776 | tf_op jit(solution)/shard_map/all_to_all | solution.py:138
  61.3 1.0 reduce.5
  67.2 13.7 %all_to_all.25 = bf16[32,2,576]{2,1,0:T(2,128)(2,1)S(1)} all-to-all(bf16[32,2,576]{2,1,0:T(2,128)(2,1)S(1)} %reshape.539), channel_id=1, replica_groups=mesh['seq'=32,'req'=16] {'seq'}, dimensions={0} | all-to-all | bytes 147456 | tf_op jit(solution)/shard_map/all_to_all | solution.py:51
  81.6 1.1 reshape.541
  82.7 4.0 %all-to-all-start.3 = ((f32[32,1,1152]{2,1,0:T(1,128)}), f32[32,1,1152]{2,1,0:T(1,128)S(1)}, u32[]{:S(2)}, u32[]{:S(2)}) async-start(f32[32,1,1152]{2,1,0:T(1,128)} %reshape.541), calls=%async_computation.3 | async-start | bytes 294912 | tf_op jit(solution)/shard_map/all_to_all | solution.py:51
  86.9 10.0 %all-to-all-done.3 = f32[32,1,1152]{2,1,0:T(1,128)S(1)} async-done(((f32[32,1,1152]{2,1,0:T(1,128)}), f32[32,1,1152]{2,1,0:T(1,128)S(1)}, u32[]{:S(2)}, u32[]{:S(2)}) %all-to-all-start.3) | async-done | bytes 147488 | tf_op jit(solution)/shard_map/all_to_all | solution.py:51
  96.9 1.0 reduce.6
  98.9 2.5 %fusion = f32[24,1024]{1,0:T(8,128)S(1)} fusion(bf16[1536,1536]{1,0:T(8,128)(2,1)} %all-gather.2.cloned.1.call-done, f32[24,1536]{1,0:T(8,128)S(1)} %add.271, f32[1536]{0:T(1024)S(1)} %copy-done.6, f32[24]{0:T(128)S(1)} %rsqrt.25), kind=kOutput, calls=%fused_computation.8 | convolution fusion | flops 75608064 | bytes 3397728 | tf_op jit(solution)/shard_map/dot_general | solution.py:186
  101.4 1.9 %convolution_multiply_fusion = f32[24,1536]{1,0:T(8,128)S(1)} fusion(bf16[1536,1536]{1,0:T(8,128)(2,1)} %all-gather.2.cloned.1.call-done, f32[24]{0:T(128)S(1)} %mul.230, f32[24,1024]{1,0:T(8,128)S(1)} %fusion), kind=kOutput, calls=%fused_computation.10 | convolution fusion | flops 37859328 | bytes 1818720 | tf_op jit(solution)/shard_map/dot_general | solution.py:188
  103.7 1.0 reshape.543
  104.8 3.9 %all-to-all-start.4 = ((f32[32,1,1152]{2,1,0:T(1,128)}), f32[32,1,1152]{2,1,0:T(1,128)S(1)}, u32[]{:S(2)}, u32[]{:S(2)}) async-start(f32[32,1,1152]{2,1,0:T(1,128)} %reshape.543), calls=%async_computation.4 | async-start | bytes 294912 | tf_op jit(solution)/shard_map/all_to_all | solution.py:60
  108.7 10.3 %all-to-all-done.4 = f32[32,1,1152]{2,1,0:T(1,128)S(1)} async-done(((f32[32,1,1152]{2,1,0:T(1,128)}), f32[32,1,1152]{2,1,0:T(1,128)S(1)}, u32[]{:S(2)}, u32[]{:S(2)}) %all-to-all-start.4) | async-done | bytes 147488 | tf_op jit(solution)/shard_map/all_to_all | solution.py:60
  119.0 1.0 reduce.7
  (134 shorter events, 22.3 us)
Async XLA Ops:
  6.5 3.8 %copy-start = (bf16[1536,80]{0,1:T(8,128)(2,1)S(1)}, bf16[1536,80]{0,1:T(8,128)(2,1)}, u32[]{:S(2)}) copy-start(bf16[1536,80]{0,1:T(8,128)(2,1)} %param.21) | copy-start | bytes 737284
  6.5 22.8 %copy-start.10 = (s32[6]{0:T(128)S(1)}, s32[6]{0:T(128)}, u32[]{:S(2)}) copy-start(s32[6]{0:T(128)} %param.26) | copy-start | bytes 76
  6.5 22.4 %copy-start.1 = (bf16[6,128,512]{2,1,0:T(8,128)(2,1)S(1)}, bf16[6,128,512]{2,1,0:T(8,128)(2,1)}, u32[]{:S(2)}) copy-start(bf16[6,128,512]{2,1,0:T(8,128)(2,1)} %param.24) | copy-start | bytes 2359300
  6.5 92.4 %all-gather.2.cloned.1.call-start = ((), (), s32[]{:S(2)}) async-start(), calls=%async_computation.5 | async-start | bytes 5013504 | tf_op jit(solution)/shard_map/all_gather | solution.py:79
  12.1 24.5 %all-to-all-start = ((f32[32,24,80]{2,1,0:T(8,128)}), f32[32,24,80]{2,1,0:T(8,128)S(1)}, u32[]{:S(2)}, u32[]{:S(2)}) async-start(f32[32,24,80]{2,1,0:T(8,128)} %broadcast_in_dim.130), calls=%async_computation | async-start | bytes 786432 | tf_op jit(solution)/shard_map/all_to_all | solution.py:51
  41.9 8.3 %copy-start.8 = (pred[2]{0:T(512)(128)(4,1)S(1)}, pred[2]{0:T(512)(128)(4,1)}, u32[]{:S(2)}) copy-start(pred[2]{0:T(512)(128)(4,1)} %get-tuple-element.8) | copy-start | bytes 10
  41.9 9.3 %copy-start.11 = (pred[2]{0:T(512)(128)(4,1)S(1)}, pred[2]{0:T(512)(128)(4,1)}, u32[]{:S(2)}) copy-start(pred[2]{0:T(512)(128)(4,1)} %get-tuple-element.33) | copy-start | bytes 10
  41.9 9.3 %copy-start.12 = (pred[4,4]{0,1:T(4,128)(4,1)S(1)}, pred[4,4]{0,1:T(4,128)(4,1)}, u32[]{:S(2)}) copy-start(pred[4,4]{0,1:T(4,128)(4,1)} %iota_compare_fusion) | copy-start | bytes 52
  43.4 23.0 %copy-start.7 = (pred[48]{0:T(512)(128)(4,1)S(1)}, pred[48]{0:T(512)(128)(4,1)}, u32[]{:S(2)}) copy-start(pred[48]{0:T(512)(128)(4,1)} %get-tuple-element.30) | copy-start | bytes 148
  43.7 23.0 %copy-start.9 = (pred[48]{0:T(512)(128)(4,1)S(1)}, pred[48]{0:T(512)(128)(4,1)}, u32[]{:S(2)}) copy-start(pred[48]{0:T(512)(128)(4,1)} %get-tuple-element.29) | copy-start | bytes 148
  45.0 15.8 %all-to-all-start.1 = ((f32[32,1,1248]{2,1,0:T(1,128)}), f32[32,1,1248]{2,1,0:T(1,128)S(1)}, u32[]{:S(2)}, u32[]{:S(2)}) async-start(f32[32,1,1248]{2,1,0:T(1,128)} %reshape.537), calls=%async_computation.1 | async-start | bytes 327680 | tf_op jit(solution)/shard_map/all_to_all | solution.py:138
  50.1 31.3 %copy-start.3 = (bf16[1536,48]{0,1:T(8,128)(2,1)S(1)}, bf16[1536,48]{0,1:T(8,128)(2,1)}, u32[]{:S(2)}) copy-start(bf16[1536,48]{0,1:T(8,128)(2,1)} %param.22) | copy-start | bytes 442372
  62.5 24.2 %copy-start.4 = (f32[6,4,8]{2,1,0:T(4,128)S(1)}, f32[6,4,8]{2,1,0:T(4,128)}, u32[]{:S(2)}) copy-start(f32[6,4,8]{2,1,0:T(4,128)} %param.28) | copy-start | bytes 2308
  62.5 24.2 %copy-start.5 = (s32[6,4,8]{2,1,0:T(4,128)S(1)}, s32[6,4,8]{2,1,0:T(4,128)}, u32[]{:S(2)}) copy-start(s32[6,4,8]{2,1,0:T(4,128)} %param.27) | copy-start | bytes 2308
  64.7 33.9 %copy-start.2 = (bf16[6,4,1536]{2,1,0:T(4,128)(2,1)S(1)}, bf16[6,4,1536]{2,1,0:T(4,128)(2,1)}, u32[]{:S(2)}) copy-start(bf16[6,4,1536]{2,1,0:T(4,128)(2,1)} %param.18) | copy-start | bytes 221188
  64.7 34.2 %copy-start.6 = (f32[1536]{0:T(1024)S(1)}, f32[1536]{0:T(1024)}, u32[]{:S(2)}) copy-start(f32[1536]{0:T(1024)} %param.20) | copy-start | bytes 18436
  82.7 14.2 %all-to-all-start.3 = ((f32[32,1,1152]{2,1,0:T(1,128)}), f32[32,1,1152]{2,1,0:T(1,128)S(1)}, u32[]{:S(2)}, u32[]{:S(2)}) async-start(f32[32,1,1152]{2,1,0:T(1,128)} %reshape.541), calls=%async_computation.3 | async-start | bytes 294912 | tf_op jit(solution)/shard_map/all_to_all | solution.py:51
  104.8 14.2 %all-to-all-start.4 = ((f32[32,1,1152]{2,1,0:T(1,128)}), f32[32,1,1152]{2,1,0:T(1,128)S(1)}, u32[]{:S(2)}, u32[]{:S(2)}) async-start(f32[32,1,1152]{2,1,0:T(1,128)} %reshape.543), calls=%async_computation.4 | async-start | bytes 294912 | tf_op jit(solution)/shard_map/all_to_all | solution.py:60
Sparse Core Ops, SparseCore 0:
  9.5 43.8 all-gather.1

commit v8 on v6

--- a/solution.py
+++ b/solution.py
@@ -127,16 +127,15 @@
     local_top = local_top.reshape(row_count, HEADS)
 
     width = ATT // seq_count
+    pair_starts = [min(c * width // HD, HEADS - 2) for c in range(seq_count)]
     sum_chunks = jnp.moveaxis(local_sums.reshape(row_count, seq_count, width), 1, 0)
-    extras = jnp.broadcast_to(
-        jnp.concatenate([local_total, local_top], axis=1)[None],
-        (seq_count, row_count, 2 * HEADS),
-    )
-    outgoing = jnp.concatenate([sum_chunks, extras], axis=2)
+    pair_totals = jnp.stack([local_total[:, h : h + 2] for h in pair_starts])
+    pair_tops = jnp.stack([local_top[:, h : h + 2] for h in pair_starts])
+    outgoing = jnp.concatenate([sum_chunks, pair_totals, pair_tops], axis=2)
     arrived = lax.all_to_all(outgoing, "seq", split_axis=0, concat_axis=0, tiled=True)
     part_sums = arrived[:, :, :width]
-    part_totals = arrived[:, :, width : width + HEADS]
-    part_tops = arrived[:, :, width + HEADS :]
+    part_totals = arrived[:, :, width : width + 2]
+    part_tops = arrived[:, :, width + 2 :]
 
     causal = (
         jnp.arange(NSTEP, dtype=jnp.int32)[:, None] >= jnp.arange(NSTEP, dtype=jnp.int32)[None, :]
@@ -146,22 +145,29 @@
         * scale
     )
     fresh = jnp.where(causal, fresh, NEG).reshape(row_count, HEADS, NSTEP)
-    cache_top = jnp.max(part_tops, axis=0)
-    highest = jnp.maximum(cache_top, jnp.max(fresh, axis=-1))
+    start = me * width
+    pair_start = jnp.minimum(start // HD, HEADS - 2)
+    fresh_top = jnp.max(fresh, axis=-1)
+    highest = jnp.maximum(
+        jnp.max(part_tops, axis=0), lax.dynamic_slice_in_dim(fresh_top, pair_start, 2, 1)
+    )
     factors = jnp.exp(part_tops - highest[None])
-    fresh_exp = jnp.exp(fresh - highest[:, :, None])
-    denominator = jnp.sum(part_totals * factors, axis=0) + jnp.sum(fresh_exp, axis=-1)
+    fresh_exp = jnp.exp(
+        fresh - lax.dynamic_update_slice_in_dim(fresh_top, highest, pair_start, 1)[:, :, None]
+    )
+    denominator = jnp.sum(part_totals * factors, axis=0) + lax.dynamic_slice_in_dim(
+        jnp.sum(fresh_exp, axis=-1), pair_start, 2, 1
+    )
     fresh_probs = fresh_exp.reshape(local_requests, NSTEP, KVH, GROUP, NSTEP).astype(jnp.bfloat16)
     fresh_sums = jnp.einsum(
         "rskgu,rukd->rskgd", fresh_probs, values_new, preferred_element_type=jnp.float32
     ).reshape(row_count, ATT)
-    start = me * width
-    head_of = (start + jnp.arange(width, dtype=jnp.int32)) // HD
-    chunk_factors = jnp.take(factors, head_of, axis=2)
+    first = (start + jnp.arange(width, dtype=jnp.int32)) // HD == pair_start
+    chunk_factors = jnp.where(first[None, None, :], factors[:, :, 0:1], factors[:, :, 1:2])
     numerator = jnp.sum(part_sums * chunk_factors, axis=0) + lax.dynamic_slice_in_dim(
         fresh_sums, start, width, 1
     )
-    chunk_denominator = jnp.take(denominator, head_of, axis=1)
+    chunk_denominator = jnp.where(first[None, :], denominator[:, 0:1], denominator[:, 1:2])
     attended_part = (numerator / chunk_denominator).astype(jnp.bfloat16)
     attended = gather_columns(attended_part, "seq")
     attn_mixed = gather_columns(

time: 128 us -> 129 us (level)
  local copies, waits for them, and re-layouts: 13.6 us -> 19.2 us
  waiting for transfers between devices: 32.9 us -> 29.2 us
  blocking collectives: 29.1 us -> 27.8 us
    all_to_all x1, waiting for transfers between devices: 12.3 us -> 8.35 us  [local(): lax.all_to_all(outgoing, 'seq', split_axis=0, concat_axis=0, tiled=True)]
    another operation x2 -> x22, local copies, waits for them, and re-layouts: 0.12 us -> 2.92 us  [the longest x10 1.4 us: local(): pair_tops = jnp.stack([local_top[:, h:h + 2] for h in pair_starts])]
    slice x0 -> x22, local copies, waits for them, and re-layouts: none -> 1.83 us  [the longest x11 0.92 us: local(): pair_totals = jnp.stack([local_total[:, h:h + 2] for h in pair_starts])]
    unnamed x29 -> x30, local copies, waits for them, and re-layouts: 5.04 us -> 6.12 us
  transfers between devices with their start and end apart: 4 -> 4, of which waited for: 3 -> 3; matrix products, arithmetic and copies ran while one was open for 18% -> 23% of each run, Pallas kernels for 0% -> 0%
where the time goes in v8:
time: 129 us; the launch traced here: 128 us
  waiting for transfers between devices  29.2 us (23%)
  blocking collectives  27.8 us (22%)
  local copies, waits for them, and re-layouts  19.2 us (15%)
  starting transfers between devices  19.1 us (15%)
  between operations  13.9 us (11%)
  other arithmetic  10.6 us (8%)
  matrix products  8.12 us (6%)
    all_to_all x2, waiting for transfers between devices, gather_columns(): lax.all_to_all(copies, axis_name, split_axis=0, concat_axis=0, tiled=True)  20.8 us
    all_to_all x1, blocking collectives, sum_scatter_columns(): lax.all_to_all(chunks, axis_name, split_axis=0, concat_axis=0, tiled=True)  14 us
    all_to_all x2, starting transfers between devices, gather_columns(): lax.all_to_all(copies, axis_name, split_axis=0, concat_axis=0, tiled=True)  13.8 us
    all_to_all x1, blocking collectives, gather_columns(): lax.all_to_all(copies, axis_name, split_axis=0, concat_axis=0, tiled=True)  13.8 us
    all_to_all x1, waiting for transfers between devices, local(): lax.all_to_all(outgoing, 'seq', split_axis=0, concat_axis=0, tiled=True)  8.35 us
    unnamed x30, local copies, waits for them, and re-layouts  6.12 us
    all_to_all x1, starting transfers between devices, local(): lax.all_to_all(outgoing, 'seq', split_axis=0, concat_axis=0, tiled=True)  5.31 us
  transfers between devices with their start and end apart: 4, of which 3 were waited for; matrix products, arithmetic and copies ran while one was open for 23% of the time, Pallas kernels for 0%

profile of v8, /device:TPU:448, one launch (start us, length us, event | category | flops | bytes accessed | tf_op | source)
XLA Modules:
  0.0 128.0 jit_solution(17661558565722228219)
XLA Ops:
  6.5 1.8 %pad_maximum_fusion.1 = bf16[96,1536]{1,0:T(8,128)(2,1)} fusion(bf16[96,512]{1,0:T(8,128)(2,1)} %bitcast.178, bf16[96,1024]{1,0:T(8,128)(2,1)} %bitcast.177), kind=kLoop, calls=%fused_computation.16 | loop fusion | flops 589824 | bytes 589824 | tf_op jit(solution)/shard_map/concatenate | solution.py:79
  8.4 0.9 reshape.230
  9.3 1.0 multiply_reduce_fusion.1
  10.4 0.9 fusion.18
  11.3 0.8 broadcast_in_dim.135
  12.1 10.0 %all-to-all-start = ((f32[32,24,80]{2,1,0:T(8,128)}), f32[32,24,80]{2,1,0:T(8,128)S(1)}, u32[]{:S(2)}, u32[]{:S(2)}) async-start(f32[32,24,80]{2,1,0:T(8,128)} %broadcast_in_dim.135), calls=%async_computation | async-start | bytes 786432 | tf_op jit(solution)/shard_map/all_to_all | solution.py:50
  22.1 0.7 add_convert_fusion.3
  22.8 0.7 broadcast_multiply_fusion
  23.8 1.5 %copy.681 = bf16[6,128,512]{1,2,0:T(8,128)(2,1)S(1)} copy(bf16[6,128,512]{2,1,0:T(8,128)(2,1)} %param.18) | data formatting | bytes 1572864 | tf_op args[5]
  25.9 10.6 %all-to-all-done = f32[32,24,80]{2,1,0:T(8,128)S(1)} async-done(((f32[32,24,80]{2,1,0:T(8,128)}), f32[32,24,80]{2,1,0:T(8,128)S(1)}, u32[]{:S(2)}, u32[]{:S(2)}) %all-to-all-start) | async-done | bytes 245792 | tf_op jit(solution)/shard_map/all_to_all | solution.py:50
  45.7 1.1 reshape.249
  46.7 5.3 %all-to-all-start.1 = ((f32[32,1,1248]{2,1,0:T(1,128)}), f32[32,1,1248]{2,1,0:T(1,128)S(1)}, u32[]{:S(2)}, u32[]{:S(2)}) async-start(f32[32,1,1248]{2,1,0:T(1,128)} %reshape.249), calls=%async_computation.1 | async-start | bytes 327680 | tf_op jit(solution)/shard_map/all_to_all | solution.py:135
  52.2 1.1 fusion.39
  54.1 8.4 %all-to-all-done.1 = f32[32,1,1248]{2,1,0:T(1,128)S(1)} async-done(((f32[32,1,1248]{2,1,0:T(1,128)}), f32[32,1,1248]{2,1,0:T(1,128)S(1)}, u32[]{:S(2)}, u32[]{:S(2)}) %all-to-all-start.1) | async-done | bytes 159776 | tf_op jit(solution)/shard_map/all_to_all | solution.py:135
  63.0 1.0 reduce.5
  68.1 13.8 %all_to_all.25 = bf16[32,2,576]{2,1,0:T(2,128)(2,1)S(1)} all-to-all(bf16[32,2,576]{2,1,0:T(2,128)(2,1)S(1)} %reshape.251), channel_id=1, replica_groups=mesh['seq'=32,'req'=16] {'seq'}, dimensions={0} | all-to-all | bytes 147456 | tf_op jit(solution)/shard_map/all_to_all | solution.py:50
  82.7 1.1 reshape.253
  83.7 3.9 %all-to-all-start.3 = ((f32[32,1,1152]{2,1,0:T(1,128)}), f32[32,1,1152]{2,1,0:T(1,128)S(1)}, u32[]{:S(2)}, u32[]{:S(2)}) async-start(f32[32,1,1152]{2,1,0:T(1,128)} %reshape.253), calls=%async_computation.3 | async-start | bytes 294912 | tf_op jit(solution)/shard_map/all_to_all | solution.py:50
  87.8 10.1 %all-to-all-done.3 = f32[32,1,1152]{2,1,0:T(1,128)S(1)} async-done(((f32[32,1,1152]{2,1,0:T(1,128)}), f32[32,1,1152]{2,1,0:T(1,128)S(1)}, u32[]{:S(2)}, u32[]{:S(2)}) %all-to-all-start.3) | async-done | bytes 147488 | tf_op jit(solution)/shard_map/all_to_all | solution.py:50
  97.9 1.0 reduce.6
  99.9 2.5 %fusion = f32[24,1024]{1,0:T(8,128)S(1)} fusion(bf16[1536,1536]{1,0:T(8,128)(2,1)} %all-gather.2.cloned.1.call-done, f32[24,1536]{1,0:T(8,128)S(1)} %add.135, f32[1536]{0:T(1024)S(1)} %copy-done.6, f32[24]{0:T(128)S(1)} %rsqrt.25), kind=kOutput, calls=%fused_computation | convolution fusion | flops 75608064 | bytes 3397728 | tf_op jit(solution)/shard_map/dot_general | solution.py:183
  102.4 1.9 %convolution_multiply_fusion = f32[24,1536]{1,0:T(8,128)S(1)} fusion(bf16[1536,1536]{1,0:T(8,128)(2,1)} %all-gather.2.cloned.1.call-done, f32[24]{0:T(128)S(1)} %mul.213, f32[24,1024]{1,0:T(8,128)S(1)} %fusion), kind=kOutput, calls=%fused_computation.2 | convolution fusion | flops 37859328 | bytes 1818720 | tf_op jit(solution)/shard_map/dot_general | solution.py:185
  105.2 14.0 %all_to_all.26 = f32[32,1,1152]{2,1,0:T(1,128)S(1)} all-to-all(f32[32,1,1152]{2,1,0:T(1,128)S(1)} %reshape.255), channel_id=1, replica_groups=mesh['seq'=32,'req'=16] {'seq'}, dimensions={0} | all-to-all | bytes 294912 | tf_op jit(solution)/shard_map/all_to_all | solution.py:59
  119.2 1.0 reduce.7
  (149 shorter events, 18.9 us)
Async XLA Ops:
  6.5 3.8 %copy-start = (bf16[1536,80]{0,1:T(8,128)(2,1)S(1)}, bf16[1536,80]{0,1:T(8,128)(2,1)}, u32[]{:S(2)}) copy-start(bf16[1536,80]{0,1:T(8,128)(2,1)} %param.16) | copy-start | bytes 737284
  6.5 19.2 %copy-start.7 = (s32[6]{0:T(128)S(1)}, s32[6]{0:T(128)}, u32[]{:S(2)}) copy-start(s32[6]{0:T(128)} %param.21) | copy-start | bytes 76
  6.5 18.8 %copy-start.1 = (bf16[6,128,512]{2,1,0:T(8,128)(2,1)S(1)}, bf16[6,128,512]{2,1,0:T(8,128)(2,1)}, u32[]{:S(2)}) copy-start(bf16[6,128,512]{2,1,0:T(8,128)(2,1)} %param.19) | copy-start | bytes 2359300
  6.5 93.4 %all-gather.2.cloned.1.call-start = ((), (), s32[]{:S(2)}) async-start(), calls=%async_computation.5 | async-start | bytes 5013504 | tf_op jit(solution)/shard_map/all_gather | solution.py:78
  12.1 24.5 %all-to-all-start = ((f32[32,24,80]{2,1,0:T(8,128)}), f32[32,24,80]{2,1,0:T(8,128)S(1)}, u32[]{:S(2)}, u32[]{:S(2)}) async-start(f32[32,24,80]{2,1,0:T(8,128)} %broadcast_in_dim.135), calls=%async_computation | async-start | bytes 786432 | tf_op jit(solution)/shard_map/all_to_all | solution.py:50
  46.7 15.8 %all-to-all-start.1 = ((f32[32,1,1248]{2,1,0:T(1,128)}), f32[32,1,1248]{2,1,0:T(1,128)S(1)}, u32[]{:S(2)}, u32[]{:S(2)}) async-start(f32[32,1,1248]{2,1,0:T(1,128)} %reshape.249), calls=%async_computation.1 | async-start | bytes 327680 | tf_op jit(solution)/shard_map/all_to_all | solution.py:135
  53.4 29.1 %copy-start.3 = (bf16[1536,48]{0,1:T(8,128)(2,1)S(1)}, bf16[1536,48]{0,1:T(8,128)(2,1)}, u32[]{:S(2)}) copy-start(bf16[1536,48]{0,1:T(8,128)(2,1)} %param.17) | copy-start | bytes 442372
  64.3 23.3 %copy-start.4 = (f32[6,4,8]{2,1,0:T(4,128)S(1)}, f32[6,4,8]{2,1,0:T(4,128)}, u32[]{:S(2)}) copy-start(f32[6,4,8]{2,1,0:T(4,128)} %param.23) | copy-start | bytes 2308
  64.3 23.3 %copy-start.5 = (s32[6,4,8]{2,1,0:T(4,128)S(1)}, s32[6,4,8]{2,1,0:T(4,128)}, u32[]{:S(2)}) copy-start(s32[6,4,8]{2,1,0:T(4,128)} %param.22) | copy-start | bytes 2308
  66.1 33.6 %copy-start.2 = (bf16[6,4,1536]{2,1,0:T(4,128)(2,1)S(1)}, bf16[6,4,1536]{2,1,0:T(4,128)(2,1)}, u32[]{:S(2)}) copy-start(bf16[6,4,1536]{2,1,0:T(4,128)(2,1)} %param.13) | copy-start | bytes 221188
  66.1 33.9 %copy-start.6 = (f32[1536]{0:T(1024)S(1)}, f32[1536]{0:T(1024)}, u32[]{:S(2)}) copy-start(f32[1536]{0:T(1024)} %param.15) | copy-start | bytes 18436
  83.7 14.2 %all-to-all-start.3 = ((f32[32,1,1152]{2,1,0:T(1,128)}), f32[32,1,1152]{2,1,0:T(1,128)S(1)}, u32[]{:S(2)}, u32[]{:S(2)}) async-start(f32[32,1,1152]{2,1,0:T(1,128)} %reshape.253), calls=%async_computation.3 | async-start | bytes 294912 | tf_op jit(solution)/shard_map/all_to_all | solution.py:50
Sparse Core Ops, SparseCore 0:
  9.5 43.8 all-gather.1

commit v9 on v6

--- a/solution.py
+++ b/solution.py
@@ -56,8 +56,10 @@
     count = lax.axis_size(axis_name)
     rows, width = value.shape
     chunks = jnp.moveaxis(value.reshape(rows, count, width // count), 1, 0)
-    pieces = lax.all_to_all(chunks, axis_name, split_axis=0, concat_axis=0, tiled=True)
-    return jnp.sum(pieces, axis=0)
+    pieces = lax.all_to_all(
+        chunks.astype(jnp.bfloat16), axis_name, split_axis=0, concat_axis=0, tiled=True
+    )
+    return jnp.sum(pieces.astype(jnp.float32), axis=0)
 
 
 def local(

time: 128 us -> 126 us (0.984)
  no operation moved by 1% of the time
where the time goes in v9:
time: 126 us
  waiting for transfers between devices  32.9 us (26%)
  blocking collectives  28.9 us (23%)
  starting transfers between devices  19.1 us (15%)
  between operations  13.9 us (11%)
  local copies, waits for them, and re-layouts  13.4 us (11%)
  other arithmetic  9.45 us (7%)
  matrix products  8.1 us (6%)
    all_to_all x2, waiting for transfers between devices, gather_columns(): lax.all_to_all(copies, axis_name, split_axis=0, concat_axis=0, tiled=True)  20.6 us
    all_to_all x1, blocking collectives, gather_columns(): lax.all_to_all(copies, axis_name, split_axis=0, concat_axis=0, tiled=True)  15.1 us
    all_to_all x2, starting transfers between devices, gather_columns(): lax.all_to_all(copies, axis_name, split_axis=0, concat_axis=0, tiled=True)  14 us
    all_to_all x1, blocking collectives, sum_scatter_columns(): lax.all_to_all(chunks.astype(jnp.bfloat16), axis_name, split_axis=0, conc...  13.8 us
    all_to_all x1, waiting for transfers between devices, local(): lax.all_to_all(outgoing, 'seq', split_axis=0, concat_axis=0, tiled=True)  12.3 us
    all_to_all x1, starting transfers between devices, local(): lax.all_to_all(outgoing, 'seq', split_axis=0, concat_axis=0, tiled=True)  5.13 us
    unnamed x29, local copies, waits for them, and re-layouts  4.99 us
  transfers between devices with their start and end apart: 4, of which 3 were waited for; matrix products, arithmetic and copies ran while one was open for 18% of the time, Pallas kernels for 0%

profile of v9, /device:TPU:448, one launch (start us, length us, event | category | flops | bytes accessed | tf_op | source)
XLA Modules:
  0.0 125.7 jit_solution(17927141794469015108)
XLA Ops:
  6.5 1.8 %pad_maximum_fusion.1 = bf16[96,1536]{1,0:T(8,128)(2,1)} fusion(bf16[96,512]{1,0:T(8,128)(2,1)} %bitcast.82, bf16[96,1024]{1,0:T(8,128)(2,1)} %bitcast.81), kind=kLoop, calls=%fused_computation.19 | loop fusion | flops 589824 | bytes 589824 | tf_op jit(solution)/shard_map/concatenate | solution.py:81
  8.4 0.9 reshape.266
  9.3 1.0 multiply_reduce_fusion.2
  10.4 0.9 fusion.19
  11.3 0.8 broadcast_in_dim.66
  12.1 10.0 %all-to-all-start = ((f32[32,24,80]{2,1,0:T(8,128)}), f32[32,24,80]{2,1,0:T(8,128)S(1)}, u32[]{:S(2)}, u32[]{:S(2)}) async-start(f32[32,24,80]{2,1,0:T(8,128)} %broadcast_in_dim.66), calls=%async_computation | async-start | bytes 786432 | tf_op jit(solution)/shard_map/all_to_all | solution.py:50
  22.1 0.7 add_convert_fusion.3
  22.8 0.7 broadcast_multiply_fusion
  23.8 1.5 %copy.66 = bf16[6,128,512]{1,2,0:T(8,128)(2,1)S(1)} copy(bf16[6,128,512]{2,1,0:T(8,128)(2,1)} %param.18) | data formatting | bytes 1572864 | tf_op args[5]
  26.0 10.6 %all-to-all-done = f32[32,24,80]{2,1,0:T(8,128)S(1)} async-done(((f32[32,24,80]{2,1,0:T(8,128)}), f32[32,24,80]{2,1,0:T(8,128)S(1)}, u32[]{:S(2)}, u32[]{:S(2)}) %all-to-all-start) | async-done | bytes 245792 | tf_op jit(solution)/shard_map/all_to_all | solution.py:50
  40.7 0.9 pad_maximum_fusion
  41.6 5.1 %all-to-all-start.1 = ((f32[32,24,96]{2,1,0:T(8,128)}), f32[32,24,96]{2,1,0:T(8,128)S(1)}, u32[]{:S(2)}, u32[]{:S(2)}) async-start(f32[32,24,96]{2,1,0:T(8,128)} %pad_maximum_fusion), calls=%async_computation.1 | async-start | bytes 786432 | tf_op jit(solution)/shard_map/all_to_all | solution.py:138
  47.1 1.1 fusion.37
  48.4 12.3 %all-to-all-done.1 = f32[32,24,96]{2,1,0:T(8,128)S(1)} async-done(((f32[32,24,96]{2,1,0:T(8,128)}), f32[32,24,96]{2,1,0:T(8,128)S(1)}, u32[]{:S(2)}, u32[]{:S(2)}) %all-to-all-start.1) | async-done | bytes 294944 | tf_op jit(solution)/shard_map/all_to_all | solution.py:138
  63.5 0.6 gather_fusion
  65.5 15.1 %all_to_all.25 = bf16[32,2,576]{2,1,0:T(2,128)(2,1)S(1)} all-to-all(bf16[32,2,576]{2,1,0:T(2,128)(2,1)S(1)} %reshape.302), channel_id=1, replica_groups=mesh['seq'=32,'req'=16] {'seq'}, dimensions={0} | all-to-all | bytes 147456 | tf_op jit(solution)/shard_map/all_to_all | solution.py:50
  81.3 1.1 reshape.304
  82.4 4.0 %all-to-all-start.3 = ((f32[32,1,1152]{2,1,0:T(1,128)}), f32[32,1,1152]{2,1,0:T(1,128)S(1)}, u32[]{:S(2)}, u32[]{:S(2)}) async-start(f32[32,1,1152]{2,1,0:T(1,128)} %reshape.304), calls=%async_computation.3 | async-start | bytes 294912 | tf_op jit(solution)/shard_map/all_to_all | solution.py:50
  86.6 10.0 %all-to-all-done.3 = f32[32,1,1152]{2,1,0:T(1,128)S(1)} async-done(((f32[32,1,1152]{2,1,0:T(1,128)}), f32[32,1,1152]{2,1,0:T(1,128)S(1)}, u32[]{:S(2)}, u32[]{:S(2)}) %all-to-all-start.3) | async-done | bytes 147488 | tf_op jit(solution)/shard_map/all_to_all | solution.py:50
  97.1 1.0 reduce.5
  99.1 2.5 %fusion = f32[24,1024]{1,0:T(8,128)S(1)} fusion(bf16[1536,1536]{1,0:T(8,128)(2,1)} %all-gather.2.cloned.1.call-done, f32[24,1536]{1,0:T(8,128)S(1)} %add.165, f32[1536]{0:T(1024)S(1)} %copy-done.6, f32[24]{0:T(128)S(1)} %rsqrt.25), kind=kOutput, calls=%fused_computation.2 | convolution fusion | flops 75608064 | bytes 3397728 | tf_op jit(solution)/shard_map/dot_general | solution.py:179
  101.6 1.9 %fusion.2 = bf16[24,1536]{1,0:T(8,128)(2,1)S(1)} fusion(bf16[1536,1536]{1,0:T(8,128)(2,1)} %all-gather.2.cloned.1.call-done, f32[24]{0:T(128)S(1)} %mul.213, f32[24,1024]{1,0:T(8,128)S(1)} %fusion), kind=kOutput, calls=%fused_computation.5 | convolution fusion | flops 37896192 | bytes 1744992 | tf_op jit(solution)/shard_map/dot_general | solution.py:181
  104.1 13.8 %all_to_all.26 = bf16[32,2,576]{2,1,0:T(2,128)(2,1)S(1)} all-to-all(bf16[32,2,576]{2,1,0:T(2,128)(2,1)S(1)} %reshape.306), channel_id=1, replica_groups=mesh['seq'=32,'req'=16] {'seq'}, dimensions={0} | all-to-all | bytes 147456 | tf_op jit(solution)/shard_map/all_to_all | solution.py:59
  118.2 0.7 add_convert_fusion.2
  (105 shorter events, 12.8 us)
Async XLA Ops:
  6.5 3.8 %copy-start = (bf16[1536,80]{0,1:T(8,128)(2,1)S(1)}, bf16[1536,80]{0,1:T(8,128)(2,1)}, u32[]{:S(2)}) copy-start(bf16[1536,80]{0,1:T(8,128)(2,1)} %param.16) | copy-start | bytes 737284
  6.5 19.2 %copy-start.7 = (s32[6]{0:T(128)S(1)}, s32[6]{0:T(128)}, u32[]{:S(2)}) copy-start(s32[6]{0:T(128)} %param.21) | copy-start | bytes 76
  6.5 18.8 %copy-start.1 = (bf16[6,128,512]{2,1,0:T(8,128)(2,1)S(1)}, bf16[6,128,512]{2,1,0:T(8,128)(2,1)}, u32[]{:S(2)}) copy-start(bf16[6,128,512]{2,1,0:T(8,128)(2,1)} %param.19) | copy-start | bytes 2359300
  6.5 92.6 %all-gather.2.cloned.1.call-start = ((), (), s32[]{:S(2)}) async-start(), calls=%async_computation.5 | async-start | bytes 5013504 | tf_op jit(solution)/shard_map/all_gather | solution.py:80
  12.1 24.5 %all-to-all-start = ((f32[32,24,80]{2,1,0:T(8,128)}), f32[32,24,80]{2,1,0:T(8,128)S(1)}, u32[]{:S(2)}, u32[]{:S(2)}) async-start(f32[32,24,80]{2,1,0:T(8,128)} %broadcast_in_dim.66), calls=%async_computation | async-start | bytes 786432 | tf_op jit(solution)/shard_map/all_to_all | solution.py:50
  41.6 19.0 %all-to-all-start.1 = ((f32[32,24,96]{2,1,0:T(8,128)}), f32[32,24,96]{2,1,0:T(8,128)S(1)}, u32[]{:S(2)}, u32[]{:S(2)}) async-start(f32[32,24,96]{2,1,0:T(8,128)} %pad_maximum_fusion), calls=%async_computation.1 | async-start | bytes 786432 | tf_op jit(solution)/shard_map/all_to_all | solution.py:138
  61.5 19.6 %copy-start.3 = (bf16[1536,48]{0,1:T(8,128)(2,1)S(1)}, bf16[1536,48]{0,1:T(8,128)(2,1)}, u32[]{:S(2)}) copy-start(bf16[1536,48]{0,1:T(8,128)(2,1)} %param.17) | copy-start | bytes 442372
  62.1 24.4 %copy-start.4 = (f32[6,4,8]{2,1,0:T(4,128)S(1)}, f32[6,4,8]{2,1,0:T(4,128)}, u32[]{:S(2)}) copy-start(f32[6,4,8]{2,1,0:T(4,128)} %param.23) | copy-start | bytes 2308
  62.1 24.4 %copy-start.5 = (s32[6,4,8]{2,1,0:T(4,128)S(1)}, s32[6,4,8]{2,1,0:T(4,128)}, u32[]{:S(2)}) copy-start(s32[6,4,8]{2,1,0:T(4,128)} %param.22) | copy-start | bytes 2308
  63.2 35.7 %copy-start.2 = (bf16[6,4,1536]{2,1,0:T(4,128)(2,1)S(1)}, bf16[6,4,1536]{2,1,0:T(4,128)(2,1)}, u32[]{:S(2)}) copy-start(bf16[6,4,1536]{2,1,0:T(4,128)(2,1)} %param.13) | copy-start | bytes 221188
  63.2 35.9 %copy-start.6 = (f32[1536]{0:T(1024)S(1)}, f32[1536]{0:T(1024)}, u32[]{:S(2)}) copy-start(f32[1536]{0:T(1024)} %param.15) | copy-start | bytes 18436
  82.4 14.2 %all-to-all-start.3 = ((f32[32,1,1152]{2,1,0:T(1,128)}), f32[32,1,1152]{2,1,0:T(1,128)S(1)}, u32[]{:S(2)}, u32[]{:S(2)}) async-start(f32[32,1,1152]{2,1,0:T(1,128)} %reshape.304), calls=%async_computation.3 | async-start | bytes 294912 | tf_op jit(solution)/shard_map/all_to_all | solution.py:50
Sparse Core Ops, SparseCore 0:
  9.5 43.8 all-gather.1

commit v10 on v9

--- a/solution.py
+++ b/solution.py
@@ -167,8 +167,8 @@
     attended_part = (numerator / chunk_denominator).astype(jnp.bfloat16)
     attended = gather_columns(attended_part, "seq")
     attn_mixed = gather_columns(
-        jnp.dot(attended, w_o, preferred_element_type=jnp.float32), "seq"
-    )
+        jnp.dot(attended, w_o, preferred_element_type=jnp.float32).astype(jnp.bfloat16), "seq"
+    ).astype(jnp.float32)
     resid = inputs + attn_mixed
     mixed_in = normalize(resid, moe_gain).astype(jnp.bfloat16)
 

time: 126 us -> 124 us (0.984)
  no operation moved by 1% of the time
where the time goes in v10:
time: 124 us; the launch traced here: 123 us
  waiting for transfers between devices  32.6 us (26%)
  blocking collectives  28.4 us (23%)
  starting transfers between devices  19.1 us (15%)
  between operations  13.9 us (11%)
  local copies, waits for them, and re-layouts  12.8 us (10%)
  other arithmetic  8.49 us (7%)
  matrix products  8.1 us (7%)
    all_to_all x2, waiting for transfers between devices, gather_columns(): lax.all_to_all(copies, axis_name, split_axis=0, concat_axis=0, tiled=True)  20.3 us
    all_to_all x1, blocking collectives, gather_columns(): lax.all_to_all(copies, axis_name, split_axis=0, concat_axis=0, tiled=True)  15.1 us
    all_to_all x2, starting transfers between devices, gather_columns(): lax.all_to_all(copies, axis_name, split_axis=0, concat_axis=0, tiled=True)  14 us
    all_to_all x1, blocking collectives, sum_scatter_columns(): lax.all_to_all(chunks.astype(jnp.bfloat16), axis_name, split_axis=0, conc...  13.3 us
    all_to_all x1, waiting for transfers between devices, local(): lax.all_to_all(outgoing, 'seq', split_axis=0, concat_axis=0, tiled=True)  12.3 us
    all_to_all x1, starting transfers between devices, local(): lax.all_to_all(outgoing, 'seq', split_axis=0, concat_axis=0, tiled=True)  5.13 us
    unnamed x29, local copies, waits for them, and re-layouts  4.9 us
  transfers between devices with their start and end apart: 4, of which 3 were waited for; matrix products, arithmetic and copies ran while one was open for 18% of the time, Pallas kernels for 0%

profile of v10, /device:TPU:448, one launch (start us, length us, event | category | flops | bytes accessed | tf_op | source)
XLA Modules:
  0.0 123.4 jit_solution(8545534061053914667)
XLA Ops:
  6.5 1.8 %pad_maximum_fusion.1 = bf16[96,1536]{1,0:T(8,128)(2,1)} fusion(bf16[96,512]{1,0:T(8,128)(2,1)} %bitcast.82, bf16[96,1024]{1,0:T(8,128)(2,1)} %bitcast.81), kind=kLoop, calls=%fused_computation.21 | loop fusion | flops 589824 | bytes 589824 | tf_op jit(solution)/shard_map/concatenate | solution.py:81
  8.4 0.9 reshape.266
  9.3 1.0 multiply_reduce_fusion.2
  10.4 0.9 fusion.19
  11.3 0.8 broadcast_in_dim.66
  12.1 10.0 %all-to-all-start = ((f32[32,24,80]{2,1,0:T(8,128)}), f32[32,24,80]{2,1,0:T(8,128)S(1)}, u32[]{:S(2)}, u32[]{:S(2)}) async-start(f32[32,24,80]{2,1,0:T(8,128)} %broadcast_in_dim.66), calls=%async_computation | async-start | bytes 786432 | tf_op jit(solution)/shard_map/all_to_all | solution.py:50
  22.1 0.7 add_convert_fusion.3
  22.8 0.7 broadcast_multiply_fusion
  23.8 1.5 %copy.66 = bf16[6,128,512]{1,2,0:T(8,128)(2,1)S(1)} copy(bf16[6,128,512]{2,1,0:T(8,128)(2,1)} %param.18) | data formatting | bytes 1572864 | tf_op args[5]
  25.9 10.6 %all-to-all-done = f32[32,24,80]{2,1,0:T(8,128)S(1)} async-done(((f32[32,24,80]{2,1,0:T(8,128)}), f32[32,24,80]{2,1,0:T(8,128)S(1)}, u32[]{:S(2)}, u32[]{:S(2)}) %all-to-all-start) | async-done | bytes 245792 | tf_op jit(solution)/shard_map/all_to_all | solution.py:50
  39.4 0.6 convolution_bitcast_fusion
  40.7 0.9 pad_maximum_fusion
  41.6 5.1 %all-to-all-start.1 = ((f32[32,24,96]{2,1,0:T(8,128)}), f32[32,24,96]{2,1,0:T(8,128)S(1)}, u32[]{:S(2)}, u32[]{:S(2)}) async-start(f32[32,24,96]{2,1,0:T(8,128)} %pad_maximum_fusion), calls=%async_computation.1 | async-start | bytes 786432 | tf_op jit(solution)/shard_map/all_to_all | solution.py:138
  47.1 1.1 fusion.37
  48.4 12.3 %all-to-all-done.1 = f32[32,24,96]{2,1,0:T(8,128)S(1)} async-done(((f32[32,24,96]{2,1,0:T(8,128)}), f32[32,24,96]{2,1,0:T(8,128)S(1)}, u32[]{:S(2)}, u32[]{:S(2)}) %all-to-all-start.1) | async-done | bytes 294944 | tf_op jit(solution)/shard_map/all_to_all | solution.py:138
  63.5 0.6 gather_fusion
  65.5 15.1 %all_to_all.25 = bf16[32,2,576]{2,1,0:T(2,128)(2,1)S(1)} all-to-all(bf16[32,2,576]{2,1,0:T(2,128)(2,1)S(1)} %reshape.302), channel_id=1, replica_groups=mesh['seq'=32,'req'=16] {'seq'}, dimensions={0} | all-to-all | bytes 147456 | tf_op jit(solution)/shard_map/all_to_all | solution.py:50
  81.3 0.9 reshape.304
  82.3 4.0 %all-to-all-start.3 = ((bf16[32,2,576]{2,1,0:T(2,128)(2,1)}), bf16[32,2,576]{2,1,0:T(2,128)(2,1)S(1)}, u32[]{:S(2)}, u32[]{:S(2)}) async-start(bf16[32,2,576]{2,1,0:T(2,128)(2,1)} %reshape.304), calls=%async_computation.3 | async-start | bytes 163840 | tf_op jit(solution)/shard_map/all_to_all | solution.py:50
  86.5 9.7 %all-to-all-done.3 = bf16[32,2,576]{2,1,0:T(2,128)(2,1)S(1)} async-done(((bf16[32,2,576]{2,1,0:T(2,128)(2,1)}), bf16[32,2,576]{2,1,0:T(2,128)(2,1)S(1)}, u32[]{:S(2)}, u32[]{:S(2)}) %all-to-all-start.3) | async-done | bytes 73760 | tf_op jit(solution)/shard_map/all_to_all | solution.py:50
  97.3 2.5 %fusion = f32[24,1024]{1,0:T(8,128)S(1)} fusion(bf16[1536,1536]{1,0:T(8,128)(2,1)} %all-gather.2.cloned.1.call-done, f32[24,1536]{1,0:T(8,128)S(1)} %add.165, f32[1536]{0:T(1024)S(1)} %copy-done.6, f32[24]{0:T(128)S(1)} %rsqrt.25), kind=kOutput, calls=%fused_computation.2 | convolution fusion | flops 75608064 | bytes 3397728 | tf_op jit(solution)/shard_map/dot_general | solution.py:179
  99.7 1.9 %fusion.2 = bf16[24,1536]{1,0:T(8,128)(2,1)S(1)} fusion(bf16[1536,1536]{1,0:T(8,128)(2,1)} %all-gather.2.cloned.1.call-done, f32[24]{0:T(128)S(1)} %mul.213, f32[24,1024]{1,0:T(8,128)S(1)} %fusion), kind=kOutput, calls=%fused_computation.5 | convolution fusion | flops 37896192 | bytes 1744992 | tf_op jit(solution)/shard_map/dot_general | solution.py:181
  102.3 13.3 %all_to_all.26 = bf16[32,2,576]{2,1,0:T(2,128)(2,1)S(1)} all-to-all(bf16[32,2,576]{2,1,0:T(2,128)(2,1)S(1)} %reshape.306), channel_id=1, replica_groups=mesh['seq'=32,'req'=16] {'seq'}, dimensions={0} | all-to-all | bytes 147456 | tf_op jit(solution)/shard_map/all_to_all | solution.py:59
  115.9 0.7 add_convert_fusion.2
  (104 shorter events, 11.8 us)
Async XLA Ops:
  6.5 3.8 %copy-start = (bf16[1536,80]{0,1:T(8,128)(2,1)S(1)}, bf16[1536,80]{0,1:T(8,128)(2,1)}, u32[]{:S(2)}) copy-start(bf16[1536,80]{0,1:T(8,128)(2,1)} %param.16) | copy-start | bytes 737284
  6.5 19.2 %copy-start.7 = (s32[6]{0:T(128)S(1)}, s32[6]{0:T(128)}, u32[]{:S(2)}) copy-start(s32[6]{0:T(128)} %param.21) | copy-start | bytes 76
  6.5 18.8 %copy-start.1 = (bf16[6,128,512]{2,1,0:T(8,128)(2,1)S(1)}, bf16[6,128,512]{2,1,0:T(8,128)(2,1)}, u32[]{:S(2)}) copy-start(bf16[6,128,512]{2,1,0:T(8,128)(2,1)} %param.19) | copy-start | bytes 2359300
  6.5 90.7 %all-gather.2.cloned.1.call-start = ((), (), s32[]{:S(2)}) async-start(), calls=%async_computation.5 | async-start | bytes 5013504 | tf_op jit(solution)/shard_map/all_gather | solution.py:80
  12.1 24.5 %all-to-all-start = ((f32[32,24,80]{2,1,0:T(8,128)}), f32[32,24,80]{2,1,0:T(8,128)S(1)}, u32[]{:S(2)}, u32[]{:S(2)}) async-start(f32[32,24,80]{2,1,0:T(8,128)} %broadcast_in_dim.66), calls=%async_computation | async-start | bytes 786432 | tf_op jit(solution)/shard_map/all_to_all | solution.py:50
  41.6 19.0 %all-to-all-start.1 = ((f32[32,24,96]{2,1,0:T(8,128)}), f32[32,24,96]{2,1,0:T(8,128)S(1)}, u32[]{:S(2)}, u32[]{:S(2)}) async-start(f32[32,24,96]{2,1,0:T(8,128)} %pad_maximum_fusion), calls=%async_computation.1 | async-start | bytes 786432 | tf_op jit(solution)/shard_map/all_to_all | solution.py:138
  61.5 19.6 %copy-start.3 = (bf16[1536,48]{0,1:T(8,128)(2,1)S(1)}, bf16[1536,48]{0,1:T(8,128)(2,1)}, u32[]{:S(2)}) copy-start(bf16[1536,48]{0,1:T(8,128)(2,1)} %param.17) | copy-start | bytes 442372
  61.6 24.7 %copy-start.4 = (f32[6,4,8]{2,1,0:T(4,128)S(1)}, f32[6,4,8]{2,1,0:T(4,128)}, u32[]{:S(2)}) copy-start(f32[6,4,8]{2,1,0:T(4,128)} %param.23) | copy-start | bytes 2308
  61.6 24.7 %copy-start.5 = (s32[6,4,8]{2,1,0:T(4,128)S(1)}, s32[6,4,8]{2,1,0:T(4,128)}, u32[]{:S(2)}) copy-start(s32[6,4,8]{2,1,0:T(4,128)} %param.22) | copy-start | bytes 2308
  62.8 34.3 %copy-start.2 = (bf16[6,4,1536]{2,1,0:T(4,128)(2,1)S(1)}, bf16[6,4,1536]{2,1,0:T(4,128)(2,1)}, u32[]{:S(2)}) copy-start(bf16[6,4,1536]{2,1,0:T(4,128)(2,1)} %param.13) | copy-start | bytes 221188
  63.1 34.2 %copy-start.6 = (f32[1536]{0:T(1024)S(1)}, f32[1536]{0:T(1024)}, u32[]{:S(2)}) copy-start(f32[1536]{0:T(1024)} %param.15) | copy-start | bytes 18436
  82.3 13.9 %all-to-all-start.3 = ((bf16[32,2,576]{2,1,0:T(2,128)(2,1)}), bf16[32,2,576]{2,1,0:T(2,128)(2,1)S(1)}, u32[]{:S(2)}, u32[]{:S(2)}) async-start(bf16[32,2,576]{2,1,0:T(2,128)(2,1)} %reshape.304), calls=%async_computation.3 | async-start | bytes 163840 | tf_op jit(solution)/shard_map/all_to_all | solution.py:50
Sparse Core Ops, SparseCore 0:
  9.5 43.7 all-gather.1

commit v11 on v8

--- a/solution.py
+++ b/solution.py
@@ -56,8 +56,10 @@
     count = lax.axis_size(axis_name)
     rows, width = value.shape
     chunks = jnp.moveaxis(value.reshape(rows, count, width // count), 1, 0)
-    pieces = lax.all_to_all(chunks, axis_name, split_axis=0, concat_axis=0, tiled=True)
-    return jnp.sum(pieces, axis=0)
+    pieces = lax.all_to_all(
+        chunks.astype(jnp.bfloat16), axis_name, split_axis=0, concat_axis=0, tiled=True
+    )
+    return jnp.sum(pieces.astype(jnp.float32), axis=0)
 
 
 def local(
@@ -171,8 +173,8 @@
     attended_part = (numerator / chunk_denominator).astype(jnp.bfloat16)
     attended = gather_columns(attended_part, "seq")
     attn_mixed = gather_columns(
-        jnp.dot(attended, w_o, preferred_element_type=jnp.float32), "seq"
-    )
+        jnp.dot(attended, w_o, preferred_element_type=jnp.float32).astype(jnp.bfloat16), "seq"
+    ).astype(jnp.float32)
     resid = inputs + attn_mixed
     mixed_in = normalize(resid, moe_gain).astype(jnp.bfloat16)
 

time: 129 us -> 125 us (0.969)
  other arithmetic: 10.6 us -> 8.64 us
    all_to_all x2 -> x0, other arithmetic: 1.99 us -> none  [the longest x1 1 us: gather_columns(): lax.all_to_all(copies, axis_name, split_axis=0, concat_axis=0, tiled=True)]
  transfers between devices with their start and end apart: 4 -> 4, of which waited for: 3 -> 3; matrix products, arithmetic and copies ran while one was open for 23% -> 22% of each run, Pallas kernels for 0% -> 0%
where the time goes in v11:
time: 125 us
  waiting for transfers between devices  28.9 us (23%)
  blocking collectives  27.1 us (22%)
  starting transfers between devices  19.1 us (15%)
  local copies, waits for them, and re-layouts  19 us (15%)
  between operations  13.9 us (11%)
  other arithmetic  8.64 us (7%)
  matrix products  8.13 us (7%)
    all_to_all x2, waiting for transfers between devices, gather_columns(): lax.all_to_all(copies, axis_name, split_axis=0, concat_axis=0, tiled=True)  20.5 us
    all_to_all x1, blocking collectives, gather_columns(): lax.all_to_all(copies, axis_name, split_axis=0, concat_axis=0, tiled=True)  13.8 us
    all_to_all x2, starting transfers between devices, gather_columns(): lax.all_to_all(copies, axis_name, split_axis=0, concat_axis=0, tiled=True)  13.8 us
    all_to_all x1, blocking collectives, sum_scatter_columns(): lax.all_to_all(chunks.astype(jnp.bfloat16), axis_name, split_axis=0, conc...  13.3 us
    all_to_all x1, waiting for transfers between devices, local(): lax.all_to_all(outgoing, 'seq', split_axis=0, concat_axis=0, tiled=True)  8.35 us
    unnamed x30, local copies, waits for them, and re-layouts  5.98 us
    all_to_all x1, starting transfers between devices, local(): lax.all_to_all(outgoing, 'seq', split_axis=0, concat_axis=0, tiled=True)  5.31 us
  transfers between devices with their start and end apart: 4, of which 3 were waited for; matrix products, arithmetic and copies ran while one was open for 22% of the time, Pallas kernels for 0%

profile of v11, /device:TPU:448, one launch (start us, length us, event | category | flops | bytes accessed | tf_op | source)
XLA Modules:
  0.0 124.8 jit_solution(3497552278785829944)
XLA Ops:
  6.5 1.8 %pad_maximum_fusion.1 = bf16[96,1536]{1,0:T(8,128)(2,1)} fusion(bf16[96,512]{1,0:T(8,128)(2,1)} %bitcast.178, bf16[96,1024]{1,0:T(8,128)(2,1)} %bitcast.177), kind=kLoop, calls=%fused_computation.19 | loop fusion | flops 589824 | bytes 589824 | tf_op jit(solution)/shard_map/concatenate | solution.py:81
  8.4 0.9 reshape.229
  9.3 1.0 multiply_reduce_fusion.1
  10.4 0.9 fusion.19
  11.3 0.8 broadcast_in_dim.135
  12.1 10.0 %all-to-all-start = ((f32[32,24,80]{2,1,0:T(8,128)}), f32[32,24,80]{2,1,0:T(8,128)S(1)}, u32[]{:S(2)}, u32[]{:S(2)}) async-start(f32[32,24,80]{2,1,0:T(8,128)} %broadcast_in_dim.135), calls=%async_computation | async-start | bytes 786432 | tf_op jit(solution)/shard_map/all_to_all | solution.py:50
  22.1 0.7 add_convert_fusion.3
  22.8 0.7 broadcast_multiply_fusion
  23.8 1.5 %copy.681 = bf16[6,128,512]{1,2,0:T(8,128)(2,1)S(1)} copy(bf16[6,128,512]{2,1,0:T(8,128)(2,1)} %param.18) | data formatting | bytes 1572864 | tf_op args[5]
  25.9 10.6 %all-to-all-done = f32[32,24,80]{2,1,0:T(8,128)S(1)} async-done(((f32[32,24,80]{2,1,0:T(8,128)}), f32[32,24,80]{2,1,0:T(8,128)S(1)}, u32[]{:S(2)}, u32[]{:S(2)}) %all-to-all-start) | async-done | bytes 245792 | tf_op jit(solution)/shard_map/all_to_all | solution.py:50
  42.9 0.6 convolution_bitcast_fusion
  45.7 1.1 reshape.247
  46.7 5.3 %all-to-all-start.1 = ((f32[32,1,1248]{2,1,0:T(1,128)}), f32[32,1,1248]{2,1,0:T(1,128)S(1)}, u32[]{:S(2)}, u32[]{:S(2)}) async-start(f32[32,1,1248]{2,1,0:T(1,128)} %reshape.247), calls=%async_computation.1 | async-start | bytes 327680 | tf_op jit(solution)/shard_map/all_to_all | solution.py:137
  52.2 1.1 fusion.40
  54.1 8.4 %all-to-all-done.1 = f32[32,1,1248]{2,1,0:T(1,128)S(1)} async-done(((f32[32,1,1248]{2,1,0:T(1,128)}), f32[32,1,1248]{2,1,0:T(1,128)S(1)}, u32[]{:S(2)}, u32[]{:S(2)}) %all-to-all-start.1) | async-done | bytes 159776 | tf_op jit(solution)/shard_map/all_to_all | solution.py:137
  63.0 1.1 reduce.5
  68.2 13.8 %all_to_all.25 = bf16[32,2,576]{2,1,0:T(2,128)(2,1)S(1)} all-to-all(bf16[32,2,576]{2,1,0:T(2,128)(2,1)S(1)} %reshape.249), channel_id=1, replica_groups=mesh['seq'=32,'req'=16] {'seq'}, dimensions={0} | all-to-all | bytes 147456 | tf_op jit(solution)/shard_map/all_to_all | solution.py:50
  82.7 0.9 reshape.251
  83.6 3.8 %all-to-all-start.3 = ((bf16[32,2,576]{2,1,0:T(2,128)(2,1)}), bf16[32,2,576]{2,1,0:T(2,128)(2,1)S(1)}, u32[]{:S(2)}, u32[]{:S(2)}) async-start(bf16[32,2,576]{2,1,0:T(2,128)(2,1)} %reshape.251), calls=%async_computation.3 | async-start | bytes 163840 | tf_op jit(solution)/shard_map/all_to_all | solution.py:50
  87.7 9.9 %all-to-all-done.3 = bf16[32,2,576]{2,1,0:T(2,128)(2,1)S(1)} async-done(((bf16[32,2,576]{2,1,0:T(2,128)(2,1)}), bf16[32,2,576]{2,1,0:T(2,128)(2,1)S(1)}, u32[]{:S(2)}, u32[]{:S(2)}) %all-to-all-start.3) | async-done | bytes 73760 | tf_op jit(solution)/shard_map/all_to_all | solution.py:50
  98.6 2.5 %fusion = f32[24,1024]{1,0:T(8,128)S(1)} fusion(bf16[1536,1536]{1,0:T(8,128)(2,1)} %all-gather.2.cloned.1.call-done, f32[24,1536]{1,0:T(8,128)S(1)} %add.135, f32[1536]{0:T(1024)S(1)} %copy-done.6, f32[24]{0:T(128)S(1)} %rsqrt.25), kind=kOutput, calls=%fused_computation | convolution fusion | flops 75608064 | bytes 3397728 | tf_op jit(solution)/shard_map/dot_general | solution.py:185
  101.1 1.9 %fusion.2 = bf16[24,1536]{1,0:T(8,128)(2,1)S(1)} fusion(bf16[1536,1536]{1,0:T(8,128)(2,1)} %all-gather.2.cloned.1.call-done, f32[24]{0:T(128)S(1)} %mul.213, f32[24,1024]{1,0:T(8,128)S(1)} %fusion), kind=kOutput, calls=%fused_computation.3 | convolution fusion | flops 37896192 | bytes 1744992 | tf_op jit(solution)/shard_map/dot_general | solution.py:187
  103.6 13.3 %all_to_all.26 = bf16[32,2,576]{2,1,0:T(2,128)(2,1)S(1)} all-to-all(bf16[32,2,576]{2,1,0:T(2,128)(2,1)S(1)} %reshape.253), channel_id=1, replica_groups=mesh['seq'=32,'req'=16] {'seq'}, dimensions={0} | all-to-all | bytes 147456 | tf_op jit(solution)/shard_map/all_to_all | solution.py:59
  117.2 0.7 add_convert_fusion.2
  (148 shorter events, 17.5 us)
Async XLA Ops:
  6.5 3.8 %copy-start = (bf16[1536,80]{0,1:T(8,128)(2,1)S(1)}, bf16[1536,80]{0,1:T(8,128)(2,1)}, u32[]{:S(2)}) copy-start(bf16[1536,80]{0,1:T(8,128)(2,1)} %param.16) | copy-start | bytes 737284
  6.5 19.2 %copy-start.7 = (s32[6]{0:T(128)S(1)}, s32[6]{0:T(128)}, u32[]{:S(2)}) copy-start(s32[6]{0:T(128)} %param.21) | copy-start | bytes 76
  6.5 18.8 %copy-start.1 = (bf16[6,128,512]{2,1,0:T(8,128)(2,1)S(1)}, bf16[6,128,512]{2,1,0:T(8,128)(2,1)}, u32[]{:S(2)}) copy-start(bf16[6,128,512]{2,1,0:T(8,128)(2,1)} %param.19) | copy-start | bytes 2359300
  6.5 92.1 %all-gather.2.cloned.1.call-start = ((), (), s32[]{:S(2)}) async-start(), calls=%async_computation.5 | async-start | bytes 5013504 | tf_op jit(solution)/shard_map/all_gather | solution.py:80
  12.1 24.5 %all-to-all-start = ((f32[32,24,80]{2,1,0:T(8,128)}), f32[32,24,80]{2,1,0:T(8,128)S(1)}, u32[]{:S(2)}, u32[]{:S(2)}) async-start(f32[32,24,80]{2,1,0:T(8,128)} %broadcast_in_dim.135), calls=%async_computation | async-start | bytes 786432 | tf_op jit(solution)/shard_map/all_to_all | solution.py:50
  46.7 15.8 %all-to-all-start.1 = ((f32[32,1,1248]{2,1,0:T(1,128)}), f32[32,1,1248]{2,1,0:T(1,128)S(1)}, u32[]{:S(2)}, u32[]{:S(2)}) async-start(f32[32,1,1248]{2,1,0:T(1,128)} %reshape.247), calls=%async_computation.1 | async-start | bytes 327680 | tf_op jit(solution)/shard_map/all_to_all | solution.py:137
  53.4 29.1 %copy-start.3 = (bf16[1536,48]{0,1:T(8,128)(2,1)S(1)}, bf16[1536,48]{0,1:T(8,128)(2,1)}, u32[]{:S(2)}) copy-start(bf16[1536,48]{0,1:T(8,128)(2,1)} %param.17) | copy-start | bytes 442372
  63.0 24.5 %copy-start.4 = (f32[6,4,8]{2,1,0:T(4,128)S(1)}, f32[6,4,8]{2,1,0:T(4,128)}, u32[]{:S(2)}) copy-start(f32[6,4,8]{2,1,0:T(4,128)} %param.23) | copy-start | bytes 2308
  63.0 24.5 %copy-start.5 = (s32[6,4,8]{2,1,0:T(4,128)S(1)}, s32[6,4,8]{2,1,0:T(4,128)}, u32[]{:S(2)}) copy-start(s32[6,4,8]{2,1,0:T(4,128)} %param.22) | copy-start | bytes 2308
  65.7 32.7 %copy-start.2 = (bf16[6,4,1536]{2,1,0:T(4,128)(2,1)S(1)}, bf16[6,4,1536]{2,1,0:T(4,128)(2,1)}, u32[]{:S(2)}) copy-start(bf16[6,4,1536]{2,1,0:T(4,128)(2,1)} %param.13) | copy-start | bytes 221188
  65.9 32.8 %copy-start.6 = (f32[1536]{0:T(1024)S(1)}, f32[1536]{0:T(1024)}, u32[]{:S(2)}) copy-start(f32[1536]{0:T(1024)} %param.15) | copy-start | bytes 18436
  83.6 13.9 %all-to-all-start.3 = ((bf16[32,2,576]{2,1,0:T(2,128)(2,1)}), bf16[32,2,576]{2,1,0:T(2,128)(2,1)S(1)}, u32[]{:S(2)}, u32[]{:S(2)}) async-start(bf16[32,2,576]{2,1,0:T(2,128)(2,1)} %reshape.251), calls=%async_computation.3 | async-start | bytes 163840 | tf_op jit(solution)/shard_map/all_to_all | solution.py:50
Sparse Core Ops, SparseCore 0:
  9.5 43.8 all-gather.1

commit v12 on v10

--- a/solution.py
+++ b/solution.py
@@ -87,11 +87,15 @@
     me = lax.axis_index("seq")
     local_requests = x_in.shape[0]
     row_count = local_requests * NSTEP
-    inputs = x_in.astype(jnp.float32).reshape(row_count, D)
-    normed = normalize(inputs, attn_gain).astype(jnp.bfloat16)
+    inputs_by_request = x_in.astype(jnp.float32)
+    normed = normalize(inputs_by_request, attn_gain).astype(jnp.bfloat16)
     projected = gather_columns(
-        jnp.dot(normed, w_qkv, preferred_element_type=jnp.float32), "seq"
-    )
+        jnp.einsum("rsd,dc->rsc", normed, w_qkv, preferred_element_type=jnp.float32).reshape(
+            row_count, w_qkv.shape[1]
+        ),
+        "seq",
+    )
+    inputs = inputs_by_request.reshape(row_count, D)
     queries = projected[:, :ATT].reshape(local_requests, NSTEP, HEADS, HD)
     keys_new = projected[:, ATT : ATT + KVD].reshape(local_requests, NSTEP, KVH, HD)
     values_new = (

time: 124 us -> 123 us (level)
  transfers between devices with their start and end apart: 4 -> 4, of which waited for: 3 -> 3; matrix products, arithmetic and copies ran while one was open for 18% -> 17% of each run, Pallas kernels for 0% -> 0%
where the time goes in v12:
time: 123 us
  waiting for transfers between devices  32.6 us (27%)
  blocking collectives  28.4 us (23%)
  starting transfers between devices  19.1 us (16%)
  between operations  13.9 us (11%)
  local copies, waits for them, and re-layouts  11.8 us (10%)
  other arithmetic  8.49 us (7%)
  matrix products  8.31 us (7%)
    all_to_all x2, waiting for transfers between devices, gather_columns(): lax.all_to_all(copies, axis_name, split_axis=0, concat_axis=0, tiled=True)  20.3 us
    all_to_all x1, blocking collectives, gather_columns(): lax.all_to_all(copies, axis_name, split_axis=0, concat_axis=0, tiled=True)  15.1 us
    all_to_all x2, starting transfers between devices, gather_columns(): lax.all_to_all(copies, axis_name, split_axis=0, concat_axis=0, tiled=True)  14 us
    all_to_all x1, blocking collectives, sum_scatter_columns(): lax.all_to_all(chunks.astype(jnp.bfloat16), axis_name, split_axis=0, conc...  13.3 us
    all_to_all x1, waiting for transfers between devices, local(): lax.all_to_all(outgoing, 'seq', split_axis=0, concat_axis=0, tiled=True)  12.3 us
    all_to_all x1, starting transfers between devices, local(): lax.all_to_all(outgoing, 'seq', split_axis=0, concat_axis=0, tiled=True)  5.13 us
    unnamed x29, local copies, waits for them, and re-layouts  4.9 us
  transfers between devices with their start and end apart: 4, of which 3 were waited for; matrix products, arithmetic and copies ran while one was open for 17% of the time, Pallas kernels for 0%

profile of v12, /device:TPU:448, one launch (start us, length us, event | category | flops | bytes accessed | tf_op | source)
XLA Modules:
  0.0 122.7 jit_solution(12721005514535116650)
XLA Ops:
  6.5 1.8 %pad_maximum_fusion.1 = bf16[96,1536]{1,0:T(8,128)(2,1)} fusion(bf16[96,512]{1,0:T(8,128)(2,1)} %bitcast.85, bf16[96,1024]{1,0:T(8,128)(2,1)} %bitcast.84), kind=kLoop, calls=%fused_computation.21 | loop fusion | flops 589824 | bytes 589824 | tf_op jit(solution)/shard_map/concatenate | solution.py:81
  8.4 1.0 multiply_reduce_fusion.2
  9.4 1.1 fusion.9
  10.5 0.8 broadcast_in_dim.105
  11.3 10.0 %all-to-all-start = ((f32[32,24,80]{2,1,0:T(8,128)}), f32[32,24,80]{2,1,0:T(8,128)S(1)}, u32[]{:S(2)}, u32[]{:S(2)}) async-start(f32[32,24,80]{2,1,0:T(8,128)} %broadcast_in_dim.105), calls=%async_computation | async-start | bytes 786432 | tf_op jit(solution)/shard_map/all_to_all | solution.py:50
  21.3 0.7 add_convert_fusion.3
  22.1 0.7 broadcast_multiply_fusion
  23.0 1.5 %copy.69 = bf16[6,128,512]{1,2,0:T(8,128)(2,1)S(1)} copy(bf16[6,128,512]{2,1,0:T(8,128)(2,1)} %param.18) | data formatting | bytes 1572864 | tf_op args[5]
  25.2 10.6 %all-to-all-done = f32[32,24,80]{2,1,0:T(8,128)S(1)} async-done(((f32[32,24,80]{2,1,0:T(8,128)}), f32[32,24,80]{2,1,0:T(8,128)S(1)}, u32[]{:S(2)}, u32[]{:S(2)}) %all-to-all-start) | async-done | bytes 245792 | tf_op jit(solution)/shard_map/all_to_all | solution.py:50
  38.6 0.6 convolution_bitcast_fusion
  39.9 0.9 pad_maximum_fusion
  40.8 5.1 %all-to-all-start.1 = ((f32[32,24,96]{2,1,0:T(8,128)}), f32[32,24,96]{2,1,0:T(8,128)S(1)}, u32[]{:S(2)}, u32[]{:S(2)}) async-start(f32[32,24,96]{2,1,0:T(8,128)} %pad_maximum_fusion), calls=%async_computation.1 | async-start | bytes 786432 | tf_op jit(solution)/shard_map/all_to_all | solution.py:142
  46.3 1.1 fusion.38
  47.6 12.3 %all-to-all-done.1 = f32[32,24,96]{2,1,0:T(8,128)S(1)} async-done(((f32[32,24,96]{2,1,0:T(8,128)}), f32[32,24,96]{2,1,0:T(8,128)S(1)}, u32[]{:S(2)}, u32[]{:S(2)}) %all-to-all-start.1) | async-done | bytes 294944 | tf_op jit(solution)/shard_map/all_to_all | solution.py:142
  62.7 0.6 gather_fusion
  63.3 0.6 gather_fusion.1
  64.7 15.1 %all_to_all.25 = bf16[32,2,576]{2,1,0:T(2,128)(2,1)S(1)} all-to-all(bf16[32,2,576]{2,1,0:T(2,128)(2,1)S(1)} %reshape.294), channel_id=1, replica_groups=mesh['seq'=32,'req'=16] {'seq'}, dimensions={0} | all-to-all | bytes 147456 | tf_op jit(solution)/shard_map/all_to_all | solution.py:50
  80.6 0.9 reshape.296
  81.5 4.0 %all-to-all-start.3 = ((bf16[32,2,576]{2,1,0:T(2,128)(2,1)}), bf16[32,2,576]{2,1,0:T(2,128)(2,1)S(1)}, u32[]{:S(2)}, u32[]{:S(2)}) async-start(bf16[32,2,576]{2,1,0:T(2,128)(2,1)} %reshape.296), calls=%async_computation.3 | async-start | bytes 163840 | tf_op jit(solution)/shard_map/all_to_all | solution.py:50
  85.7 9.7 %all-to-all-done.3 = bf16[32,2,576]{2,1,0:T(2,128)(2,1)S(1)} async-done(((bf16[32,2,576]{2,1,0:T(2,128)(2,1)}), bf16[32,2,576]{2,1,0:T(2,128)(2,1)S(1)}, u32[]{:S(2)}, u32[]{:S(2)}) %all-to-all-start.3) | async-done | bytes 73760 | tf_op jit(solution)/shard_map/all_to_all | solution.py:50
  96.5 2.5 %fusion = f32[24,1024]{1,0:T(8,128)S(1)} fusion(bf16[1536,1536]{1,0:T(8,128)(2,1)} %all-gather.2.cloned.1.call-done, f32[24,1536]{1,0:T(8,128)S(1)} %add.164, f32[1536]{0:T(1024)S(1)} %copy-done.6, f32[24]{0:T(128)S(1)} %rsqrt.21), kind=kOutput, calls=%fused_computation.2 | convolution fusion | flops 75608064 | bytes 3397728 | tf_op jit(solution)/shard_map/dot_general | solution.py:183
  99.0 1.9 %fusion.2 = bf16[24,1536]{1,0:T(8,128)(2,1)S(1)} fusion(bf16[1536,1536]{1,0:T(8,128)(2,1)} %all-gather.2.cloned.1.call-done, f32[24]{0:T(128)S(1)} %mul.212, f32[24,1024]{1,0:T(8,128)S(1)} %fusion), kind=kOutput, calls=%fused_computation.5 | convolution fusion | flops 37896192 | bytes 1744992 | tf_op jit(solution)/shard_map/dot_general | solution.py:185
  101.5 13.3 %all_to_all.26 = bf16[32,2,576]{2,1,0:T(2,128)(2,1)S(1)} all-to-all(bf16[32,2,576]{2,1,0:T(2,128)(2,1)S(1)} %reshape.298), channel_id=1, replica_groups=mesh['seq'=32,'req'=16] {'seq'}, dimensions={0} | all-to-all | bytes 147456 | tf_op jit(solution)/shard_map/all_to_all | solution.py:59
  115.1 0.7 add_convert_fusion.2
  (103 shorter events, 11.1 us)
Async XLA Ops:
  6.5 2.8 %copy-start = (bf16[1536,80]{0,1:T(8,128)(2,1)S(1)}, bf16[1536,80]{0,1:T(8,128)(2,1)}, u32[]{:S(2)}) copy-start(bf16[1536,80]{0,1:T(8,128)(2,1)} %param.16) | copy-start | bytes 737284
  6.5 18.4 %copy-start.7 = (s32[6]{0:T(128)S(1)}, s32[6]{0:T(128)}, u32[]{:S(2)}) copy-start(s32[6]{0:T(128)} %param.21) | copy-start | bytes 76
  6.5 18.0 %copy-start.1 = (bf16[6,128,512]{2,1,0:T(8,128)(2,1)S(1)}, bf16[6,128,512]{2,1,0:T(8,128)(2,1)}, u32[]{:S(2)}) copy-start(bf16[6,128,512]{2,1,0:T(8,128)(2,1)} %param.19) | copy-start | bytes 2359300
  6.5 90.0 %all-gather.2.cloned.1.call-start = ((), (), s32[]{:S(2)}) async-start(), calls=%async_computation.5 | async-start | bytes 5013504 | tf_op jit(solution)/shard_map/all_gather | solution.py:80
  11.3 24.5 %all-to-all-start = ((f32[32,24,80]{2,1,0:T(8,128)}), f32[32,24,80]{2,1,0:T(8,128)S(1)}, u32[]{:S(2)}, u32[]{:S(2)}) async-start(f32[32,24,80]{2,1,0:T(8,128)} %broadcast_in_dim.105), calls=%async_computation | async-start | bytes 786432 | tf_op jit(solution)/shard_map/all_to_all | solution.py:50
  40.8 19.0 %all-to-all-start.1 = ((f32[32,24,96]{2,1,0:T(8,128)}), f32[32,24,96]{2,1,0:T(8,128)S(1)}, u32[]{:S(2)}, u32[]{:S(2)}) async-start(f32[32,24,96]{2,1,0:T(8,128)} %pad_maximum_fusion), calls=%async_computation.1 | async-start | bytes 786432 | tf_op jit(solution)/shard_map/all_to_all | solution.py:142
  60.7 19.6 %copy-start.3 = (bf16[1536,48]{0,1:T(8,128)(2,1)S(1)}, bf16[1536,48]{0,1:T(8,128)(2,1)}, u32[]{:S(2)}) copy-start(bf16[1536,48]{0,1:T(8,128)(2,1)} %param.17) | copy-start | bytes 442372
  60.9 24.7 %copy-start.2 = (bf16[6,4,1536]{2,1,0:T(4,128)(2,1)S(1)}, bf16[6,4,1536]{2,1,0:T(4,128)(2,1)}, u32[]{:S(2)}) copy-start(bf16[6,4,1536]{2,1,0:T(4,128)(2,1)} %param.13) | copy-start | bytes 221188
  60.9 24.7 %copy-start.4 = (f32[6,4,8]{2,1,0:T(4,128)S(1)}, f32[6,4,8]{2,1,0:T(4,128)}, u32[]{:S(2)}) copy-start(f32[6,4,8]{2,1,0:T(4,128)} %param.23) | copy-start | bytes 2308
  60.9 24.7 %copy-start.5 = (s32[6,4,8]{2,1,0:T(4,128)S(1)}, s32[6,4,8]{2,1,0:T(4,128)}, u32[]{:S(2)}) copy-start(s32[6,4,8]{2,1,0:T(4,128)} %param.22) | copy-start | bytes 2308
  62.3 34.2 %copy-start.6 = (f32[1536]{0:T(1024)S(1)}, f32[1536]{0:T(1024)}, u32[]{:S(2)}) copy-start(f32[1536]{0:T(1024)} %param.15) | copy-start | bytes 18436
  81.5 13.9 %all-to-all-start.3 = ((bf16[32,2,576]{2,1,0:T(2,128)(2,1)}), bf16[32,2,576]{2,1,0:T(2,128)(2,1)S(1)}, u32[]{:S(2)}, u32[]{:S(2)}) async-start(bf16[32,2,576]{2,1,0:T(2,128)(2,1)} %reshape.296), calls=%async_computation.3 | async-start | bytes 163840 | tf_op jit(solution)/shard_map/all_to_all | solution.py:50
Sparse Core Ops, SparseCore 0:
  9.5 43.7 all-gather.1

commit v13 on v12

--- a/solution.py
+++ b/solution.py
@@ -162,12 +162,15 @@
         "rskgu,rukd->rskgd", fresh_probs, values_new, preferred_element_type=jnp.float32
     ).reshape(row_count, ATT)
     start = me * width
-    head_of = (start + jnp.arange(width, dtype=jnp.int32)) // HD
-    chunk_factors = jnp.take(factors, head_of, axis=2)
+    pair_start = jnp.minimum(start // HD, HEADS - 2)
+    first = (start + jnp.arange(width, dtype=jnp.int32)) // HD == pair_start
+    pair_factors = lax.dynamic_slice_in_dim(factors, pair_start, 2, 2)
+    chunk_factors = jnp.where(first[None, None, :], pair_factors[:, :, 0:1], pair_factors[:, :, 1:2])
     numerator = jnp.sum(part_sums * chunk_factors, axis=0) + lax.dynamic_slice_in_dim(
         fresh_sums, start, width, 1
     )
-    chunk_denominator = jnp.take(denominator, head_of, axis=1)
+    pair_denominator = lax.dynamic_slice_in_dim(denominator, pair_start, 2, 1)
+    chunk_denominator = jnp.where(first[None, :], pair_denominator[:, 0:1], pair_denominator[:, 1:2])
     attended_part = (numerator / chunk_denominator).astype(jnp.bfloat16)
     attended = gather_columns(attended_part, "seq")
     attn_mixed = gather_columns(

time: 123 us -> 122 us (level)
    unnamed x29 -> x27, local copies, waits for them, and re-layouts: 4.9 us -> 4.55 us
  transfers between devices with their start and end apart: 4 -> 4, of which waited for: 3 -> 3; matrix products, arithmetic and copies ran while one was open for 17% -> 16% of each run, Pallas kernels for 0% -> 0%
where the time goes in v13:
time: 122 us; the launch traced here: 121 us
  waiting for transfers between devices  32.6 us (27%)
  blocking collectives  28.4 us (23%)
  starting transfers between devices  19.1 us (16%)
  between operations  13.9 us (11%)
  local copies, waits for them, and re-layouts  11 us (9%)
  matrix products  8.32 us (7%)
  other arithmetic  7.67 us (6%)
    all_to_all x2, waiting for transfers between devices, gather_columns(): lax.all_to_all(copies, axis_name, split_axis=0, concat_axis=0, tiled=True)  20.3 us
    all_to_all x1, blocking collectives, gather_columns(): lax.all_to_all(copies, axis_name, split_axis=0, concat_axis=0, tiled=True)  15.1 us
    all_to_all x2, starting transfers between devices, gather_columns(): lax.all_to_all(copies, axis_name, split_axis=0, concat_axis=0, tiled=True)  14 us
    all_to_all x1, blocking collectives, sum_scatter_columns(): lax.all_to_all(chunks.astype(jnp.bfloat16), axis_name, split_axis=0, conc...  13.3 us
    all_to_all x1, waiting for transfers between devices, local(): lax.all_to_all(outgoing, 'seq', split_axis=0, concat_axis=0, tiled=True)  12.2 us
    all_to_all x1, starting transfers between devices, local(): lax.all_to_all(outgoing, 'seq', split_axis=0, concat_axis=0, tiled=True)  5.13 us
    unnamed x27, local copies, waits for them, and re-layouts  4.55 us
    dot_general x1, matrix products, local(): gate_up = jnp.dot(mixed_in, expert_in, preferred_element_type=jnp.float32)  2.46 us
  transfers between devices with their start and end apart: 4, of which 3 were waited for; matrix products, arithmetic and copies ran while one was open for 16% of the time, Pallas kernels for 0%

profile of v13, /device:TPU:448, one launch (start us, length us, event | category | flops | bytes accessed | tf_op | source)
XLA Modules:
  0.0 121.0 jit_solution(6159272990899420373)
XLA Ops:
  6.5 1.8 %pad_maximum_fusion.1 = bf16[96,1536]{1,0:T(8,128)(2,1)} fusion(bf16[96,512]{1,0:T(8,128)(2,1)} %bitcast.81, bf16[96,1024]{1,0:T(8,128)(2,1)} %bitcast.80), kind=kLoop, calls=%fused_computation.19 | loop fusion | flops 589824 | bytes 589824 | tf_op jit(solution)/shard_map/concatenate | solution.py:81
  8.4 1.0 multiply_reduce_fusion.2
  9.4 1.1 fusion.9
  10.5 0.8 broadcast_in_dim.143
  11.3 10.0 %all-to-all-start = ((f32[32,24,80]{2,1,0:T(8,128)}), f32[32,24,80]{2,1,0:T(8,128)S(1)}, u32[]{:S(2)}, u32[]{:S(2)}) async-start(f32[32,24,80]{2,1,0:T(8,128)} %broadcast_in_dim.143), calls=%async_computation | async-start | bytes 786432 | tf_op jit(solution)/shard_map/all_to_all | solution.py:50
  21.3 0.7 add_convert_fusion.3
  22.0 0.7 broadcast_multiply_fusion
  23.0 1.5 %copy.97 = bf16[6,128,512]{1,2,0:T(8,128)(2,1)S(1)} copy(bf16[6,128,512]{2,1,0:T(8,128)(2,1)} %param.18) | data formatting | bytes 1572864 | tf_op args[5]
  25.2 10.6 %all-to-all-done = f32[32,24,80]{2,1,0:T(8,128)S(1)} async-done(((f32[32,24,80]{2,1,0:T(8,128)}), f32[32,24,80]{2,1,0:T(8,128)S(1)}, u32[]{:S(2)}, u32[]{:S(2)}) %all-to-all-start) | async-done | bytes 245792 | tf_op jit(solution)/shard_map/all_to_all | solution.py:50
  36.6 0.5 fusion.37
  37.5 0.5 fusion.13
  38.6 0.6 convolution_bitcast_fusion
  39.8 1.0 copy.102
  40.8 5.1 %all-to-all-start.1 = ((f32[32,24,96]{2,1,0:T(8,128)}), f32[32,24,96]{2,1,0:T(8,128)S(1)}, u32[]{:S(2)}, u32[]{:S(2)}) async-start(f32[32,24,96]{2,1,0:T(8,128)} %copy.102), calls=%async_computation.1 | async-start | bytes 786432 | tf_op jit(solution)/shard_map/all_to_all | solution.py:142
  46.2 1.1 fusion.38
  47.6 12.2 %all-to-all-done.1 = f32[32,24,96]{2,1,0:T(8,128)S(1)} async-done(((f32[32,24,96]{2,1,0:T(8,128)}), f32[32,24,96]{2,1,0:T(8,128)S(1)}, u32[]{:S(2)}, u32[]{:S(2)}) %all-to-all-start.1) | async-done | bytes 294944 | tf_op jit(solution)/shard_map/all_to_all | solution.py:142
  63.1 15.1 %all_to_all.25 = bf16[32,2,576]{2,1,0:T(2,128)(2,1)S(1)} all-to-all(bf16[32,2,576]{2,1,0:T(2,128)(2,1)S(1)} %reshape.252), channel_id=1, replica_groups=mesh['seq'=32,'req'=16] {'seq'}, dimensions={0} | all-to-all | bytes 147456 | tf_op jit(solution)/shard_map/all_to_all | solution.py:50
  79.0 0.9 reshape.254
  79.9 4.0 %all-to-all-start.3 = ((bf16[32,2,576]{2,1,0:T(2,128)(2,1)}), bf16[32,2,576]{2,1,0:T(2,128)(2,1)S(1)}, u32[]{:S(2)}, u32[]{:S(2)}) async-start(bf16[32,2,576]{2,1,0:T(2,128)(2,1)} %reshape.254), calls=%async_computation.3 | async-start | bytes 163840 | tf_op jit(solution)/shard_map/all_to_all | solution.py:50
  84.1 9.7 %all-to-all-done.3 = bf16[32,2,576]{2,1,0:T(2,128)(2,1)S(1)} async-done(((bf16[32,2,576]{2,1,0:T(2,128)(2,1)}), bf16[32,2,576]{2,1,0:T(2,128)(2,1)S(1)}, u32[]{:S(2)}, u32[]{:S(2)}) %all-to-all-start.3) | async-done | bytes 73760 | tf_op jit(solution)/shard_map/all_to_all | solution.py:50
  94.9 2.5 %fusion = f32[24,1024]{1,0:T(8,128)S(1)} fusion(bf16[1536,1536]{1,0:T(8,128)(2,1)} %all-gather.2.cloned.1.call-done, f32[24,1536]{1,0:T(8,128)S(1)} %add.133, f32[1536]{0:T(1024)S(1)} %copy-done.6, f32[24]{0:T(128)S(1)} %rsqrt.21), kind=kOutput, calls=%fused_computation | convolution fusion | flops 75608064 | bytes 3397728 | tf_op jit(solution)/shard_map/dot_general | solution.py:186
  97.4 1.9 %fusion.2 = bf16[24,1536]{1,0:T(8,128)(2,1)S(1)} fusion(bf16[1536,1536]{1,0:T(8,128)(2,1)} %all-gather.2.cloned.1.call-done, f32[24]{0:T(128)S(1)} %mul.212, f32[24,1024]{1,0:T(8,128)S(1)} %fusion), kind=kOutput, calls=%fused_computation.3 | convolution fusion | flops 37896192 | bytes 1744992 | tf_op jit(solution)/shard_map/dot_general | solution.py:188
  99.9 13.3 %all_to_all.26 = bf16[32,2,576]{2,1,0:T(2,128)(2,1)S(1)} all-to-all(bf16[32,2,576]{2,1,0:T(2,128)(2,1)S(1)} %reshape.256), channel_id=1, replica_groups=mesh['seq'=32,'req'=16] {'seq'}, dimensions={0} | all-to-all | bytes 147456 | tf_op jit(solution)/shard_map/all_to_all | solution.py:59
  113.5 0.7 add_convert_fusion.2
  (99 shorter events, 9.7 us)
Async XLA Ops:
  6.5 2.8 %copy-start = (bf16[1536,80]{0,1:T(8,128)(2,1)S(1)}, bf16[1536,80]{0,1:T(8,128)(2,1)}, u32[]{:S(2)}) copy-start(bf16[1536,80]{0,1:T(8,128)(2,1)} %param.16) | copy-start | bytes 737284
  6.5 18.4 %copy-start.7 = (s32[6]{0:T(128)S(1)}, s32[6]{0:T(128)}, u32[]{:S(2)}) copy-start(s32[6]{0:T(128)} %param.21) | copy-start | bytes 76
  6.5 18.0 %copy-start.1 = (bf16[6,128,512]{2,1,0:T(8,128)(2,1)S(1)}, bf16[6,128,512]{2,1,0:T(8,128)(2,1)}, u32[]{:S(2)}) copy-start(bf16[6,128,512]{2,1,0:T(8,128)(2,1)} %param.19) | copy-start | bytes 2359300
  6.5 88.4 %all-gather.2.cloned.1.call-start = ((), (), s32[]{:S(2)}) async-start(), calls=%async_computation.5 | async-start | bytes 5013504 | tf_op jit(solution)/shard_map/all_gather | solution.py:80
  11.3 24.5 %all-to-all-start = ((f32[32,24,80]{2,1,0:T(8,128)}), f32[32,24,80]{2,1,0:T(8,128)S(1)}, u32[]{:S(2)}, u32[]{:S(2)}) async-start(f32[32,24,80]{2,1,0:T(8,128)} %broadcast_in_dim.143), calls=%async_computation | async-start | bytes 786432 | tf_op jit(solution)/shard_map/all_to_all | solution.py:50
  40.8 19.0 %all-to-all-start.1 = ((f32[32,24,96]{2,1,0:T(8,128)}), f32[32,24,96]{2,1,0:T(8,128)S(1)}, u32[]{:S(2)}, u32[]{:S(2)}) async-start(f32[32,24,96]{2,1,0:T(8,128)} %copy.102), calls=%async_computation.1 | async-start | bytes 786432 | tf_op jit(solution)/shard_map/all_to_all | solution.py:142
  47.4 31.3 %copy-start.3 = (bf16[1536,48]{0,1:T(8,128)(2,1)S(1)}, bf16[1536,48]{0,1:T(8,128)(2,1)}, u32[]{:S(2)}) copy-start(bf16[1536,48]{0,1:T(8,128)(2,1)} %param.17) | copy-start | bytes 442372
  47.6 36.3 %copy-start.2 = (bf16[6,4,1536]{2,1,0:T(4,128)(2,1)S(1)}, bf16[6,4,1536]{2,1,0:T(4,128)(2,1)}, u32[]{:S(2)}) copy-start(bf16[6,4,1536]{2,1,0:T(4,128)(2,1)} %param.13) | copy-start | bytes 221188
  60.1 23.8 %copy-start.4 = (f32[6,4,8]{2,1,0:T(4,128)S(1)}, f32[6,4,8]{2,1,0:T(4,128)}, u32[]{:S(2)}) copy-start(f32[6,4,8]{2,1,0:T(4,128)} %param.23) | copy-start | bytes 2308
  60.2 23.8 %copy-start.5 = (s32[6,4,8]{2,1,0:T(4,128)S(1)}, s32[6,4,8]{2,1,0:T(4,128)}, u32[]{:S(2)}) copy-start(s32[6,4,8]{2,1,0:T(4,128)} %param.22) | copy-start | bytes 2308
  61.2 33.7 %copy-start.6 = (f32[1536]{0:T(1024)S(1)}, f32[1536]{0:T(1024)}, u32[]{:S(2)}) copy-start(f32[1536]{0:T(1024)} %param.15) | copy-start | bytes 18436
  79.9 13.9 %all-to-all-start.3 = ((bf16[32,2,576]{2,1,0:T(2,128)(2,1)}), bf16[32,2,576]{2,1,0:T(2,128)(2,1)S(1)}, u32[]{:S(2)}, u32[]{:S(2)}) async-start(bf16[32,2,576]{2,1,0:T(2,128)(2,1)} %reshape.254), calls=%async_computation.3 | async-start | bytes 163840 | tf_op jit(solution)/shard_map/all_to_all | solution.py:50
Sparse Core Ops, SparseCore 0:
  9.5 43.8 all-gather.1

commit v14 on v13

--- a/solution.py
+++ b/solution.py
@@ -172,9 +172,18 @@
     pair_denominator = lax.dynamic_slice_in_dim(denominator, pair_start, 2, 1)
     chunk_denominator = jnp.where(first[None, :], pair_denominator[:, 0:1], pair_denominator[:, 1:2])
     attended_part = (numerator / chunk_denominator).astype(jnp.bfloat16)
-    attended = gather_columns(attended_part, "seq")
+    attended_pieces = lax.all_to_all(
+        jnp.broadcast_to(attended_part[None], (seq_count,) + attended_part.shape),
+        "seq", split_axis=0, concat_axis=0, tiled=True,
+    )
     attn_mixed = gather_columns(
-        jnp.dot(attended, w_o, preferred_element_type=jnp.float32).astype(jnp.bfloat16), "seq"
+        jnp.einsum(
+            "ird,idc->rc",
+            attended_pieces,
+            w_o.reshape(seq_count, width, w_o.shape[1]),
+            preferred_element_type=jnp.float32,
+        ).astype(jnp.bfloat16),
+        "seq",
     ).astype(jnp.float32)
     resid = inputs + attn_mixed
     mixed_in = normalize(resid, moe_gain).astype(jnp.bfloat16)

time: 122 us -> 122 us (level)
  blocking collectives: 28.4 us -> 13.3 us
  waiting for transfers between devices: 32.6 us -> 42.5 us
  starting transfers between devices: 19.1 us -> 24.3 us
    all_to_all x1 -> x0, blocking collectives: 15.1 us -> none  [gather_columns(): lax.all_to_all(copies, axis_name, split_axis=0, concat_axis=0, tiled=True)]
    all_to_all x0 -> x1, waiting for transfers between devices: none -> 9.85 us  [local(): lax.all_to_all(jnp.broadcast_to(attended_part[None], (seq_count,) + atten...]
    all_to_all x0 -> x1, starting transfers between devices: none -> 5.21 us  [local(): lax.all_to_all(jnp.broadcast_to(attended_part[None], (seq_count,) + atten...]
  transfers between devices with their start and end apart: 4 -> 5, of which waited for: 3 -> 4; matrix products, arithmetic and copies ran while one was open for 16% -> 16% of each run, Pallas kernels for 0% -> 0%
where the time goes in v14:
time: 122 us
  waiting for transfers between devices  42.5 us (35%)
  starting transfers between devices  24.3 us (20%)
  between operations  13.9 us (11%)
  blocking collectives  13.3 us (11%)
  local copies, waits for them, and re-layouts  11.6 us (10%)
  matrix products  8.41 us (7%)
  other arithmetic  7.67 us (6%)
    all_to_all x2, waiting for transfers between devices, gather_columns(): lax.all_to_all(copies, axis_name, split_axis=0, concat_axis=0, tiled=True)  20.3 us
    all_to_all x2, starting transfers between devices, gather_columns(): lax.all_to_all(copies, axis_name, split_axis=0, concat_axis=0, tiled=True)  14 us
    all_to_all x1, blocking collectives, sum_scatter_columns(): lax.all_to_all(chunks.astype(jnp.bfloat16), axis_name, split_axis=0, conc...  13.3 us
    all_to_all x1, waiting for transfers between devices, local(): lax.all_to_all(outgoing, 'seq', split_axis=0, concat_axis=0, tiled=True)  12.2 us
    all_to_all x1, waiting for transfers between devices, local(): lax.all_to_all(jnp.broadcast_to(attended_part[None], (seq_count,) + atten...  9.85 us
    all_to_all x1, starting transfers between devices, local(): lax.all_to_all(jnp.broadcast_to(attended_part[None], (seq_count,) + atten...  5.21 us
    unnamed x27, local copies, waits for them, and re-layouts  5.19 us
    all_to_all x1, starting transfers between devices, local(): lax.all_to_all(outgoing, 'seq', split_axis=0, concat_axis=0, tiled=True)  5.13 us
  transfers between devices with their start and end apart: 5, of which 4 were waited for; matrix products, arithmetic and copies ran while one was open for 16% of the time, Pallas kernels for 0%

profile of v14, /device:TPU:448, one launch (start us, length us, event | category | flops | bytes accessed | tf_op | source)
XLA Modules:
  0.0 121.7 jit_solution(8159005730086210835)
XLA Ops:
  6.5 1.8 %pad_maximum_fusion.1 = bf16[96,1536]{1,0:T(8,128)(2,1)} fusion(bf16[96,512]{1,0:T(8,128)(2,1)} %bitcast.85, bf16[96,1024]{1,0:T(8,128)(2,1)} %bitcast.84), kind=kLoop, calls=%fused_computation.20 | loop fusion | flops 589824 | bytes 589824 | tf_op jit(solution)/shard_map/concatenate | solution.py:81
  8.4 1.0 multiply_reduce_fusion.2
  9.4 1.1 fusion.10
  10.5 0.8 broadcast_in_dim.143
  11.3 10.0 %all-to-all-start = ((f32[32,24,80]{2,1,0:T(8,128)}), f32[32,24,80]{2,1,0:T(8,128)S(1)}, u32[]{:S(2)}, u32[]{:S(2)}) async-start(f32[32,24,80]{2,1,0:T(8,128)} %broadcast_in_dim.143), calls=%async_computation | async-start | bytes 786432 | tf_op jit(solution)/shard_map/all_to_all | solution.py:50
  21.3 0.7 add_convert_fusion.3
  22.0 0.7 broadcast_multiply_fusion
  23.0 1.5 %copy.100 = bf16[6,128,512]{1,2,0:T(8,128)(2,1)S(1)} copy(bf16[6,128,512]{2,1,0:T(8,128)(2,1)} %param.18) | data formatting | bytes 1572864 | tf_op args[5]
  25.2 10.6 %all-to-all-done = f32[32,24,80]{2,1,0:T(8,128)S(1)} async-done(((f32[32,24,80]{2,1,0:T(8,128)}), f32[32,24,80]{2,1,0:T(8,128)S(1)}, u32[]{:S(2)}, u32[]{:S(2)}) %all-to-all-start) | async-done | bytes 245792 | tf_op jit(solution)/shard_map/all_to_all | solution.py:50
  38.6 0.6 convolution_bitcast_fusion
  39.8 1.0 copy.105
  40.8 5.1 %all-to-all-start.1 = ((f32[32,24,96]{2,1,0:T(8,128)}), f32[32,24,96]{2,1,0:T(8,128)S(1)}, u32[]{:S(2)}, u32[]{:S(2)}) async-start(f32[32,24,96]{2,1,0:T(8,128)} %copy.105), calls=%async_computation.1 | async-start | bytes 786432 | tf_op jit(solution)/shard_map/all_to_all | solution.py:142
  46.2 1.1 fusion.39
  47.6 12.2 %all-to-all-done.1 = f32[32,24,96]{2,1,0:T(8,128)S(1)} async-done(((f32[32,24,96]{2,1,0:T(8,128)}), f32[32,24,96]{2,1,0:T(8,128)S(1)}, u32[]{:S(2)}, u32[]{:S(2)}) %all-to-all-start.1) | async-done | bytes 294944 | tf_op jit(solution)/shard_map/all_to_all | solution.py:142
  62.9 0.9 reshape.253
  63.8 5.2 %all-to-all-start.2 = ((bf16[32,2,576]{2,1,0:T(2,128)(2,1)}), bf16[32,2,576]{2,1,0:T(2,128)(2,1)S(1)}, u32[]{:S(2)}, u32[]{:S(2)}) async-start(bf16[32,2,576]{2,1,0:T(2,128)(2,1)} %reshape.253), calls=%async_computation.2 | async-start | bytes 163840 | tf_op jit(solution)/shard_map/all_to_all | solution.py:175
  69.2 9.8 %all-to-all-done.2 = bf16[32,2,576]{2,1,0:T(2,128)(2,1)S(1)} async-done(((bf16[32,2,576]{2,1,0:T(2,128)(2,1)}), bf16[32,2,576]{2,1,0:T(2,128)(2,1)S(1)}, u32[]{:S(2)}, u32[]{:S(2)}) %all-to-all-start.2) | async-done | bytes 73760 | tf_op jit(solution)/shard_map/all_to_all | solution.py:175
  79.6 0.9 reshape.255
  80.5 4.0 %all-to-all-start.3 = ((bf16[32,2,576]{2,1,0:T(2,128)(2,1)}), bf16[32,2,576]{2,1,0:T(2,128)(2,1)S(1)}, u32[]{:S(2)}, u32[]{:S(2)}) async-start(bf16[32,2,576]{2,1,0:T(2,128)(2,1)} %reshape.255), calls=%async_computation.3 | async-start | bytes 163840 | tf_op jit(solution)/shard_map/all_to_all | solution.py:50
  84.8 9.7 %all-to-all-done.3 = bf16[32,2,576]{2,1,0:T(2,128)(2,1)S(1)} async-done(((bf16[32,2,576]{2,1,0:T(2,128)(2,1)}), bf16[32,2,576]{2,1,0:T(2,128)(2,1)S(1)}, u32[]{:S(2)}, u32[]{:S(2)}) %all-to-all-start.3) | async-done | bytes 73760 | tf_op jit(solution)/shard_map/all_to_all | solution.py:50
  95.6 2.5 %fusion = f32[24,1024]{1,0:T(8,128)S(1)} fusion(bf16[1536,1536]{1,0:T(8,128)(2,1)} %all-gather.2.cloned.1.call-done, f32[24,1536]{1,0:T(8,128)S(1)} %add.133, f32[1536]{0:T(1024)S(1)} %copy-done.6, f32[24]{0:T(128)S(1)} %rsqrt.21), kind=kOutput, calls=%fused_computation | convolution fusion | flops 75608064 | bytes 3397728 | tf_op jit(solution)/shard_map/dot_general | solution.py:195
  98.0 1.9 %fusion.2 = bf16[24,1536]{1,0:T(8,128)(2,1)S(1)} fusion(bf16[1536,1536]{1,0:T(8,128)(2,1)} %all-gather.2.cloned.1.call-done, f32[24]{0:T(128)S(1)} %mul.212, f32[24,1024]{1,0:T(8,128)S(1)} %fusion), kind=kOutput, calls=%fused_computation.3 | convolution fusion | flops 37896192 | bytes 1744992 | tf_op jit(solution)/shard_map/dot_general | solution.py:197
  100.6 13.3 %all_to_all.25 = bf16[32,2,576]{2,1,0:T(2,128)(2,1)S(1)} all-to-all(bf16[32,2,576]{2,1,0:T(2,128)(2,1)S(1)} %reshape.257), channel_id=1, replica_groups=mesh['seq'=32,'req'=16] {'seq'}, dimensions={0} | all-to-all | bytes 147456 | tf_op jit(solution)/shard_map/all_to_all | solution.py:59
  114.2 0.7 add_convert_fusion.2
  (99 shorter events, 10.4 us)
Async XLA Ops:
  6.5 2.8 %copy-start = (bf16[1536,80]{0,1:T(8,128)(2,1)S(1)}, bf16[1536,80]{0,1:T(8,128)(2,1)}, u32[]{:S(2)}) copy-start(bf16[1536,80]{0,1:T(8,128)(2,1)} %param.16) | copy-start | bytes 737284
  6.5 18.4 %copy-start.7 = (s32[6]{0:T(128)S(1)}, s32[6]{0:T(128)}, u32[]{:S(2)}) copy-start(s32[6]{0:T(128)} %param.21) | copy-start | bytes 76
  6.5 18.0 %copy-start.1 = (bf16[6,128,512]{2,1,0:T(8,128)(2,1)S(1)}, bf16[6,128,512]{2,1,0:T(8,128)(2,1)}, u32[]{:S(2)}) copy-start(bf16[6,128,512]{2,1,0:T(8,128)(2,1)} %param.19) | copy-start | bytes 2359300
  6.5 89.0 %all-gather.2.cloned.1.call-start = ((), (), s32[]{:S(2)}) async-start(), calls=%async_computation.5 | async-start | bytes 5013504 | tf_op jit(solution)/shard_map/all_gather | solution.py:80
  11.3 24.5 %all-to-all-start = ((f32[32,24,80]{2,1,0:T(8,128)}), f32[32,24,80]{2,1,0:T(8,128)S(1)}, u32[]{:S(2)}, u32[]{:S(2)}) async-start(f32[32,24,80]{2,1,0:T(8,128)} %broadcast_in_dim.143), calls=%async_computation | async-start | bytes 786432 | tf_op jit(solution)/shard_map/all_to_all | solution.py:50
  40.8 19.0 %all-to-all-start.1 = ((f32[32,24,96]{2,1,0:T(8,128)}), f32[32,24,96]{2,1,0:T(8,128)S(1)}, u32[]{:S(2)}, u32[]{:S(2)}) async-start(f32[32,24,96]{2,1,0:T(8,128)} %copy.105), calls=%async_computation.1 | async-start | bytes 786432 | tf_op jit(solution)/shard_map/all_to_all | solution.py:142
  46.2 22.8 %copy-start.3 = (bf16[1536,48]{0,1:T(8,128)(2,1)S(1)}, bf16[1536,48]{0,1:T(8,128)(2,1)}, u32[]{:S(2)}) copy-start(bf16[1536,48]{0,1:T(8,128)(2,1)} %param.17) | copy-start | bytes 442372
  60.1 24.4 %copy-start.2 = (bf16[6,4,1536]{2,1,0:T(4,128)(2,1)S(1)}, bf16[6,4,1536]{2,1,0:T(4,128)(2,1)}, u32[]{:S(2)}) copy-start(bf16[6,4,1536]{2,1,0:T(4,128)(2,1)} %param.13) | copy-start | bytes 221188
  60.2 24.4 %copy-start.4 = (f32[6,4,8]{2,1,0:T(4,128)S(1)}, f32[6,4,8]{2,1,0:T(4,128)}, u32[]{:S(2)}) copy-start(f32[6,4,8]{2,1,0:T(4,128)} %param.23) | copy-start | bytes 2308
  60.2 24.4 %copy-start.5 = (s32[6,4,8]{2,1,0:T(4,128)S(1)}, s32[6,4,8]{2,1,0:T(4,128)}, u32[]{:S(2)}) copy-start(s32[6,4,8]{2,1,0:T(4,128)} %param.22) | copy-start | bytes 2308
  61.6 34.0 %copy-start.6 = (f32[1536]{0:T(1024)S(1)}, f32[1536]{0:T(1024)}, u32[]{:S(2)}) copy-start(f32[1536]{0:T(1024)} %param.15) | copy-start | bytes 18436
  63.8 15.3 %all-to-all-start.2 = ((bf16[32,2,576]{2,1,0:T(2,128)(2,1)}), bf16[32,2,576]{2,1,0:T(2,128)(2,1)S(1)}, u32[]{:S(2)}, u32[]{:S(2)}) async-start(bf16[32,2,576]{2,1,0:T(2,128)(2,1)} %reshape.253), calls=%async_computation.2 | async-start | bytes 163840 | tf_op jit(solution)/shard_map/all_to_all | solution.py:175
  80.5 13.9 %all-to-all-start.3 = ((bf16[32,2,576]{2,1,0:T(2,128)(2,1)}), bf16[32,2,576]{2,1,0:T(2,128)(2,1)S(1)}, u32[]{:S(2)}, u32[]{:S(2)}) async-start(bf16[32,2,576]{2,1,0:T(2,128)(2,1)} %reshape.255), calls=%async_computation.3 | async-start | bytes 163840 | tf_op jit(solution)/shard_map/all_to_all | solution.py:50
Sparse Core Ops, SparseCore 0:
  9.5 43.8 all-gather.1
